TPU v7x, 32 devices: a whole 2x2x4 slice. The times are simulated.
32 devices in a mesh: rep: 4 (over y, x), fsdp: 8 (over z, core).
Axes of the slice: x: 2, y: 2, z: 4, core: 2. Of those that a mesh axis runs over, the one named last changes fastest.
Arguments:
- content_stream: bfloat16 [64, 512, 768], P(('rep', 'fsdp')), may hold values from -6 to 6
- query_stream: bfloat16 [64, 512, 768], P(('rep', 'fsdp')), may hold values from -6 to 6
- lengths: int32 [64], P(('rep', 'fsdp')), may hold values from 64 to 512, as said below
- factor_order: int32 [64, 512], P(('rep', 'fsdp')), may hold values from 0 to 511, each once within a row
- qkv_weight: float32 [768, 2304], P('fsdp'), may hold values from -0.21875 to 0.21875
- qv_bias: float32 [1536], P('fsdp'), may hold values from -3 to 3
- out_weight: float32 [768, 768], P('fsdp'), may hold values from -0.625 to 0.625
- out_bias: float32 [768], P('fsdp'), may hold values from -2 to 2
- norm1_gain: float32 [768], P('fsdp'), may hold values from 0.5 to 1.5
- norm1_bias: float32 [768], P('fsdp'), may hold values from -2 to 2
- rel_table: float32 [32, 12], P('fsdp'), may hold values from -4 to 4
- ffn_in_weight: float32 [768, 3072], P('fsdp'), may hold values from -0.21875 to 0.21875
- ffn_in_bias: float32 [3072], P('fsdp'), may hold values from -2 to 2
- ffn_out_weight: float32 [3072, 768], P('fsdp'), may hold values from -0.109375 to 0.109375
- ffn_out_bias: float32 [768], P('fsdp'), may hold values from -2 to 2
- norm2_gain: float32 [768], P('fsdp'), may hold values from 0.5 to 1.5
- norm2_bias: float32 [768], P('fsdp'), may hold values from -2 to 2
- content_cot: bfloat16 [64, 512, 768], P(('rep', 'fsdp')), may hold values from -6 to 6
- query_cot: bfloat16 [64, 512, 768], P(('rep', 'fsdp')), may hold values from -6 to 6
Outputs:
- content_out: bfloat16 [64, 512, 768], P(('rep', 'fsdp'))
- query_out: bfloat16 [64, 512, 768], P(('rep', 'fsdp'))
- content_grad: bfloat16 [64, 512, 768], P(('rep', 'fsdp'))
- query_grad: bfloat16 [64, 512, 768], P(('rep', 'fsdp'))
- qkv_weight_grad: float32 [768, 2304], P('fsdp')
- qv_bias_grad: float32 [1536], P('fsdp')
- out_weight_grad: float32 [768, 768], P('fsdp')
- out_bias_grad: float32 [768], P('fsdp')
- norm1_gain_grad: float32 [768], P('fsdp')
- norm1_bias_grad: float32 [768], P('fsdp')
- rel_table_grad: float32 [32, 12], P('fsdp')
- ffn_in_weight_grad: float32 [768, 3072], P('fsdp')
- ffn_in_bias_grad: float32 [3072], P('fsdp')
- ffn_out_weight_grad: float32 [3072, 768], P('fsdp')
- ffn_out_bias_grad: float32 [768], P('fsdp')
- norm2_gain_grad: float32 [768], P('fsdp')
- norm2_bias_grad: float32 [768], P('fsdp')
Inputs may be any that keep to these rules, and one draw needn't show every extreme that they name: `lengths`: the first sequence of the batch has 512 real tokens. `factor_order`: each row is a permutation of the positions.
All inputs are finite; a program needn't handle non-finite values.
Results may differ from a plain program's by a relative error of at most 0.02.
Values may be sent and summed in bfloat16 or wider, within the bound.
A program may use at most 320 MiB of HBM per device.

v0:
```python
import math

import jax
import jax.numpy as jnp
import numpy as np
from jax import lax
from jax.sharding import PartitionSpec as P

HEADS = 12
HEAD = 64
BUCKETS = 32
MAX_DIST = 128


eps_norm = 1e-05
root_half = 0.7071067811865476
inv_root_tau = 0.3989422804014327


def bucket_of(offset):
    half_count = BUCKETS // 2
    result = (offset < 0).astype(np.int64) * half_count
    distance = np.abs(offset)
    exact_count = half_count // 2
    fraction = np.log(np.maximum(distance, 1) / exact_count) / np.log(MAX_DIST / exact_count)
    beyond = exact_count + (fraction * (half_count - exact_count)).astype(np.int64)
    beyond = np.minimum(beyond, half_count - 1)
    result = result + np.where(distance < exact_count, distance, beyond)
    return result.astype(np.int32)


def relative_buckets(length):
    places = np.arange(length)
    return bucket_of(places[:, None] - places[None, :])


def diagonal_sums(grid):
    head_count, seq_len, _ = grid.shape
    flipped = grid[:, :, ::-1]
    padded = jnp.pad(flipped, ((0, 0), (0, 0), (0, seq_len)))
    skewed = padded.reshape(head_count, 2 * seq_len * seq_len)[:, : seq_len * (2 * seq_len - 1)]
    return jnp.sum(skewed.reshape(head_count, seq_len, 2 * seq_len - 1), 1)


def norm_forward(summed, gain_vec, shift_vec):
    row_mean = jnp.mean(summed, -1, keepdims=True)
    centered = summed - row_mean
    inverse = lax.rsqrt(jnp.mean(centered * centered, -1, keepdims=True) + eps_norm)
    normed = centered * inverse
    return (normed * gain_vec + shift_vec, normed, inverse)


def norm_backward(upstream, normed, inverse, gain_vec):
    scaled = upstream * gain_vec
    centered = (
        scaled
        - jnp.mean(scaled, -1, keepdims=True)
        - normed * jnp.mean(scaled * normed, -1, keepdims=True)
    )
    return (inverse * centered, jnp.sum(upstream * normed, 0), jnp.sum(upstream, 0))


def gelu_value(hidden_in):
    return 0.5 * hidden_in * (1.0 + lax.erf(hidden_in * root_half))


def gelu_slope(hidden_in):
    return (
        0.5 * (1.0 + lax.erf(hidden_in * root_half))
        + hidden_in * jnp.exp(-0.5 * hidden_in * hidden_in) * inv_root_tau
    )


def rows_inner(left_op, right_op):
    return lax.dot_general(
        left_op, right_op, (((0,), (0,)), ((), ())), preferred_element_type=jnp.float32
    )


def times_transpose(left_op, right_op):
    return lax.dot_general(
        left_op, right_op, (((1,), (1,)), ((), ())), preferred_element_type=jnp.float32
    )


def key_masks(length_one, rank_row):
    places = jnp.arange(rank_row.shape[0])
    visible = (places < length_one)[None, :]
    first_key = (places == 0)[None, :]
    content_mask = visible & (first_key | (rank_row[None, :] <= rank_row[:, None]))
    query_mask = visible & (first_key | (rank_row[None, :] < rank_row[:, None]))
    return (content_mask, query_mask)


def scores_of(query_block, key_block, bias_full, allowed_mask):
    score_scale = 1.0 / math.sqrt(HEAD)
    logits = (
        jnp.einsum("ihd,jhd->hij", query_block, key_block, preferred_element_type=jnp.float32)
        * score_scale
        + bias_full
    )
    return jnp.where(allowed_mask[None], logits, -jnp.inf)


def attend_forward(query_block, key_block, value_block, bias_full, allowed_mask):
    logits = scores_of(query_block, key_block, bias_full, allowed_mask)
    row_max = jnp.max(logits, -1, keepdims=True)
    exp_scores = jnp.exp(logits - row_max)
    row_total = jnp.sum(exp_scores, -1, keepdims=True)
    attn_probs = (exp_scores / row_total).astype(jnp.bfloat16)
    mixed_heads = jnp.einsum(
        "hij,jhd->ihd", attn_probs, value_block, preferred_element_type=jnp.float32
    )
    return (mixed_heads.astype(jnp.bfloat16), (row_max + jnp.log(row_total))[..., 0])


def attend_backward(
    query_block, key_block, value_block, bias_full, allowed_mask, log_total, grad_mixed
):
    score_scale = 1.0 / math.sqrt(HEAD)
    logits = scores_of(query_block, key_block, bias_full, allowed_mask)
    attn_probs = jnp.exp(logits - log_total[..., None])
    grad_values = jnp.einsum(
        "hij,ihd->jhd",
        attn_probs.astype(jnp.bfloat16),
        grad_mixed,
        preferred_element_type=jnp.float32,
    )
    grad_probs = jnp.einsum(
        "ihd,jhd->hij", grad_mixed, value_block, preferred_element_type=jnp.float32
    )
    grad_logits = attn_probs * (grad_probs - jnp.sum(attn_probs * grad_probs, -1, keepdims=True))
    grad_low = grad_logits.astype(jnp.bfloat16)
    grad_queries = (
        jnp.einsum("hij,jhd->ihd", grad_low, key_block, preferred_element_type=jnp.float32)
        * score_scale
    )
    grad_keys = (
        jnp.einsum("hij,ihd->jhd", grad_low, query_block, preferred_element_type=jnp.float32)
        * score_scale
    )
    return (grad_queries, grad_keys, grad_values, grad_logits)


def on_device(
    content_stream,
    query_stream,
    lengths,
    factor_order,
    qkv_weight,
    qv_bias,
    out_weight,
    out_bias,
    norm1_gain,
    norm1_bias,
    rel_table,
    ffn_in_weight,
    ffn_in_bias,
    ffn_out_weight,
    ffn_out_bias,
    norm2_gain,
    norm2_bias,
    content_cot,
    query_cot,
):
    seq_count, seq_len, width = content_stream.shape
    head_count = HEADS
    head_width = width // head_count
    row_count = seq_count * seq_len
    attn_full = (
        lax.all_gather(qkv_weight.astype(jnp.bfloat16), "fsdp", axis=0, tiled=True),
        lax.all_gather(qv_bias.astype(jnp.bfloat16), "fsdp", axis=0, tiled=True),
        lax.all_gather(out_weight.astype(jnp.bfloat16), "fsdp", axis=0, tiled=True),
        lax.all_gather(out_bias.astype(jnp.bfloat16), "fsdp", axis=0, tiled=True),
        lax.all_gather(norm1_gain.astype(jnp.bfloat16), "fsdp", axis=0, tiled=True),
        lax.all_gather(norm1_bias.astype(jnp.bfloat16), "fsdp", axis=0, tiled=True),
        lax.all_gather(rel_table.astype(jnp.bfloat16), "fsdp", axis=0, tiled=True),
    )
    joined_proj, proj_bias, out_proj, out_shift, gain_one, shift_one, bias_table = attn_full
    proj_shift = proj_bias.astype(jnp.float32)
    content_rows = content_stream.reshape(row_count, width)
    query_rows = query_stream.reshape(row_count, width)
    content_proj = jnp.dot(content_rows, joined_proj, preferred_element_type=jnp.float32)
    content_queries = (content_proj[:, :width] + proj_shift[:width]).astype(jnp.bfloat16)
    content_keys = content_proj[:, width : 2 * width].astype(jnp.bfloat16)
    content_values = (content_proj[:, 2 * width :] + proj_shift[width:]).astype(jnp.bfloat16)
    stream_queries = (
        jnp.dot(query_rows, joined_proj[:, :width], preferred_element_type=jnp.float32)
        + proj_shift[:width]
    ).astype(jnp.bfloat16)
    bucket_index = jnp.asarray(relative_buckets(seq_len)).reshape(1, seq_len * seq_len)
    one_hot = (bucket_index == jnp.arange(BUCKETS, dtype=jnp.int32)[:, None]).astype(jnp.bfloat16)
    bias_full = rows_inner(bias_table, one_hot).reshape(head_count, seq_len, seq_len)
    ffn_full = (
        lax.all_gather(ffn_in_weight.astype(jnp.bfloat16), "fsdp", axis=0, tiled=True),
        lax.all_gather(ffn_in_bias.astype(jnp.bfloat16), "fsdp", axis=0, tiled=True),
        lax.all_gather(ffn_out_weight.astype(jnp.bfloat16), "fsdp", axis=0, tiled=True),
        lax.all_gather(ffn_out_bias.astype(jnp.bfloat16), "fsdp", axis=0, tiled=True),
        lax.all_gather(norm2_gain.astype(jnp.bfloat16), "fsdp", axis=0, tiled=True),
        lax.all_gather(norm2_bias.astype(jnp.bfloat16), "fsdp", axis=0, tiled=True),
    )
    in_proj, in_shift, out_ffn, ffn_shift, gain_two, shift_two = ffn_full

    def shaped(rows_in):
        return rows_in.reshape(seq_count, seq_len, head_count, head_width)

    def forward_one(entries):
        own_query, own_keys, own_values, other_query, length_one, rank_row = entries
        content_mask, query_mask = key_masks(length_one, rank_row)
        mixed_own, total_own = attend_forward(
            own_query, own_keys, own_values, bias_full, content_mask
        )
        mixed_other, total_other = attend_forward(
            other_query, own_keys, own_values, bias_full, query_mask
        )
        return (mixed_own, mixed_other, total_own, total_other)

    mixed_content, mixed_query, total_content, total_query = lax.map(
        forward_one,
        (
            shaped(content_queries),
            shaped(content_keys),
            shaped(content_values),
            shaped(stream_queries),
            lengths,
            factor_order,
        ),
    )
    mixed_rows = jnp.concatenate(
        [mixed_content.reshape(row_count, width), mixed_query.reshape(row_count, width)], 0
    )
    input_rows = jnp.concatenate([content_rows, query_rows], 0).astype(jnp.float32)
    branch = jnp.dot(mixed_rows, out_proj, preferred_element_type=jnp.float32) + out_shift.astype(
        jnp.float32
    )
    first_out, normed_one, inverse_one = norm_forward(
        input_rows + branch, gain_one.astype(jnp.float32), shift_one.astype(jnp.float32)
    )
    first_low = first_out.astype(jnp.bfloat16)
    hidden_in = jnp.dot(first_low, in_proj, preferred_element_type=jnp.float32) + in_shift.astype(
        jnp.float32
    )
    hidden_low = gelu_value(hidden_in).astype(jnp.bfloat16)
    ffn_rows = jnp.dot(hidden_low, out_ffn, preferred_element_type=jnp.float32) + ffn_shift.astype(
        jnp.float32
    )
    final_rows, normed_two, inverse_two = norm_forward(
        first_low.astype(jnp.float32) + ffn_rows,
        gain_two.astype(jnp.float32),
        shift_two.astype(jnp.float32),
    )
    attn_back = (
        lax.all_gather(qkv_weight.astype(jnp.bfloat16), "fsdp", axis=0, tiled=True),
        lax.all_gather(qv_bias.astype(jnp.bfloat16), "fsdp", axis=0, tiled=True),
        lax.all_gather(out_weight.astype(jnp.bfloat16), "fsdp", axis=0, tiled=True),
        lax.all_gather(out_bias.astype(jnp.bfloat16), "fsdp", axis=0, tiled=True),
        lax.all_gather(norm1_gain.astype(jnp.bfloat16), "fsdp", axis=0, tiled=True),
        lax.all_gather(norm1_bias.astype(jnp.bfloat16), "fsdp", axis=0, tiled=True),
        lax.all_gather(rel_table.astype(jnp.bfloat16), "fsdp", axis=0, tiled=True),
    )
    ffn_back = (
        lax.all_gather(ffn_in_weight.astype(jnp.bfloat16), "fsdp", axis=0, tiled=True),
        lax.all_gather(ffn_in_bias.astype(jnp.bfloat16), "fsdp", axis=0, tiled=True),
        lax.all_gather(ffn_out_weight.astype(jnp.bfloat16), "fsdp", axis=0, tiled=True),
        lax.all_gather(ffn_out_bias.astype(jnp.bfloat16), "fsdp", axis=0, tiled=True),
        lax.all_gather(norm2_gain.astype(jnp.bfloat16), "fsdp", axis=0, tiled=True),
        lax.all_gather(norm2_bias.astype(jnp.bfloat16), "fsdp", axis=0, tiled=True),
    )
    back_joined = attn_back[0]
    back_out_proj = attn_back[2]
    back_gain_one = attn_back[4].astype(jnp.float32)
    back_in_proj = ffn_back[0]
    back_out_ffn = ffn_back[2]
    back_gain_two = ffn_back[4].astype(jnp.float32)
    valid_rows = (
        (jnp.arange(seq_len)[None, :] < lengths[:, None]).reshape(row_count, 1).astype(jnp.float32)
    )
    valid_both = jnp.concatenate([valid_rows, valid_rows], 0)
    upstream = (
        jnp.concatenate(
            [content_cot.reshape(row_count, width), query_cot.reshape(row_count, width)], 0
        ).astype(jnp.float32)
        * valid_both
    )
    grad_sum_two, grad_gain_two, grad_shift_two = norm_backward(
        upstream, normed_two, inverse_two, back_gain_two
    )
    grad_ffn = grad_sum_two.astype(jnp.bfloat16)
    grad_ffn_shift = jnp.sum(grad_ffn.astype(jnp.float32), 0)
    grad_out_ffn = rows_inner(hidden_low, grad_ffn)
    grad_hidden = (times_transpose(grad_ffn, back_out_ffn) * gelu_slope(hidden_in)).astype(
        jnp.bfloat16
    )
    grad_in_shift = jnp.sum(grad_hidden.astype(jnp.float32), 0)
    grad_in_proj = rows_inner(first_low, grad_hidden)
    grad_first = grad_sum_two + times_transpose(grad_hidden, back_in_proj)
    ffn_grads = (
        lax.psum_scatter(
            grad_in_proj.astype(jnp.bfloat16), "fsdp", scatter_dimension=0, tiled=True
        ).astype(jnp.float32),
        lax.psum_scatter(
            grad_in_shift.astype(jnp.bfloat16), "fsdp", scatter_dimension=0, tiled=True
        ).astype(jnp.float32),
        lax.psum_scatter(
            grad_out_ffn.astype(jnp.bfloat16), "fsdp", scatter_dimension=0, tiled=True
        ).astype(jnp.float32),
        lax.psum_scatter(
            grad_ffn_shift.astype(jnp.bfloat16), "fsdp", scatter_dimension=0, tiled=True
        ).astype(jnp.float32),
        lax.psum_scatter(
            grad_gain_two.astype(jnp.bfloat16), "fsdp", scatter_dimension=0, tiled=True
        ).astype(jnp.float32),
        lax.psum_scatter(
            grad_shift_two.astype(jnp.bfloat16), "fsdp", scatter_dimension=0, tiled=True
        ).astype(jnp.float32),
    )
    grad_sum_one, grad_gain_one, grad_shift_one = norm_backward(
        grad_first, normed_one, inverse_one, back_gain_one
    )
    grad_branch = grad_sum_one.astype(jnp.bfloat16)
    grad_out_shift = jnp.sum(grad_branch.astype(jnp.float32), 0)
    grad_out_proj = rows_inner(mixed_rows, grad_branch)
    grad_mixed = times_transpose(grad_branch, back_out_proj).astype(jnp.bfloat16)

    def backward_one(running, entries):
        (
            own_query,
            own_keys,
            own_values,
            other_query,
            length_one,
            rank_row,
            total_own,
            total_other,
            grad_own,
            grad_other,
        ) = entries
        content_mask, query_mask = key_masks(length_one, rank_row)
        query_own, keys_own, values_own, logits_own = attend_backward(
            own_query, own_keys, own_values, bias_full, content_mask, total_own, grad_own
        )
        query_other, keys_other, values_other, logits_other = attend_backward(
            other_query, own_keys, own_values, bias_full, query_mask, total_other, grad_other
        )
        flat_shape = (seq_len, width)
        results = (
            query_own.reshape(flat_shape).astype(jnp.bfloat16),
            (keys_own + keys_other).reshape(flat_shape).astype(jnp.bfloat16),
            (values_own + values_other).reshape(flat_shape).astype(jnp.bfloat16),
            query_other.reshape(flat_shape).astype(jnp.bfloat16),
        )
        return (running + logits_own + logits_other, results)

    grad_bias_full, (grad_cq, grad_keys_all, grad_values_all, grad_sq) = lax.scan(
        backward_one,
        jnp.zeros((head_count, seq_len, seq_len), jnp.float32),
        (
            shaped(content_queries),
            shaped(content_keys),
            shaped(content_values),
            shaped(stream_queries),
            lengths,
            factor_order,
            total_content,
            total_query,
            shaped(grad_mixed[:row_count]),
            shaped(grad_mixed[row_count:]),
        ),
    )
    grad_joined_rows = jnp.concatenate([grad_cq, grad_keys_all, grad_values_all], -1).reshape(
        row_count, 3 * width
    )
    grad_stream_rows = grad_sq.reshape(row_count, width)
    grad_joined = rows_inner(content_rows, grad_joined_rows)
    grad_joined = jnp.concatenate(
        [grad_joined[:, :width] + rows_inner(query_rows, grad_stream_rows), grad_joined[:, width:]],
        1,
    )
    grad_proj_shift = jnp.concatenate(
        [
            jnp.sum(grad_joined_rows[:, :width].astype(jnp.float32), 0)
            + jnp.sum(grad_stream_rows.astype(jnp.float32), 0),
            jnp.sum(grad_joined_rows[:, 2 * width :].astype(jnp.float32), 0),
        ]
    )
    offset_totals = diagonal_sums(grad_bias_full)
    offset_bucket = jnp.asarray(bucket_of(np.arange(2 * seq_len - 1) - (seq_len - 1)))
    bucket_match = offset_bucket[None, :] == jnp.arange(BUCKETS, dtype=jnp.int32)[:, None]
    grad_table = jnp.sum(jnp.where(bucket_match[:, None, :], offset_totals[None, :, :], 0.0), -1)
    content_grad_rows = grad_sum_one[:row_count] + times_transpose(grad_joined_rows, back_joined)
    query_grad_rows = grad_sum_one[row_count:] + times_transpose(
        grad_stream_rows, back_joined[:, :width]
    )
    attn_grads = (
        lax.psum_scatter(
            grad_joined.astype(jnp.bfloat16), "fsdp", scatter_dimension=0, tiled=True
        ).astype(jnp.float32),
        lax.psum_scatter(
            grad_proj_shift.astype(jnp.bfloat16), "fsdp", scatter_dimension=0, tiled=True
        ).astype(jnp.float32),
        lax.psum_scatter(
            grad_out_proj.astype(jnp.bfloat16), "fsdp", scatter_dimension=0, tiled=True
        ).astype(jnp.float32),
        lax.psum_scatter(
            grad_out_shift.astype(jnp.bfloat16), "fsdp", scatter_dimension=0, tiled=True
        ).astype(jnp.float32),
        lax.psum_scatter(
            grad_gain_one.astype(jnp.bfloat16), "fsdp", scatter_dimension=0, tiled=True
        ).astype(jnp.float32),
        lax.psum_scatter(
            grad_shift_one.astype(jnp.bfloat16), "fsdp", scatter_dimension=0, tiled=True
        ).astype(jnp.float32),
        lax.psum_scatter(
            grad_table.astype(jnp.bfloat16), "fsdp", scatter_dimension=0, tiled=True
        ).astype(jnp.float32),
    )
    summed = (
        lax.psum(attn_grads[0].astype(jnp.bfloat16), "rep").astype(jnp.float32),
        lax.psum(attn_grads[1].astype(jnp.bfloat16), "rep").astype(jnp.float32),
        lax.psum(attn_grads[2].astype(jnp.bfloat16), "rep").astype(jnp.float32),
        lax.psum(attn_grads[3].astype(jnp.bfloat16), "rep").astype(jnp.float32),
        lax.psum(attn_grads[4].astype(jnp.bfloat16), "rep").astype(jnp.float32),
        lax.psum(attn_grads[5].astype(jnp.bfloat16), "rep").astype(jnp.float32),
        lax.psum(attn_grads[6].astype(jnp.bfloat16), "rep").astype(jnp.float32),
        lax.psum(ffn_grads[0].astype(jnp.bfloat16), "rep").astype(jnp.float32),
        lax.psum(ffn_grads[1].astype(jnp.bfloat16), "rep").astype(jnp.float32),
        lax.psum(ffn_grads[2].astype(jnp.bfloat16), "rep").astype(jnp.float32),
        lax.psum(ffn_grads[3].astype(jnp.bfloat16), "rep").astype(jnp.float32),
        lax.psum(ffn_grads[4].astype(jnp.bfloat16), "rep").astype(jnp.float32),
        lax.psum(ffn_grads[5].astype(jnp.bfloat16), "rep").astype(jnp.float32),
    )
    block_shape = (seq_count, seq_len, width)
    return (
        final_rows[:row_count].reshape(block_shape).astype(jnp.bfloat16),
        final_rows[row_count:].reshape(block_shape).astype(jnp.bfloat16),
        content_grad_rows.reshape(block_shape).astype(jnp.bfloat16),
        query_grad_rows.reshape(block_shape).astype(jnp.bfloat16),
        summed[0],
        summed[1],
        summed[2],
        summed[3],
        summed[4],
        summed[5],
        summed[6],
        summed[7],
        summed[8],
        summed[9],
        summed[10],
        summed[11],
        summed[12],
    )


def solution(mesh):
    in_specs = (
        P(("rep", "fsdp"), None, None),
        P(("rep", "fsdp"), None, None),
        P(("rep", "fsdp")),
        P(("rep", "fsdp"), None),
        P("fsdp", None),
        P("fsdp"),
        P("fsdp", None),
        P("fsdp"),
        P("fsdp"),
        P("fsdp"),
        P("fsdp", None),
        P("fsdp", None),
        P("fsdp"),
        P("fsdp", None),
        P("fsdp"),
        P("fsdp"),
        P("fsdp"),
        P(("rep", "fsdp"), None, None),
        P(("rep", "fsdp"), None, None),
    )
    out_specs = (
        P(("rep", "fsdp"), None, None),
        P(("rep", "fsdp"), None, None),
        P(("rep", "fsdp"), None, None),
        P(("rep", "fsdp"), None, None),
        P("fsdp", None),
        P("fsdp"),
        P("fsdp", None),
        P("fsdp"),
        P("fsdp"),
        P("fsdp"),
        P("fsdp", None),
        P("fsdp", None),
        P("fsdp"),
        P("fsdp", None),
        P("fsdp"),
        P("fsdp"),
        P("fsdp"),
    )
    return jax.shard_map(
        on_device, mesh=mesh, in_specs=in_specs, out_specs=out_specs, check_vma=False
    )
```

profile of v0, /device:TPU:0, one launch (start us, length us, event | category | flops | bytes accessed | tf_op | source)
XLA Modules:
  0.0 1033.8 jit_solution(10308287838263649911)
XLA Ops:
  19.7 32.4 %all-reduce.18 = (bf16[1536]{0:T(1024)(128)(2,1)S(1)}, bf16[768]{0:T(1024)(128)(2,1)S(1)}, bf16[768]{0:T(1024)(128)(2,1)S(1)}, bf16[768]{0:T(1024)(128)(2,1)S(1)...) all-reduce(bf16[1536]{0:T(1024)(128)(2,1)S(1)} %dynamic-update-slic, ...), channel_id=1, replica_groups=mesh['rep'=4,'fsdp'=8] {'fsdp'}, use_global_device_ids=true, to_apply=%add.1 | all-reduce | flops 5376 | bytes 21504
  55.7 8.4 all-gather
  64.2 13.1 %all-gather.1 = bf16[8,1,384]{2,1,0:T(2,128)(2,1)S(1)} all-gather(bf16[1,1,384]{2,1,0:T(2,128)(2,1)S(1)} %reshape.592), channel_id=1, replica_groups=mesh['rep'=4,'fsdp'=8] {'fsdp'}, dimensions={0}, use_global_device_ids=true | all-gather | bytes 6912 | tf_op jit(solution)/shard_map/all_gather | solution.py:196
  83.7 19.1 %copy.167 = f32[2,8,512,512]{3,2,1,0:T(8,128)} copy(f32[2,8,512,512]{3,1,2,0:T(8,128)S(1)} %bitcast.270) | data formatting | bytes 33554432
  102.8 10.8 %slice.91 = f32[12,512,512]{2,1,0:T(8,128)} slice(f32[16,512,512]{2,1,0:T(8,128)} %bitcast.273), slice={[0:12], [0:512], [0:512]} | slice | bytes 25165824 | tf_op jit(solution)/shard_map/reshape | solution.py:193
  113.6 12.8 %copy.138 = f32[12,512,512]{1,2,0:T(8,128)} copy(f32[12,512,512]{2,1,0:T(8,128)} %slice.91) | data formatting | bytes 25165824 | tf_op jit(solution)/shard_map/while | solution.py:218
  169.1 85.7 %while.35 = (s32[]{:T(128)}, bf16[2,512,12,64]{1,3,2,0:T(8,128)(2,1)}, bf16[2,512,12,64]{1,3,2,0:T(8,128)(2,1)}, f32[2,12,512]{2,1,0:T(8,128)}, f32[2,12,512]{2,...) while((s32[]{:T(128)}, ...), condition=%wide.region_5.6_spmd, body=%wide.region_0.5_spmd.sunk | while | flops 1669583872 | bytes 215413072 | solution.py:218
  171.2 9.0 fusion.166
  180.3 6.6 fusion.167
  186.9 7.0 fusion.168
  200.2 6.5 fusion.170
  213.9 8.9 fusion.166
  222.9 6.5 fusion.167
  229.4 7.0 fusion.168
  242.7 6.5 fusion.170
  261.9 6.6 fusion.104
  272.1 20.1 %multiply_convert_fusion.3 = (bf16[2048,3072]{1,0:T(8,128)(2,1)}, f32[2048,3072]{1,0:T(8,128)}) fusion(f32[3072]{0:T(1024)S(1)} %bitcast.298, bf16[768,3072]{1,0:T(8,128)(2,1)} %all-gather.11.cloned.1.call-done, f32[2048,768]{1,0:T(8,128)} %copy-done.12, f32[768]{0:T(1024)S(1)} %copy-done.58, f32[768]{0:T(1024)S(1)} %copy-done.49, ...), kind=kOutput, calls=%fused_computation.118 | convolution fusion | flops 9709289472 | bytes 48793600 | tf_op jit(solution)/shard_map/dot_general | solution.py:240
  292.2 16.2 %fusion.105 = (f32[2048]{0:T(1024)S(1)}, f32[2048,768]{1,0:T(8,128)S(1)}) fusion(f32[768]{0:T(1024)S(1)} %copy-done.60, bf16[2048,3072]{1,0:T(8,128)(2,1)} %get-tuple-element.552, bf16[3072,768]{1,0:T(8,128)(2,1)} %all-gather.13.cloned.1.call-done, f32[768]{0:T(1024)S(1)} %copy-done.58, f32[768]{0:T(1024)S(1)} %copy-done.49, ...), kind=kOutput, calls=%fused_computation.200 | convolution fusion | flops 9677830144 | bytes 29918208 | tf_op jit(solution)/shard_map/dot_general | solution.py:244
  323.3 24.3 %fusion.106 = (bf16[3072]{0:T(1024)(128)(2,1)}, bf16[2048,3072]{1,0:T(8,128)(2,1)}) fusion(f32[2048,3072]{1,0:T(8,128)} %get-tuple-element.553, f32[3072]{0:T(1024)S(1)} %bitcast.299, bf16[3072,768]{1,0:T(8,128)(2,1)S(1)} %bitcast.301, f32[2048,768]{1,0:T(8,128)S(1)} %get-tuple-element.516), kind=kOutput, calls=%fused_computation.201 | convolution fusion | flops 9740743680 | bytes 48777216 | tf_op jit(solution)/shard_map/dot_general | solution.py:81
  347.6 19.1 %multiply_reduce_fusion.3 = (bf16[768]{0:T(1024)(128)(2,1)}, f32[2048]{0:T(1024)S(1)}, f32[2048]{0:T(1024)S(1)}, bf16[768]{0:T(1024)(128)(2,1)}, f32[2048,768]{1,0:T(8,128)}) fusion(f32[2048,768]{1,0:T(8,128)S(1)} %bitcast.275, f32[2048]{0:T(1024)S(1)} %add_rsqrt_fusion.1, f32[2048]{0:T(1024)S(1)} %broadcast_multiply_fusion.5, f32[768]{0:T(1024)S(1)} %copy-done.49, ...), kind=kOutput, calls=%fused_computation.122 | convolution fusion | flops 9679398912 | bytes 36214784 | tf_op jit(solution)/shard_map/dot_general | solution.py:81
  391.8 194.9 %while.36 = (s32[]{:T(128)}, f32[12,512,512]{1,2,0:T(8,128)}, bf16[2,512,768]{1,2,0:T(8,128)(2,1)}, bf16[2,512,768]{1,2,0:T(8,128)(2,1)}, bf16[2,512,768]{1,2,0:...) while((s32[]{:T(128)}, f32[12,512,512]{1,2,0:T(8,128)}, ...), condition=%wide.region_17.18_spmd.clone, body=%wide.region_14.17_spmd.clone.sunk | while | flops 4103984128 | bytes 424424064 | solution.py:354
  394.5 8.3 fusion.188
  402.9 10.3 multiply_reduce_fusion.11
  413.1 8.1 fusion.192
  427.6 10.3 multiply_reduce_fusion.12
  437.9 7.2 add_convert_fusion.9
  445.1 26.9 %fusion.190 = (bf16[12,512,512]{1,2,0:T(8,128)(2,1)}, f32[12,512,512]{1,2,0:T(8,128)}, bf16[12,512,512]{1,2,0:T(8,128)(2,1)}) fusion(f32[12,512,512]{1,2,0:T(8,128)} %get-tuple-element.770, f32[12,512,512]{1,2,0:T(8,128)} %fusion.188, f32[12,512]{1,0:T(8,128)S(1)} %get-tuple-element.771, f32[12,512,512]{1,2,0:T(8,128)} %get-tuple-element.774, ...), kind=kLoop, calls=%fused_computation.52.clone.1 | loop fusion | flops 28311552 | bytes 88129536 | tf_op jit(solution)/shard_map/while/body/eval_jaxpr/convert_element_type | solution.py:133
  489.8 8.3 fusion.188
  498.1 10.3 multiply_reduce_fusion.11
  508.4 8.1 fusion.192
  522.9 10.3 multiply_reduce_fusion.12
  533.2 7.2 add_convert_fusion.9
  540.4 30.6 %fusion.190 = (bf16[12,512,512]{1,2,0:T(8,128)(2,1)}, f32[12,512,512]{1,2,0:T(8,128)}, bf16[12,512,512]{1,2,0:T(8,128)(2,1)}) fusion(f32[12,512,512]{1,2,0:T(8,128)} %get-tuple-element.770, f32[12,512,512]{1,2,0:T(8,128)} %fusion.188, f32[12,512]{1,0:T(8,128)S(1)} %get-tuple-element.771, f32[12,512,512]{1,2,0:T(8,128)} %get-tuple-element.774, ...), kind=kLoop, calls=%fused_computation.52.clone.1 | loop fusion | flops 28311552 | bytes 88129536 | tf_op jit(solution)/shard_map/while/body/eval_jaxpr/convert_element_type | solution.py:133
  602.3 7.4 convolution_convert_fusion.3
  609.8 16.5 %convolution_convert_fusion = bf16[3072,768]{1,0:T(8,128)(2,1)} fusion(bf16[2048,3072]{1,0:T(8,128)(2,1)} %get-tuple-element.552, f32[2048,768]{1,0:T(8,128)} %copy-done.16), kind=kOutput, calls=%fused_computation.141 | convolution fusion | flops 9667608576 | bytes 23592960 | tf_op jit(solution)/shard_map/dot_general | solution.py:75
  626.5 18.1 %convolution_convert_fusion.1 = bf16[768,3072]{1,0:T(8,128)(2,1)} fusion(bf16[2048,3072]{1,0:T(8,128)(2,1)} %get-tuple-element.558, f32[2048,768]{1,0:T(8,128)} %copy-done.12, f32[768]{0:T(1024)S(1)} %copy-done.59, f32[768]{0:T(1024)S(1)} %copy-done.50, f32[2048]{0:T(1024)S(1)} %copy-done.47, f32[2048]{0:T(1024)S(1)} %copy-done.42), kind=kOutput, calls=%fused_computation.142 | convolution fusion | flops 9673900032 | bytes 23615488 | tf_op jit(solution)/shard_map/dot_general | solution.py:75
  649.3 6.8 copy.151
  656.1 96.0 %rev.3 = f32[12,512,512]{1,2,0:T(8,128)} reverse(f32[12,512,512]{1,2,0:T(8,128)} %get-tuple-element.181), dimensions={2} | reverse | bytes 25165824 | tf_op jit(solution)/shard_map/rev | solution.py:39
  752.1 12.7 %copy.166 = f32[12,512,512]{2,1,0:T(8,128)} copy(f32[12,512,512]{1,2,0:T(8,128)} %rev.3) | data formatting | bytes 25165824
  764.8 14.5 %pad.4.clone = f32[12,512,1024]{2,1,0:T(8,128)} pad(f32[12,512,512]{2,1,0:T(8,128)} %copy.166, f32[]{:T(128)} %constant.84.clone.1), padding=0_0x0_0x0_512 | pad | bytes 37748740 | tf_op jit(solution)/shard_map/jit(_pad)/pad | solution.py:40
  779.3 11.0 %pad.15 = f32[16,512,1024]{2,1,0:T(8,128)S(1)} pad(f32[12,512,1024]{2,1,0:T(8,128)} %pad.4.clone, f32[]{:T(128)} %constant.84.clone.1), padding=0_4x0_0x0_0 | pad | bytes 58720260
  790.3 39.7 %copy.171 = f32[2,8,512,1024]{3,1,2,0:T(8,128)} copy(f32[2,8,512,1024]{3,2,1,0:T(8,128)S(1)} %bitcast.268) | data formatting | bytes 67108864
  830.1 22.6 %slice.90 = f32[12,523776]{1,0:T(8,128)} slice(f32[12,524288]{1,0:T(8,128)} %bitcast.269), slice={[0:12], [0:523776]} | slice | bytes 50282496 | tf_op jit(solution)/shard_map/slice | solution.py:41
  852.7 41.6 %reshape.567 = f32[12,512,1023]{2,1,0:T(8,128)} reshape(f32[12,523776]{1,0:T(8,128)} %slice.90) | data formatting | bytes 50282496 | tf_op jit(solution)/shard_map/reshape | solution.py:42
  894.4 9.0 reduce_sum.239
  907.5 27.2 %all-reduce.17 = (bf16[768]{0:T(1024)(128)(2,1)S(1)}, bf16[1536]{0:T(1024)(128)(2,1)S(1)}, bf16[768]{0:T(1024)(128)(2,1)S(1)}, bf16[768]{0:T(1024)(128)(2,1)S(1)...) all-reduce(bf16[768]{0:T(1024)(128)(2,1)S(1)} %dynamic-update-slice, ...), channel_id=1, replica_groups=mesh['rep'=4,'fsdp'=8] {'fsdp'}, use_global_device_ids=true, to_apply=%add.7 | all-reduce | flops 10368 | bytes 41472
  935.3 9.8 all-reduce.19
  969.7 49.2 %all-reduce.23.cloned.1.call-done = (bf16[96,2304]{0,1:T(8,128)(2,1)}, bf16[96,768]{1,0:T(8,128)(2,1)}, bf16[96,3072]{1,0:T(8,128)(2,1)}, bf16[384,768]{1,0:T(8,128)(2,1)}) async-done(((bf16[96,2304]{0,1:T(8,128)(2,1)}, bf16[96,768]{1,0:T(8,128)(2,1)}, bf16[96,3072]{1,0:T(8,128)(2,1)}, bf16[384,768]{1,0:T(8,128)(2,1)}), (bf16[96,2304]{0,1:T(8,128)(2,1)}, bf16[96,768]{1,0:T(8,128)(2,1)}, ...) | async-done | bytes 1769488 | tf_op jit(solution)/shard_map/psum | solution.py:418
  (441 shorter events, 243.5 us)
Async XLA Ops:
  7.2 70.6 %copy-start.31 = (s32[262144]{0:T(1024)S(1)}, s32[262144]{0:T(1024)}, u32[]{:S(2)}) copy-start(s32[262144]{0:T(1024)} %constant.103) | copy-start | bytes 3145732
  7.3 10.5 %copy-start.65 = (f32[4,12]{1,0:T(4,128)S(1)}, f32[4,12]{1,0:T(4,128)}, u32[]{:S(2)}) copy-start(f32[4,12]{1,0:T(4,128)} %param.35) | copy-start | bytes 580
  7.3 10.5 %copy-start.66 = (f32[384]{0:T(512)S(1)}, f32[384]{0:T(512)}, u32[]{:S(2)}) copy-start(f32[384]{0:T(512)} %param.37) | copy-start | bytes 4612
  7.3 10.5 %copy-start.67 = (s32[2]{0:T(128)S(1)}, s32[2]{0:T(128)}, u32[]{:S(2)}) copy-start(s32[2]{0:T(128)} %param.27) | copy-start | bytes 28
  7.3 119.1 %all-gather.7.cloned.1.call-start = ((), (), s32[]{:S(2)}) async-start(), calls=%async_computation.4 | async-start | bytes 3981312 | tf_op jit(solution)/shard_map/all_gather | solution.py:171
  9.4 252.5 %all-gather.9.cloned.1.call-start = ((), (), s32[]{:S(2)}) async-start(), calls=%async_computation.5 | async-start | bytes 1327104 | tf_op jit(solution)/shard_map/all_gather | solution.py:173
  11.1 260.9 %all-gather.11.cloned.1.call-start = ((), (), s32[]{:S(2)}) async-start(), calls=%async_computation.6 | async-start | bytes 5308416 | tf_op jit(solution)/shard_map/all_gather | solution.py:195
  13.4 278.8 %all-gather.13.cloned.1.call-start = ((), (), s32[]{:S(2)}) async-start(), calls=%async_computation.7 | async-start | bytes 5308416 | tf_op jit(solution)/shard_map/all_gather | solution.py:197
  15.6 937.8 %reduce-scatter.13.cloned.1.call-start = ((), (), s32[]{:S(2)}) async-start(), calls=%async_computation.11 | async-start | bytes 3981312
  113.6 12.8 %copy-start.72 = (bf16[2,512,768]{2,1,0:T(8,128)(2,1)S(1)}, bf16[2,512,768]{2,1,0:T(8,128)(2,1)}, u32[]{:S(2)}) copy-start(bf16[2,512,768]{2,1,0:T(8,128)(2,1)} %param.26) | copy-start | bytes 4718596
  157.9 11.1 %copy-start.39 = (s32[2,512]{1,0:T(2,128)S(1)}, s32[2,512]{1,0:T(2,128)}, u32[]{:S(2)}) copy-start(s32[2,512]{1,0:T(2,128)} %param.28) | copy-start | bytes 12292
  157.9 11.1 %copy-start.68 = (s32[2]{0:T(128)S(1)}, s32[2]{0:T(128)}, u32[]{:S(2)}) copy-start(s32[2]{0:T(128)} %param.27) | copy-start | bytes 28
  180.2 13.7 %slice-start = ((s8[12582912]{0:T(1024)(128)(4,1)}), s8[4194304]{0:T(1024)(128)(4,1)S(1)}, s32[]{:S(2)}) async-start(s8[12582912]{0:T(1024)(128)(4,1)} %bitcast.262), calls=%async_computation.13 | async-start | bytes 8388608 | tf_op jit(solution)/shard_map/while
  222.9 13.6 %slice-start = ((s8[12582912]{0:T(1024)(128)(4,1)}), s8[4194304]{0:T(1024)(128)(4,1)S(1)}, s32[]{:S(2)}) async-start(s8[12582912]{0:T(1024)(128)(4,1)} %bitcast.262), calls=%async_computation.13 | async-start | bytes 8388608 | tf_op jit(solution)/shard_map/while
  268.6 98.2 %copy-start.41 = (f32[2048]{0:T(1024)}, f32[2048]{0:T(1024)S(1)}, u32[]{:S(2)}) copy-start(f32[2048]{0:T(1024)S(1)} %broadcast_multiply_fusion.5) | copy-start | bytes 24580
  272.0 94.8 %copy-start.46 = (f32[2048]{0:T(1024)}, f32[2048]{0:T(1024)S(1)}, u32[]{:S(2)}) copy-start(f32[2048]{0:T(1024)S(1)} %add_rsqrt_fusion.1) | copy-start | bytes 24580
  272.1 20.1 %copy-start.60 = (f32[768]{0:T(1024)S(1)}, f32[768]{0:T(1024)}, u32[]{:S(2)}) copy-start(f32[768]{0:T(1024)} %convert_element_type.367) | copy-start | bytes 9220
  309.4 13.9 %copy-start.37 = (f32[2048]{0:T(1024)}, f32[2048]{0:T(1024)S(1)}, u32[]{:S(2)}) copy-start(f32[2048]{0:T(1024)S(1)} %add_rsqrt_fusion) | copy-start | bytes 24580
  312.6 10.6 %slice-start.9 = ((s8[4718592]{0:T(1024)(128)(4,1)}), s8[4194304]{0:T(1024)(128)(4,1)S(1)}, s32[]{:S(2)}) async-start(s8[4718592]{0:T(1024)(128)(4,1)} %bitcast.300), calls=%async_computation.22 | async-start | bytes 8388608
  318.7 28.9 %slice-start.5 = ((s8[6291456]{0:T(1024)(128)(4,1)}), s8[4194304]{0:T(1024)(128)(4,1)S(1)}, s32[]{:S(2)}) async-start(s8[6291456]{0:T(1024)(128)(4,1)} %bitcast.274), calls=%async_computation.18 | async-start | bytes 8388608
  323.2 24.4 %copy-start.16 = (f32[2048,768]{1,0:T(8,128)}, f32[2048,768]{1,0:T(8,128)S(1)}, u32[]{:S(2)}) copy-start(f32[2048,768]{1,0:T(8,128)S(1)} %get-tuple-element.516) | copy-start | bytes 18874372
  323.3 24.4 %slice-start.6 = ((s8[6291456]{0:T(1024)(128)(4,1)}), s8[2097152]{0:T(1024)(128)(4,1)S(1)}, s32[]{:S(2)}) async-start(s8[6291456]{0:T(1024)(128)(4,1)} %bitcast.274), calls=%async_computation.19 | async-start | bytes 4194304
  379.4 12.4 %copy-start.4 = (bf16[2,512,12,64]{1,3,2,0:T(8,128)(2,1)S(1)}, bf16[2,512,12,64]{1,3,2,0:T(8,128)(2,1)}, u32[]{:S(2)}) copy-start(bf16[2,512,12,64]{1,3,2,0:T(8,128)(2,1)} %copy-done.3) | copy-start | bytes 4718596
  379.4 12.4 %copy-start.33 = (f32[2,12,512]{2,1,0:T(8,128)S(1)}, f32[2,12,512]{2,1,0:T(8,128)}, u32[]{:S(2)}) copy-start(f32[2,12,512]{2,1,0:T(8,128)} %get-tuple-element.833) | copy-start | bytes 147460
  379.4 12.4 %copy-start.34 = (f32[2,12,512]{2,1,0:T(8,128)S(1)}, f32[2,12,512]{2,1,0:T(8,128)}, u32[]{:S(2)}) copy-start(f32[2,12,512]{2,1,0:T(8,128)} %get-tuple-element.829) | copy-start | bytes 147460
  379.4 12.4 %copy-start.40 = (s32[2,512]{1,0:T(2,128)S(1)}, s32[2,512]{1,0:T(2,128)}, u32[]{:S(2)}) copy-start(s32[2,512]{1,0:T(2,128)} %param.28) | copy-start | bytes 12292
  379.4 12.4 %copy-start.69 = (s32[2]{0:T(128)S(1)}, s32[2]{0:T(128)}, u32[]{:S(2)}) copy-start(s32[2]{0:T(128)} %param.27) | copy-start | bytes 28
  602.3 353.2 %reduce-scatter.7.cloned.1.call-start = ((), (), s32[]{:S(2)}) async-start(), calls=%async_computation.8 | async-start | bytes 1327104 | tf_op jit(solution)/shard_map/reduce_scatter | solution.py:401
  609.7 16.7 %copy-start.42 = (f32[2048]{0:T(1024)S(1)}, f32[2048]{0:T(1024)}, u32[]{:S(2)}) copy-start(f32[2048]{0:T(1024)} %copy-done.41) | copy-start | bytes 24580
  609.7 16.7 %copy-start.47 = (f32[2048]{0:T(1024)S(1)}, f32[2048]{0:T(1024)}, u32[]{:S(2)}) copy-start(f32[2048]{0:T(1024)} %copy-done.46) | copy-start | bytes 24580
  609.7 16.7 %copy-start.50 = (f32[768]{0:T(1024)S(1)}, f32[768]{0:T(1024)}, u32[]{:S(2)}) copy-start(f32[768]{0:T(1024)} %convert_element_type.356) | copy-start | bytes 9220
  609.7 16.7 %copy-start.59 = (f32[768]{0:T(1024)S(1)}, f32[768]{0:T(1024)}, u32[]{:S(2)}) copy-start(f32[768]{0:T(1024)} %convert_element_type.358) | copy-start | bytes 9220
  609.7 345.7 %reduce-scatter.11.cloned.1.call-start = ((), (), s32[]{:S(2)}) async-start(), calls=%async_computation.10 | async-start | bytes 5308416 | tf_op jit(solution)/shard_map/reduce_scatter | solution.py:304
  626.4 20.9 %copy-start.81 = (f32[96]{0:T(128)S(1)}, f32[96]{0:T(128)}, u32[]{:S(2)}) copy-start(f32[96]{0:T(128)} %param.41) | copy-start | bytes 1156
  626.4 21.3 %copy-start.57 = (s32[1023]{0:T(1024)S(1)}, s32[1023]{0:T(1024)}, u32[]{:S(2)}) copy-start(s32[1023]{0:T(1024)} %constant.93.clone) | copy-start | bytes 12280
  626.4 21.3 %copy-start.20 = (bf16[2,512,768]{1,2,0:T(8,128)(2,1)S(1)}, bf16[2,512,768]{1,2,0:T(8,128)(2,1)}, u32[]{:S(2)}) copy-start(bf16[2,512,768]{1,2,0:T(8,128)(2,1)} %get-tuple-element.180) | copy-start | bytes 4718596
  626.4 329.1 %reduce-scatter.9.cloned.1.call-start = ((), (), s32[]{:S(2)}) async-start(), calls=%async_computation.9 | async-start | bytes 5308416 | tf_op jit(solution)/shard_map/reduce_scatter | solution.py:298
  644.6 374.3 %all-reduce.23.cloned.1.call-start = ((), (), s32[]{:S(2)}) async-start(), calls=%async_computation.12 | async-start | bytes 3833856 | tf_op jit(solution)/shard_map/psum | solution.py:418
  894.3 13.1 %copy-start.52 = (bf16[768]{0:T(1024)(128)(2,1)S(1)}, bf16[768]{0:T(1024)(128)(2,1)}, u32[]{:S(2)}) copy-start(bf16[768]{0:T(1024)(128)(2,1)} %get-tuple-element.422) | copy-start | bytes 4612
  894.3 13.1 %copy-start.53 = (bf16[768]{0:T(1024)(128)(2,1)S(1)}, bf16[768]{0:T(1024)(128)(2,1)}, u32[]{:S(2)}) copy-start(bf16[768]{0:T(1024)(128)(2,1)} %get-tuple-element.427) | copy-start | bytes 4612
  894.3 13.1 %copy-start.54 = (bf16[768]{0:T(1024)(128)(2,1)S(1)}, bf16[768]{0:T(1024)(128)(2,1)}, u32[]{:S(2)}) copy-start(bf16[768]{0:T(1024)(128)(2,1)} %get-tuple-element.515) | copy-start | bytes 4612
  894.3 13.1 %copy-start.55 = (bf16[768]{0:T(1024)(128)(2,1)S(1)}, bf16[768]{0:T(1024)(128)(2,1)}, u32[]{:S(2)}) copy-start(bf16[768]{0:T(1024)(128)(2,1)} %get-tuple-element.517) | copy-start | bytes 4612
  894.4 13.1 %copy-start.56 = (bf16[3072]{0:T(1024)(128)(2,1)S(1)}, bf16[3072]{0:T(1024)(128)(2,1)}, u32[]{:S(2)}) copy-start(bf16[3072]{0:T(1024)(128)(2,1)} %get-tuple-element.557) | copy-start | bytes 18436
  894.4 13.1 %copy-start.62 = (bf16[768]{0:T(1024)(128)(2,1)S(1)}, bf16[768]{0:T(1024)(128)(2,1)}, u32[]{:S(2)}) copy-start(bf16[768]{0:T(1024)(128)(2,1)} %get-tuple-element.420) | copy-start | bytes 4612
  894.4 13.1 %copy-start.63 = (bf16[768]{0:T(1024)(128)(2,1)S(1)}, bf16[768]{0:T(1024)(128)(2,1)}, u32[]{:S(2)}) copy-start(bf16[768]{0:T(1024)(128)(2,1)} %get-tuple-element.425) | copy-start | bytes 4612
  894.4 55.6 %copy-start.36 = (f32[2048]{0:T(1024)S(1)}, f32[2048]{0:T(1024)}, u32[]{:S(2)}) copy-start(f32[2048]{0:T(1024)} %copy-done.35) | copy-start | bytes 24580
  894.4 55.5 %copy-start.38 = (f32[2048]{0:T(1024)S(1)}, f32[2048]{0:T(1024)}, u32[]{:S(2)}) copy-start(f32[2048]{0:T(1024)} %copy-done.37) | copy-start | bytes 24580
  894.4 55.5 %copy-start.45 = (f32[768]{0:T(1024)S(1)}, f32[768]{0:T(1024)}, u32[]{:S(2)}) copy-start(f32[768]{0:T(1024)} %convert_element_type.369) | copy-start | bytes 9220
  (75 other events, 417.6 us)
Sparse Core Ops, SparseCore 0:
  10.3 44.7 all-gather.6
  57.4 21.7 all-gather.8
  81.4 50.8 all-gather.10
  134.4 49.9 all-gather.12
  602.4 42.5 reduce-scatter.12
  647.7 31.4 reduce-scatter.6
  681.5 53.0 reduce-scatter.10
  736.9 53.3 reduce-scatter.8
  955.6 63.1 all-reduce.22
where the time goes:
time: 1050 us; the launch traced here: 1030 us
  local copies, waits for them, and re-layouts  386 us (37%)
  matrix products  336 us (32%)
  other arithmetic  150 us (14%)
  blocking collectives  90.9 us (9%)
  waiting for transfers between devices  49.4 us (5%)
  between operations  19.4 us (2%)
    unnamed x184, local copies, waits for them, and re-layouts  112 us
    rev x1, local copies, waits for them, and re-layouts, diagonal_sums(): flipped = grid[:, :, ::-1]  96 us
    dot_general x8, matrix products, scores_of(): jnp.einsum('ihd,jhd->hij', query_block, key_block, preferred_element_type...  71.4 us
    unnamed x2, blocking collectives  59.6 us
    dot_general x5, matrix products, times_transpose(): lax.dot_general(left_op, right_op, (((1,), (1,)), ((), ())), preferred_el...  58.6 us
    convert_element_type x2, other arithmetic, attend_backward(): grad_low = grad_logits.astype(jnp.bfloat16)  57.5 us
    dot_general x6, matrix products, rows_inner(): lax.dot_general(left_op, right_op, (((0,), (0,)), ((), ())), preferred_el...  53.3 us
    psum x1, waiting for transfers between devices, on_device(): lax.psum(attn_grads[0].astype(jnp.bfloat16), 'rep').astype(jnp.float32)  49.2 us
  transfers between devices with their start and end apart: 9, of which 1 were waited for; matrix products, arithmetic and copies ran while one was open for 53% of the time, Pallas kernels for 0%

commit v1 on v0

v1 whole, which is shorter than its diff:
```python
import functools, math
import jax, jax.numpy as jnp, numpy as np
from jax import lax
from jax.experimental import pallas as pl
from jax.experimental.pallas import tpu as pltpu
from jax.sharding import PartitionSpec as P

HEADS = 12
HEAD = 64
BUCKETS = 32
MAX_DIST = 128
LANE = 128
NEAR = 512
MASKED = -1e30
LOG2E = 1.4426950408889634
LN2 = 0.6931471805599453
F32 = jnp.float32
BF16 = jnp.bfloat16


def bucket_of(offset):
    half_count = BUCKETS // 2
    result = (offset < 0).astype(np.int64) * half_count
    distance = np.abs(offset)
    exact_count = half_count // 2
    fraction = np.log(np.maximum(distance, 1) / exact_count) / np.log(MAX_DIST / exact_count)
    beyond = exact_count + (fraction * (half_count - exact_count)).astype(np.int64)
    beyond = np.minimum(beyond, half_count - 1)
    result = result + np.where(distance < exact_count, distance, beyond)
    return result.astype(np.int32)


def nt(a, b):
    return lax.dot_general(a, b, (((1,), (1,)), ((), ())), preferred_element_type=F32)


def nn(a, b):
    return lax.dot_general(a, b, (((1,), (0,)), ((), ())), preferred_element_type=F32)


def signed_places():
    places = np.arange(NEAR)
    return np.where(places < NEAR - LANE + 0, places, places - NEAR)


def near_onehot(sign):
    offset = sign * (signed_places() - LANE)
    return (bucket_of(offset)[None, :] == np.arange(BUCKETS)[:, None]).astype(np.float32)


def skewed(row, width):
    wide = jnp.broadcast_to(row, (LANE, NEAR))
    return pltpu.roll(wide, 0, 1, stride=1, stride_axis=0)[:, :width]


def tile_bias(near, far_pos, far_neg, seq_len, sign):
    blocks = seq_len // LANE
    rows = []
    for rb in range(blocks):
        parts = []
        for cb in range(blocks):
            e = cb - rb
            if abs(e) <= 1:
                parts.append(near[:, (e + 1) * LANE : (e + 2) * LANE])
            else:
                parts.append(jnp.broadcast_to(far_pos if e * sign > 0 else far_neg, (LANE, LANE)))
        rows.append(jnp.concatenate(parts, 1))
    return rows


def head_lanes(shape, t):
    lane = lax.broadcasted_iota(jnp.int32, shape, 1)
    return (lane >= t * HEAD) & (lane < (t + 1) * HEAD)


def fwd_kernel(len_ref, q_ref, k_ref, v_ref, g_ref, ord_ref, near_ref, far_ref, oc_ref, og_ref, lc_ref, lg_ref, mask_ref):
    hp = pl.program_id(0)
    s = pl.program_id(1)
    seq_len = q_ref.shape[0]
    blocks = seq_len // LANE

    @pl.when(hp == 0)
    def _():
        own = ord_ref[pl.ds(s, 1), :].astype(F32)
        cols = jnp.broadcast_to(own, (LANE, seq_len)).T
        place = lax.broadcasted_iota(jnp.int32, (LANE, seq_len), 1)
        keep = place < len_ref[s]
        for rb in range(blocks):
            col = cols[rb * LANE : (rb + 1) * LANE, :]
            rank = jnp.concatenate([col] * blocks, 1)
            ok = keep & ((place == 0) | (own <= rank))
            mask_ref[s, rb * LANE : (rb + 1) * LANE, :] = jnp.where(ok, 0.0, MASKED)

    keys = k_ref[...]
    values = jnp.concatenate([v_ref[...], jnp.ones((seq_len, LANE), BF16)], 1)
    lane = lax.broadcasted_iota(jnp.int32, (seq_len, LANE), 1)
    outs = [[], []]
    totals = [jnp.zeros((seq_len, LANE), F32), jnp.zeros((seq_len, LANE), F32)]
    for t in range(2):
        head = hp * 2 + t
        sel = head_lanes((seq_len, LANE), t)
        near = skewed(near_ref[pl.ds(head, 1), :], 3 * LANE)
        far = far_ref[pl.ds(head, 1), :]
        bias = tile_bias(near, far[:, 0:1], far[:, 1:2], seq_len, -1)
        for stream in range(2):
            src = q_ref if stream == 0 else g_ref
            query = jnp.where(sel, src[...], jnp.zeros((), BF16))
            raw = nt(query, keys)
            probs = []
            maxes = []
            for rb in range(blocks):
                part = raw[rb * LANE : (rb + 1) * LANE, :] + (bias[rb] + mask_ref[s, rb * LANE : (rb + 1) * LANE, :])
                if stream == 1:
                    r = lax.broadcasted_iota(jnp.int32, (LANE, LANE), 0)
                    c = lax.broadcasted_iota(jnp.int32, (LANE, LANE), 1)
                    hit = r == c
                    if rb == 0:
                        hit = hit & (c != 0)
                    diag = jnp.where(hit, MASKED, part[:, rb * LANE : (rb + 1) * LANE])
                    pieces = []
                    if rb > 0:
                        pieces.append(part[:, : rb * LANE])
                    pieces.append(diag)
                    if rb < blocks - 1:
                        pieces.append(part[:, (rb + 1) * LANE :])
                    part = jnp.concatenate(pieces, 1)
                top = jnp.max(part, 1, keepdims=True)
                probs.append(jnp.exp2(part - top).astype(BF16))
                maxes.append(jnp.broadcast_to(top, (LANE, LANE)))
            prob = jnp.concatenate(probs, 0)
            mixed = nn(prob, values)
            total = mixed[:, LANE:]
            outs[stream].append(mixed[:, :LANE] / total)
            log_total = jnp.concatenate(maxes, 0) + jnp.log2(total)
            hi = log_total.astype(BF16).astype(F32)
            totals[stream] = jnp.where(lane == head, -hi, jnp.where(lane == head + HEAD, hi - log_total, totals[stream]))
    first = head_lanes((seq_len, LANE), 0)
    oc_ref[...] = jnp.where(first, outs[0][0], outs[0][1]).astype(BF16)
    og_ref[...] = jnp.where(first, outs[1][0], outs[1][1]).astype(BF16)
    mine = (lane == hp * 2) | (lane == hp * 2 + 1) | (lane == hp * 2 + HEAD) | (lane == hp * 2 + 1 + HEAD)
    for ref, total in ((lc_ref, totals[0]), (lg_ref, totals[1])):
        low = total.astype(BF16)

        @pl.when(hp == 0)
        def _():
            ref[s] = low

        @pl.when(hp > 0)
        def _():
            ref[s] = jnp.where(mine, low, ref[s])


def attention_forward(qkv, qg, lengths, order, table):
    rows, width = qg.shape
    seqs, seq_len = order.shape
    pairs = width // LANE
    near = jnp.dot(table.astype(F32).T, jnp.asarray(near_onehot(-1)), precision=lax.Precision.HIGHEST) * LOG2E
    tab2 = table.astype(F32).T * LOG2E
    far = jnp.concatenate([tab2[:, BUCKETS // 2 - 1 : BUCKETS // 2], tab2[:, BUCKETS - 1 : BUCKETS]], 1)
    block = lambda off: pl.BlockSpec((seq_len, LANE), lambda h, s, off=off: (s, off + h))
    whole = lambda a: pl.BlockSpec(a.shape, lambda h, s: (0,) * a.ndim)
    return pl.pallas_call(
        fwd_kernel,
        grid=(pairs, seqs),
        in_specs=[
            pl.BlockSpec(memory_space=pltpu.SMEM),
            block(0), block(pairs), block(2 * pairs), block(0),
            whole(order), whole(near), whole(far),
        ],
        out_specs=[block(0), block(0),
                   pl.BlockSpec((seqs, seq_len, LANE), lambda h, s: (0, 0, 0)),
                   pl.BlockSpec((seqs, seq_len, LANE), lambda h, s: (0, 0, 0))],
        out_shape=[jax.ShapeDtypeStruct((rows, width), BF16)] * 2 + [jax.ShapeDtypeStruct((seqs, seq_len, LANE), BF16)] * 2,
        scratch_shapes=[pltpu.VMEM((seqs, seq_len, seq_len), F32)],
        compiler_params=pltpu.CompilerParams(dimension_semantics=("arbitrary", "arbitrary"), vmem_limit_bytes=56 * 2**20),
        name="attention_forward",
    )(lengths, qkv, qkv, qkv, qg, order, near, far)


def bwd_kernel(len_ref, q_ref, k_ref, v_ref, g_ref, dc_ref, dg_ref, oc_ref, og_ref, lc_ref, lg_ref, ord_ref, near_ref, far_ref,
               dq_ref, dk_ref, dv_ref, dqg_ref, sums_ref, mask_ref, acc_ref, ds_ref):
    hp = pl.program_id(0)
    s = pl.program_id(1)
    last = pl.num_programs(1) - 1
    seq_len = q_ref.shape[0]
    blocks = seq_len // LANE
    half = seq_len // 2

    @pl.when(hp == 0)
    def _():
        own = ord_ref[pl.ds(s, 1), :].astype(F32)
        cols = jnp.broadcast_to(own, (LANE, seq_len)).T
        for rb in range(blocks):
            col = cols[rb * LANE : (rb + 1) * LANE, :]
            rank = jnp.concatenate([col] * blocks, 1)
            place = lax.broadcasted_iota(jnp.int32, (LANE, seq_len), 0) + rb * LANE
            ok = (place < len_ref[s]) & ((place == 0) | (rank <= own))
            mask_ref[s, rb * LANE : (rb + 1) * LANE, :] = jnp.where(ok, 0.0, MASKED)

    lane = lax.broadcasted_iota(jnp.int32, (seq_len, LANE), 1)
    ones = jnp.ones((seq_len, LANE), BF16)
    zero = jnp.zeros((), BF16)
    keys = k_ref[...]
    keys_wide = jnp.concatenate([keys, ones], 1)
    values_wide = jnp.concatenate([v_ref[...], ones], 1)
    keys_turned = keys.astype(F32).T.astype(BF16)
    lane_r = lax.broadcasted_iota(jnp.int32, (LANE, LANE), 0)
    lane_c = lax.broadcasted_iota(jnp.int32, (LANE, LANE), 1)
    pick = (lane_r // HEAD == lane_c).astype(BF16)
    grad_keys = None
    grad_values = None
    grad_query = [[], []]
    streams = []
    for src, grad, out, tot in ((q_ref, dc_ref, oc_ref, lc_ref), (g_ref, dg_ref, og_ref, lg_ref)):
        g = grad[...]
        delta = nn((g.astype(F32) * out[...].astype(F32)).astype(BF16), pick)
        hi = delta.astype(BF16)
        streams.append((src[...], g, -delta, tot[0]))
    for t in range(2):
        head = hp * 2 + t
        sel = head_lanes((seq_len, LANE), t)
        near = skewed(near_ref[pl.ds(head, 1), :], 3 * LANE)
        far = far_ref[pl.ds(head, 1), :]
        bias = tile_bias(near, far[:, 0:1], far[:, 1:2], seq_len, 1)
        for c0 in range(0, seq_len, half):
            both = None
            for stream in range(2):
                q, g, delta, tot = streams[stream]
                q = jnp.where(sel, q, zero)[c0 : c0 + half]
                g = jnp.where(sel, g, zero)[c0 : c0 + half]
                d = delta[c0 : c0 + half]
                ln = lane[c0 : c0 + half]
                tt = jnp.where((ln == head) | (ln == head + HEAD), tot[c0 : c0 + half], zero)
                dd = jnp.where(ln == t, d, 0.0)
                dhi = dd.astype(BF16)
                dlo = pltpu.roll(dd - dhi.astype(F32), HEAD, 1).astype(BF16)
                raw = nt(keys_wide, jnp.concatenate([q, tt], 1))
                dpr = nt(values_wide, jnp.concatenate([g, dhi + dlo], 1))
                probs, grads = [], []
                for rb in range(blocks):
                    sl = slice(rb * LANE, (rb + 1) * LANE)
                    part = raw[sl] + (bias[rb][:, c0 : c0 + half] + mask_ref[s, sl, c0 : c0 + half])
                    r0 = rb * LANE
                    if stream == 1 and c0 <= r0 < c0 + half:
                        hit = lane_r == lane_c
                        if rb == 0:
                            hit = hit & (lane_r != 0)
                        x0 = r0 - c0
                        diag = jnp.where(hit, MASKED, part[:, x0 : x0 + LANE])
                        pieces = []
                        if x0 > 0:
                            pieces.append(part[:, :x0])
                        pieces.append(diag)
                        if x0 + LANE < half:
                            pieces.append(part[:, x0 + LANE :])
                        part = jnp.concatenate(pieces, 1)
                    p = jnp.exp2(part)
                    probs.append(p.astype(BF16))
                    grads.append(p * dpr[sl])
                low = [x.astype(BF16) for x in grads]
                prob = jnp.concatenate(probs, 0)
                gl = jnp.concatenate(low, 0)
                gv = nn(prob, g)
                gk = nn(gl, q)
                grad_values = gv if grad_values is None else grad_values + gv
                grad_keys = gk if grad_keys is None else grad_keys + gk
                grad_query[stream].append(nn(keys_turned[t * HEAD : (t + 1) * HEAD], gl))
                both = grads if both is None else [a + b for a, b in zip(both, grads)]
            sums = {}
            for rb in range(blocks):
                for cb in range(half // LANE):
                    e = cb + c0 // LANE - rb
                    e = max(-2, min(2, e))
                    x = both[rb][:, cb * LANE : (cb + 1) * LANE]
                    sums[e] = x if e not in sums else sums[e] + x
            for e, x in sums.items():
                lanes = slice((e + 2) * LANE, (e + 3) * LANE)
                fresh = c0 == 0
                if fresh:
                    @pl.when(s == 0)
                    def _():
                        acc_ref[t, :, lanes] = x

                    @pl.when(s > 0)
                    def _():
                        acc_ref[t, :, lanes] = acc_ref[t, :, lanes] + x
                else:
                    acc_ref[t, :, lanes] = acc_ref[t, :, lanes] + x
            if c0 == 0:
                for e in range(-2, 3):
                    if e not in sums:
                        @pl.when(s == 0)
                        def _():
                            acc_ref[t, :, (e + 2) * LANE : (e + 3) * LANE] = jnp.zeros((LANE, LANE), F32)
    count = seq_len // half
    scale = 1.0 / math.sqrt(HEAD)
    for stream, ref in ((0, dq_ref), (1, dqg_ref)):
        pieces = grad_query[stream]
        top = jnp.concatenate(pieces[:count], 1)
        bot = jnp.concatenate(pieces[count:], 1)
        ref[...] = (jnp.concatenate([top, bot], 0) * scale).T.astype(BF16)
    dk_ref[...] = (grad_keys * LN2).astype(BF16)
    dv_ref[...] = grad_values.astype(BF16)

    @pl.when(s == last)
    def _():
        for t in range(2):
            near = jnp.concatenate([acc_ref[t, :, LANE : 4 * LANE], jnp.zeros((LANE, LANE), F32)], 1)
            mirror = (lane_r + lane_c == LANE - 1).astype(F32)
            flipped = lax.dot_general(mirror, near, (((1,), (0,)), ((), ())), precision=lax.Precision.HIGHEST, preferred_element_type=F32)
            turned = pltpu.roll(flipped, 0, 1, stride=1, stride_axis=0)
            row = jnp.sum(turned, 0, keepdims=True)
            below = jnp.sum(acc_ref[t, :, :LANE], 0, keepdims=True)
            above = jnp.sum(acc_ref[t, :, 4 * LANE :], 0, keepdims=True)
            sums_ref[pl.ds(hp * 2 + t, 1), :] = jnp.concatenate([row, below, above], 1)


def attention_backward(qkv, qg, grad_c, grad_g, out_c, out_g, tot_c, tot_g, lengths, order, table):
    rows, width = qg.shape
    seqs, seq_len = order.shape
    pairs = width // LANE
    near = jnp.dot(table.astype(F32).T, jnp.asarray(near_onehot(1)), precision=lax.Precision.HIGHEST) * LOG2E
    tab2 = table.astype(F32).T * LOG2E
    far = jnp.concatenate([tab2[:, BUCKETS // 2 - 1 : BUCKETS // 2], tab2[:, BUCKETS - 1 : BUCKETS]], 1)
    block = lambda off: pl.BlockSpec((seq_len, LANE), lambda h, s, off=off: (s, off + h))
    whole = lambda a: pl.BlockSpec(a.shape, lambda h, s: (0,) * a.ndim)
    tot = pl.BlockSpec((1, seq_len, LANE), lambda h, s: (s, 0, 0))
    outs = pl.pallas_call(
        bwd_kernel,
        grid=(pairs, seqs),
        in_specs=[
            pl.BlockSpec(memory_space=pltpu.SMEM),
            block(0), block(pairs), block(2 * pairs), block(0),
            block(0), block(0), block(0), block(0), tot, tot,
            whole(order), whole(near), whole(far),
        ],
        out_specs=[block(0)] * 4 + [pl.BlockSpec((2 * pairs, NEAR + 2 * LANE), lambda h, s: (0, 0))],
        out_shape=[jax.ShapeDtypeStruct((rows, width), BF16)] * 4 + [jax.ShapeDtypeStruct((2 * pairs, NEAR + 2 * LANE), F32)],
        scratch_shapes=[pltpu.VMEM((seqs, seq_len, seq_len), F32), pltpu.VMEM((2, LANE, 5 * LANE), F32), pltpu.VMEM((8, LANE), F32)],
        compiler_params=pltpu.CompilerParams(dimension_semantics=("arbitrary", "arbitrary"), vmem_limit_bytes=56 * 2**20),
        name="attention_backward",
    )(lengths, qkv, qkv, qkv, qg, grad_c, grad_g, out_c, out_g, tot_c, tot_g, order, near, far)
    sums = outs[4]
    fold = np.zeros((NEAR + 2 * LANE, BUCKETS), np.float32)
    fold[:NEAR] = np.roll(near_onehot(1).T, LANE - 1, 0)
    fold[NEAR : NEAR + LANE, BUCKETS - 1] = 1
    fold[NEAR + LANE :, BUCKETS // 2 - 1] = 1
    grad_table = jnp.dot(sums, jnp.asarray(fold), precision=lax.Precision.HIGHEST).T
    return list(outs[:4]) + [grad_table]


eps_norm = 1e-05
root_half = 0.7071067811865476
inv_root_tau = 0.3989422804014327


def norm_forward(summed, gain_vec, shift_vec):
    row_mean = jnp.mean(summed, -1, keepdims=True)
    centered = summed - row_mean
    inverse = lax.rsqrt(jnp.mean(centered * centered, -1, keepdims=True) + eps_norm)
    normed = centered * inverse
    return (normed * gain_vec + shift_vec, normed, inverse)


def norm_backward(upstream, normed, inverse, gain_vec):
    scaled = upstream * gain_vec
    centered = (
        scaled
        - jnp.mean(scaled, -1, keepdims=True)
        - normed * jnp.mean(scaled * normed, -1, keepdims=True)
    )
    return (inverse * centered, jnp.sum(upstream * normed, 0), jnp.sum(upstream, 0))


def gelu_value(hidden_in):
    return 0.5 * hidden_in * (1.0 + lax.erf(hidden_in * root_half))


def gelu_slope(hidden_in):
    return (
        0.5 * (1.0 + lax.erf(hidden_in * root_half))
        + hidden_in * jnp.exp(-0.5 * hidden_in * hidden_in) * inv_root_tau
    )


def rows_inner(left_op, right_op):
    return lax.dot_general(
        left_op, right_op, (((0,), (0,)), ((), ())), preferred_element_type=jnp.float32
    )


def times_transpose(left_op, right_op):
    return lax.dot_general(
        left_op, right_op, (((1,), (1,)), ((), ())), preferred_element_type=jnp.float32
    )


def pack(parts):
    flat = jnp.concatenate([p.reshape(-1) for p in parts])
    return jnp.pad(flat, (0, -flat.shape[0] % LANE))


def on_device(content_stream, query_stream, lengths, factor_order, qkv_weight, qv_bias, out_weight, out_bias, norm1_gain, norm1_bias, rel_table, ffn_in_weight, ffn_in_bias, ffn_out_weight, ffn_out_bias, norm2_gain, norm2_bias, content_cot, query_cot):
    seq_count, seq_len, width = content_stream.shape
    row_count = seq_count * seq_len
    gather = lambda a: lax.all_gather(a, "fsdp", axis=0, tiled=True)
    small = (qv_bias, out_bias, norm1_gain, norm1_bias, rel_table, ffn_in_bias, ffn_out_bias, norm2_gain, norm2_bias)
    packed = lax.all_gather(pack([p.astype(BF16) for p in small]), "fsdp", axis=0, tiled=False)
    full = []
    at = 0
    for p in small:
        full.append(packed[:, at : at + p.size].reshape((-1,) + p.shape[1:]).astype(F32))
        at += p.size
    proj_shift, out_shift, gain_one, shift_one, table, in_shift, ffn_shift, gain_two, shift_two = full
    joined_proj = gather(qkv_weight.astype(BF16))
    out_proj = gather(out_weight.astype(BF16))
    in_proj = gather(ffn_in_weight.astype(BF16))
    out_ffn = gather(ffn_out_weight.astype(BF16))
    content_rows = content_stream.reshape(row_count, width)
    query_rows = query_stream.reshape(row_count, width)
    scale = LOG2E / math.sqrt(HEAD)
    shift = jnp.concatenate([proj_shift[:width] * scale, jnp.zeros((width,), F32), proj_shift[width:]])
    factor = jnp.concatenate([jnp.full((width,), scale, F32), jnp.ones((2 * width,), F32)])
    qkv = (jnp.dot(content_rows, joined_proj, preferred_element_type=F32) * factor + shift).astype(BF16)
    qg = (jnp.dot(query_rows, joined_proj[:, :width], preferred_element_type=F32) * scale + shift[:width]).astype(BF16)
    mixed_c, mixed_g, tot_c, tot_g = attention_forward(qkv, qg, lengths, factor_order, table)
    mixed_rows = jnp.concatenate([mixed_c, mixed_g], 0)
    input_rows = jnp.concatenate([content_rows, query_rows], 0).astype(F32)
    branch = jnp.dot(mixed_rows, out_proj, preferred_element_type=F32) + out_shift
    first_out, normed_one, inverse_one = norm_forward(input_rows + branch, gain_one, shift_one)
    first_low = first_out.astype(BF16)
    hidden_in = jnp.dot(first_low, in_proj, preferred_element_type=F32) + in_shift
    hidden_low = gelu_value(hidden_in).astype(BF16)
    ffn_rows = jnp.dot(hidden_low, out_ffn, preferred_element_type=F32) + ffn_shift
    final_rows, normed_two, inverse_two = norm_forward(first_low.astype(F32) + ffn_rows, gain_two, shift_two)
    valid_rows = (jnp.arange(seq_len)[None, :] < lengths[:, None]).reshape(row_count, 1).astype(F32)
    valid_both = jnp.concatenate([valid_rows, valid_rows], 0)
    upstream = jnp.concatenate([content_cot.reshape(row_count, width), query_cot.reshape(row_count, width)], 0).astype(F32) * valid_both
    grad_sum_two, grad_gain_two, grad_shift_two = norm_backward(upstream, normed_two, inverse_two, gain_two)
    grad_ffn = grad_sum_two.astype(BF16)
    grad_ffn_shift = jnp.sum(grad_ffn.astype(F32), 0)
    grad_out_ffn = rows_inner(hidden_low, grad_ffn)
    grad_hidden = (times_transpose(grad_ffn, out_ffn) * gelu_slope(hidden_in)).astype(BF16)
    grad_in_shift = jnp.sum(grad_hidden.astype(F32), 0)
    grad_in_proj = rows_inner(first_low, grad_hidden)
    grad_first = grad_sum_two + times_transpose(grad_hidden, in_proj)
    scatter = lambda a: lax.psum_scatter(a.astype(BF16), "fsdp", scatter_dimension=0, tiled=True)
    part_in = scatter(grad_in_proj)
    part_out = scatter(grad_out_ffn)
    grad_sum_one, grad_gain_one, grad_shift_one = norm_backward(grad_first, normed_one, inverse_one, gain_one)
    grad_branch = grad_sum_one.astype(BF16)
    grad_out_shift = jnp.sum(grad_branch.astype(F32), 0)
    grad_out_proj = rows_inner(mixed_rows, grad_branch)
    part_proj = scatter(grad_out_proj)
    grad_mixed = times_transpose(grad_branch, out_proj).astype(BF16)
    grad_cq, grad_k, grad_v, grad_sq, grad_table = attention_backward(qkv, qg, grad_mixed[:row_count], grad_mixed[row_count:], mixed_c, mixed_g, tot_c, tot_g, lengths, factor_order, table)
    grad_joined_rows = jnp.concatenate([grad_cq, grad_k, grad_v], -1)
    grad_joined = rows_inner(content_rows, grad_joined_rows)
    grad_joined = jnp.concatenate([grad_joined[:, :width] + rows_inner(query_rows, grad_sq), grad_joined[:, width:]], 1)
    part_joined = scatter(grad_joined)
    grad_proj_shift = jnp.concatenate([jnp.sum(grad_cq.astype(F32), 0) + jnp.sum(grad_sq.astype(F32), 0), jnp.sum(grad_v.astype(F32), 0)])
    content_grad_rows = grad_sum_one[:row_count] + times_transpose(grad_joined_rows, joined_proj)
    query_grad_rows = grad_sum_one[row_count:] + times_transpose(grad_sq, joined_proj[:, :width])
    grads_small = (grad_proj_shift, grad_out_shift, grad_gain_one, grad_shift_one, grad_table, grad_in_shift, grad_ffn_shift, grad_gain_two, grad_shift_two)
    own = lax.axis_index("fsdp")
    packed_grads = jnp.concatenate([g.reshape(packed.shape[0], -1) for g in grads_small], 1)
    packed_grads = lax.psum(packed_grads, ("rep", "fsdp"))
    mine = lax.dynamic_slice_in_dim(packed_grads, own, 1, 0)[0]
    outs_small = []
    at = 0
    for p in small:
        outs_small.append(mine[at : at + p.size].reshape(p.shape))
        at += p.size
    g_shift, g_out_shift, g_gain_one, g_shift_one, g_table, g_in_shift, g_ffn_shift, g_gain_two, g_shift_two = outs_small
    over = lambda a: lax.psum(a, "rep").astype(F32)
    block_shape = (seq_count, seq_len, width)
    return (
        final_rows[:row_count].reshape(block_shape).astype(BF16),
        final_rows[row_count:].reshape(block_shape).astype(BF16),
        content_grad_rows.reshape(block_shape).astype(BF16),
        query_grad_rows.reshape(block_shape).astype(BF16),
        over(part_joined), g_shift, over(part_proj), g_out_shift, g_gain_one, g_shift_one, g_table,
        over(part_in), g_in_shift, over(part_out), g_ffn_shift, g_gain_two, g_shift_two,
    )


def solution(mesh):
    in_specs = (
        P(("rep", "fsdp"), None, None),
        P(("rep", "fsdp"), None, None),
        P(("rep", "fsdp")),
        P(("rep", "fsdp"), None),
        P("fsdp", None),
        P("fsdp"),
        P("fsdp", None),
        P("fsdp"),
        P("fsdp"),
        P("fsdp"),
        P("fsdp", None),
        P("fsdp", None),
        P("fsdp"),
        P("fsdp", None),
        P("fsdp"),
        P("fsdp"),
        P("fsdp"),
        P(("rep", "fsdp"), None, None),
        P(("rep", "fsdp"), None, None),
    )
    out_specs = (
        P(("rep", "fsdp"), None, None),
        P(("rep", "fsdp"), None, None),
        P(("rep", "fsdp"), None, None),
        P(("rep", "fsdp"), None, None),
        P("fsdp", None),
        P("fsdp"),
        P("fsdp", None),
        P("fsdp"),
        P("fsdp"),
        P("fsdp"),
        P("fsdp", None),
        P("fsdp", None),
        P("fsdp"),
        P("fsdp", None),
        P("fsdp"),
        P("fsdp"),
        P("fsdp"),
    )
    return jax.shard_map(
        on_device, mesh=mesh, in_specs=in_specs, out_specs=out_specs, check_vma=False
    )
```

time: 1050 us -> 612 us (0.58); the launches traced: 1030 us -> 608 us
  local copies, waits for them, and re-layouts: 386 us -> 35.6 us
  matrix products: 336 us -> 164 us
  waiting for transfers between devices: 49.4 us -> 218 us
  other arithmetic: 150 us -> 39.3 us
  Pallas kernels: 0 us -> 79.8 us
  blocking collectives: 90.9 us -> 55.6 us
    dot_general x33 -> x8, matrix products: 224 us -> 56.5 us  [the longest x1 20.7 us: on_device(): jnp.dot(first_low, in_proj, preferred_element_type=F32) + in_shift]
    rev x1 -> x0, local copies, waits for them, and re-layouts: 96 us -> none  [diagonal_sums(): flipped = grid[:, :, ::-1]]
    unnamed x184 -> x89, local copies, waits for them, and re-layouts: 112 us -> 19.1 us
    reduce_scatter x3, waiting for transfers between devices: 0.01 us -> 86.2 us  [on_device(): lax.psum_scatter(a.astype(BF16), 'fsdp', scatter_dimension=0, tiled=True)]
    pallas_call x0 -> x2, Pallas kernels: none -> 79.8 us  [the longest x1 52.1 us: attention_backward(): pl.pallas_call(bwd_kernel, grid=(pairs, seqs), in_specs=[pl.BlockSpec(mem...]
    all_gather x4, waiting for transfers between devices: 0.05 us -> 76.7 us  [on_device(): gather = lambda a: lax.all_gather(a, 'fsdp', axis=0, tiled=True)]
    convert_element_type x34 -> x19, other arithmetic: 82.1 us -> 14.1 us  [the longest x3 5.97 us: on_device(): over = lambda a: lax.psum(a, 'rep').astype(F32)]
    reshape x8 -> x11, local copies, waits for them, and re-layouts: 72.8 us -> 6.1 us  [the longest x8 5.28 us: on_device(): g.reshape(packed.shape[0], -1)]
  transfers between devices with their start and end apart: 9 -> 9, of which waited for: 1 -> 6; matrix products, arithmetic and copies ran while one was open for 53% -> 21% of each run, Pallas kernels for 0% -> 5%
where the time goes in v1:
time: 612 us; the launch traced here: 608 us
  waiting for transfers between devices  218 us (36%)
  matrix products  164 us (27%)
  Pallas kernels  79.8 us (13%)
  blocking collectives  55.6 us (9%)
  other arithmetic  39.3 us (6%)
  local copies, waits for them, and re-layouts  35.6 us (6%)
  between operations  14.7 us (2%)
    reduce_scatter x3, waiting for transfers between devices, on_device(): lax.psum_scatter(a.astype(BF16), 'fsdp', scatter_dimension=0, tiled=True)  86.2 us
    all_gather x4, waiting for transfers between devices, on_device(): gather = lambda a: lax.all_gather(a, 'fsdp', axis=0, tiled=True)  76.7 us
    dot_general x5, matrix products, times_transpose(): lax.dot_general(left_op, right_op, (((1,), (1,)), ((), ())), preferred_el...  60.2 us
    psum x1, waiting for transfers between devices, on_device(): over = lambda a: lax.psum(a, 'rep').astype(F32)  54.9 us
    pallas_call x1, Pallas kernels, attention_backward(): pl.pallas_call(bwd_kernel, grid=(pairs, seqs), in_specs=[pl.BlockSpec(mem...  52.1 us
    dot_general x5, matrix products, rows_inner(): lax.dot_general(left_op, right_op, (((0,), (0,)), ((), ())), preferred_el...  47.6 us
    psum x1, blocking collectives, on_device(): packed_grads = lax.psum(packed_grads, ('rep', 'fsdp'))  39.5 us
    pallas_call x1, Pallas kernels, attention_forward(): pl.pallas_call(fwd_kernel, grid=(pairs, seqs), in_specs=[pl.BlockSpec(mem...  27.8 us
  transfers between devices with their start and end apart: 9, of which 6 were waited for; matrix products, arithmetic and copies ran while one was open for 21% of the time, Pallas kernels for 5%

profile of v1, /device:TPU:0, one launch (start us, length us, event | category | flops | bytes accessed | tf_op | source)
XLA Modules:
  0.0 607.9 jit_solution(227644887035281321)
XLA Ops:
  7.4 2.0 convert_element_type.224
  9.5 1.6 convert_element_type.238
  11.2 2.2 convert_element_type.247
  13.4 2.1 convert_element_type.251
  16.0 16.1 %all-gather.1 = bf16[8,1,1280]{2,1,0:T(2,128)(2,1)S(1)} all-gather(bf16[1,1,1280]{2,1,0:T(2,128)(2,1)S(1)} %reshape.260), channel_id=2, replica_groups=mesh['rep'=4,'fsdp'=8] {'fsdp'}, dimensions={0}, use_global_device_ids=true | all-gather | bytes 23040 | tf_op jit(solution)/shard_map/all_gather | solution.py:408
  35.5 19.2 %all-gather.7.cloned.1.call-done = bf16[768,2304]{1,0:T(8,128)(2,1)} async-done(((bf16[96,2304]{1,0:T(8,128)(2,1)}), bf16[768,2304]{1,0:T(8,128)(2,1)}) %all-gather.7.cloned.1.call-update) | async-done | bytes 3538960 | tf_op jit(solution)/shard_map/all_gather | solution.py:406
  54.8 4.4 add_convert_fusion.3.g_ref
  59.2 5.6 add_convert_fusion.q_ref.k_ref.v_ref
  64.8 27.8 %attention_forward.1 = (bf16[1024,768]{1,0:T(8,128)(2,1)}, bf16[1024,768]{1,0:T(8,128)(2,1)}, bf16[2,512,128]{2,1,0:T(8,128)(2,1)}, bf16[2,512,128]{2,1,0:T(8,128)(2,1)}) custom-call(s32[2]{0:T(128)} %len_ref.3, bf16[1024,2304]{1,0:T(8,128)(2,1)} %add_convert_fusion.q_ref.k_ref.v_ref, bf16[1024,2304]{1,0:T(8,128)(2,1)} %add_convert_fusion.q_ref.k_ref.v_ref, ...), custom_call_target="tpu_custom_call" | custom-call | tf_op jit(solution)/shard_map/attention_forward/pallas_call | solution.py:162
  94.1 1.5 constant_dynamic-update-slice_fusion
  95.7 6.5 %fusion.21 = (f32[2048]{0:T(1024)S(1)}, f32[2048,768]{1,0:T(8,128)S(1)}) fusion(f32[768]{0:T(1024)S(1)} %reshape.251, bf16[2048,768]{1,0:T(8,128)(2,1)S(1)} %constant_dynamic-update-slice_fusion, bf16[768,768]{1,0:T(8,128)(2,1)} %all-gather.9.cloned.1.call-done, bf16[1024,768]{1,0:T(8,128)(2,1)} %bitcast.89, bf16[1024,768]{1,0:T(8,128)(2,1)} %bitcast.85), kind=kOutput, calls=%fused_computation.100 | convolution fusion | flops 2426927104 | bytes 13773824 | tf_op jit(solution)/shard_map/dot_general | solution.py:429
  102.2 2.6 copy-done
  105.7 26.1 %all-gather.11.cloned.1.call-done = bf16[768,3072]{1,0:T(8,128)(2,1)} async-done(((bf16[96,3072]{1,0:T(8,128)(2,1)}), bf16[768,3072]{1,0:T(8,128)(2,1)}) %all-gather.11.cloned.1.call-update) | async-done | bytes 4718608 | tf_op jit(solution)/shard_map/all_gather | solution.py:406
  131.8 20.7 %multiply_convert_fusion = (bf16[2048,3072]{1,0:T(8,128)(2,1)}, f32[2048,3072]{1,0:T(8,128)}) fusion(f32[3072]{0:T(1024)S(1)} %reshape.254, bf16[768,3072]{1,0:T(8,128)(2,1)} %all-gather.11.cloned.1.call-done, f32[2048,768]{1,0:T(8,128)} %copy-done, f32[768]{0:T(1024)S(1)} %reshape.253, f32[768]{0:T(1024)S(1)} %reshape.252, f32[2048]{0:T(1024)S(1)} %add_rsqrt_fusion.1, ...), kind=kOutput, calls=%fused_computation.8 | convolution fusion | flops 9709289472 | bytes 48793600 | tf_op jit(solution)/shard_map/dot_general | solution.py:432
  152.5 31.4 %all-gather.13.cloned.1.call-done = bf16[3072,768]{1,0:T(8,128)(2,1)} async-done(((bf16[384,768]{1,0:T(8,128)(2,1)}), bf16[3072,768]{1,0:T(8,128)(2,1)}) %all-gather.13.cloned.1.call-update) | async-done | bytes 4718608 | tf_op jit(solution)/shard_map/all_gather | solution.py:406
  183.8 16.0 %fusion.22 = (f32[2048]{0:T(1024)S(1)}, f32[2048,768]{1,0:T(8,128)S(1)}) fusion(f32[768]{0:T(1024)S(1)} %reshape.255, bf16[2048,3072]{1,0:T(8,128)(2,1)} %get-tuple-element.125, bf16[3072,768]{1,0:T(8,128)(2,1)} %all-gather.13.cloned.1.call-done, f32[768]{0:T(1024)S(1)} %reshape.253, f32[768]{0:T(1024)S(1)} %reshape.252, f32[2048]{0:T(1024)S(1)} %add_rsqrt_fusion.1, ...), kind=kOutput, calls=%fused_computation.101 | convolution fusion | flops 9677830144 | bytes 29918208 | tf_op jit(solution)/shard_map/dot_general | solution.py:434
  201.8 6.1 multiply_reduce_fusion
  207.9 5.8 convert_reduce_fusion.1
  213.7 24.2 %convert_reduce_fusion = (f32[3072]{0:T(1024)}, bf16[2048,3072]{1,0:T(8,128)(2,1)}) fusion(f32[2048,3072]{1,0:T(8,128)} %get-tuple-element.126, f32[3072]{0:T(1024)S(1)} %reshape.254, bf16[3072,768]{1,0:T(8,128)(2,1)S(1)} %bitcast.84, f32[2048,768]{1,0:T(8,128)S(1)} %get-tuple-element.99), kind=kOutput, calls=%fused_computation.7 | convolution fusion | flops 9747035136 | bytes 48783360 | tf_op jit(solution)/shard_map/dot_general | solution.py:393
  237.9 19.6 %multiply_reduce_fusion.1 = (f32[768]{0:T(1024)}, f32[2048]{0:T(1024)S(1)}, f32[2048]{0:T(1024)S(1)}, f32[768]{0:T(1024)}, f32[2048,768]{1,0:T(8,128)}) fusion(f32[2048,768]{1,0:T(8,128)S(1)} %bitcast.66, f32[2048]{0:T(1024)S(1)} %add_rsqrt_fusion.1, f32[2048]{0:T(1024)S(1)} %broadcast_multiply_fusion.5, f32[768]{0:T(1024)S(1)} %reshape.252, ...), kind=kOutput, calls=%fused_computation.13 | convolution fusion | flops 9679398912 | bytes 36217856 | tf_op jit(solution)/shard_map/dot_general | solution.py:393
  257.6 5.3 convert_reduce_fusion.2
  262.8 2.9 convolution_convert_fusion.2
  265.8 1.9 fusion.18
  267.6 52.1 %attention_backward.1 = (bf16[1024,768]{1,0:T(8,128)(2,1)}, bf16[1024,768]{1,0:T(8,128)(2,1)}, bf16[1024,768]{1,0:T(8,128)(2,1)}, bf16[1024,768]{1,0:T(8,128)(2,1)}, f32[12,768]{1,0:T(8,128)}) custom-call(s32[2]{0:T(128)} %len_ref.3, bf16[1024,2304]{1,0:T(8,128)(2,1)} %add_convert_fusion.q_ref.k_ref.v_ref, ...), custom_call_target="tpu_custom_call" | custom-call | tf_op jit(solution)/shard_map/attention_backward/pallas_call | solution.py:328
  319.8 1.7 constant_dynamic-update-slice_fusion.4
  323.1 2.2 copy-done.9
  325.3 4.0 convolution_bitcast_fusion
  329.6 1.5 fusion.11
  331.4 4.0 copy.48
  335.4 7.4 %convolution_convert_fusion.3 = bf16[768,768]{1,0:T(8,128)(2,1)} fusion(bf16[2048,768]{1,0:T(8,128)(2,1)} %copy-done.8, f32[2048,768]{1,0:T(8,128)} %copy-done.3), kind=kOutput, calls=%fused_computation.50 | convolution fusion | flops 2418081792 | bytes 10616832 | tf_op jit(solution)/shard_map/dot_general | solution.py:387
  343.0 18.2 %convolution_convert_fusion.1 = bf16[768,3072]{1,0:T(8,128)(2,1)} fusion(bf16[2048,3072]{1,0:T(8,128)(2,1)} %get-tuple-element.131, f32[2048,768]{1,0:T(8,128)} %copy-done, f32[768]{0:T(1024)S(1)} %copy-done.17, f32[768]{0:T(1024)S(1)} %copy-done.14, f32[2048]{0:T(1024)S(1)} %add_rsqrt_fusion.1, f32[2048]{0:T(1024)S(1)} %broadcast_multiply_fusion.5), kind=kOutput, calls=%fused_computation.34 | convolution fusion | flops 9673900032 | bytes 23615488 | tf_op jit(solution)/shard_map/dot_general | solution.py:387
  361.2 16.5 %convolution_convert_fusion = bf16[3072,768]{1,0:T(8,128)(2,1)} fusion(bf16[2048,3072]{1,0:T(8,128)(2,1)} %get-tuple-element.125, f32[2048,768]{1,0:T(8,128)} %copy-done.4), kind=kOutput, calls=%fused_computation.33 | convolution fusion | flops 9667608576 | bytes 23592960 | tf_op jit(solution)/shard_map/dot_general | solution.py:387
  378.0 1.9 convert_reduce_fusion.4
  379.9 1.7 convert_reduce_fusion.5
  382.3 1.7 convert_reduce_fusion.3
  384.6 1.6 fusion.23
  392.3 39.5 %psum.36 = f32[8,1200]{1,0:T(8,128)S(1)} all-reduce(f32[8,1200]{1,0:T(8,128)S(1)} %concatenate.50), channel_id=1, replica_groups=mesh['rep'=4,'fsdp'=8] {'rep','fsdp'}, use_global_device_ids=true, to_apply=%region_20.21 | all-reduce | flops 9600 | bytes 76800 | tf_op jit(solution)/shard_map/psum | solution.py:467
  433.2 1.9 fusion.19
  435.1 2.2 copy.49
  437.3 30.5 %reduce-scatter.9.cloned.1.call-done = bf16[96,3072]{1,0:T(8,128)(2,1)} async-done(((bf16[768,3072]{1,0:T(8,128)(2,1)}), bf16[96,3072]{1,0:T(8,128)(2,1)}) %reduce-scatter.9.cloned.1.call-update) | async-done | bytes 589840 | tf_op jit(solution)/shard_map/reduce_scatter | solution.py:447
  467.8 55.7 %reduce-scatter.11.cloned.1.call-done = bf16[384,768]{1,0:T(8,128)(2,1)} async-done(((bf16[3072,768]{1,0:T(8,128)(2,1)}), bf16[384,768]{1,0:T(8,128)(2,1)}) %reduce-scatter.11.cloned.1.call-update) | async-done | bytes 589840 | tf_op jit(solution)/shard_map/reduce_scatter | solution.py:447
  524.7 5.4 fusion.9
  530.1 8.0 %fusion.10 = bf16[1024,768]{1,0:T(8,128)(2,1)} fusion(f32[2048,768]{1,0:T(8,128)S(1)} %bitcast.68, bf16[1024,2304]{1,0:T(8,128)(2,1)} %copy-done.9, bf16[768,2304]{1,0:T(8,128)(2,1)S(1)} %copy-done.21), kind=kOutput, calls=%fused_computation.42 | convolution fusion | flops 3625451520 | bytes 12976128 | tf_op jit(solution)/shard_map/dot_general | solution.py:393
  538.1 54.9 %all-reduce.4.cloned.1.call-done = (bf16[96,2304]{0,1:T(8,128)(2,1)}, bf16[96,768]{1,0:T(8,128)(2,1)}, bf16[96,3072]{1,0:T(8,128)(2,1)}, bf16[384,768]{1,0:T(8,128)(2,1)}) async-done(((bf16[96,2304]{0,1:T(8,128)(2,1)}, bf16[96,768]{1,0:T(8,128)(2,1)}, bf16[96,3072]{1,0:T(8,128)(2,1)}, bf16[384,768]{1,0:T(8,128)(2,1)}), (bf16[96,2304]{0,1:T(8,128)(2,1)}, bf16[96,768]{1,0:T(8,128)(2,1)}, ...) | async-done | bytes 1769488 | tf_op jit(solution)/shard_map/psum | solution.py:475
  593.0 2.2 convert_element_type.280
  595.1 2.2 convert_element_type.282
  597.3 2.2 copy.46
  599.5 1.6 convert_element_type.278
  (174 shorter events, 20.9 us)
Async XLA Ops:
  7.2 26.7 %copy-start.12 = (f32[32,512]{1,0:T(8,128)S(1)}, f32[32,512]{1,0:T(8,128)}, u32[]{:S(2)}) copy-start(f32[32,512]{1,0:T(8,128)} %constant.50.clone) | copy-start | bytes 196612
  7.2 27.5 %copy-start.11 = (f32[32,512]{1,0:T(8,128)S(1)}, f32[32,512]{1,0:T(8,128)}, u32[]{:S(2)}) copy-start(f32[32,512]{1,0:T(8,128)} %constant.51.clone) | copy-start | bytes 196612
  7.2 8.4 %copy-start.18 = (f32[4,12]{1,0:T(4,128)S(1)}, f32[4,12]{1,0:T(4,128)}, u32[]{:S(2)}) copy-start(f32[4,12]{1,0:T(4,128)} %param.32) | copy-start | bytes 580
  7.2 8.5 %copy-start.19 = (f32[384]{0:T(512)S(1)}, f32[384]{0:T(512)}, u32[]{:S(2)}) copy-start(f32[384]{0:T(512)} %param.34) | copy-start | bytes 4612
  7.2 8.5 %copy-start.26 = (f32[192]{0:T(256)S(1)}, f32[192]{0:T(256)}, u32[]{:S(2)}) copy-start(f32[192]{0:T(256)} %param.27) | copy-start | bytes 2308
  7.2 8.5 %copy-start.27 = (f32[96]{0:T(128)S(1)}, f32[96]{0:T(128)}, u32[]{:S(2)}) copy-start(f32[96]{0:T(128)} %param.29) | copy-start | bytes 1156
  7.3 8.5 %copy-start.28 = (f32[96]{0:T(128)S(1)}, f32[96]{0:T(128)}, u32[]{:S(2)}) copy-start(f32[96]{0:T(128)} %param.30) | copy-start | bytes 1156
  7.3 8.5 %copy-start.29 = (f32[96]{0:T(128)S(1)}, f32[96]{0:T(128)}, u32[]{:S(2)}) copy-start(f32[96]{0:T(128)} %param.31) | copy-start | bytes 1156
  7.3 8.5 %copy-start.30 = (f32[96]{0:T(128)S(1)}, f32[96]{0:T(128)}, u32[]{:S(2)}) copy-start(f32[96]{0:T(128)} %param.36) | copy-start | bytes 1156
  7.3 8.6 %copy-start.31 = (f32[96]{0:T(128)S(1)}, f32[96]{0:T(128)}, u32[]{:S(2)}) copy-start(f32[96]{0:T(128)} %param.37) | copy-start | bytes 1156
  7.3 8.6 %copy-start.32 = (f32[96]{0:T(128)S(1)}, f32[96]{0:T(128)}, u32[]{:S(2)}) copy-start(f32[96]{0:T(128)} %param.38) | copy-start | bytes 1156
  7.3 26.4 %copy-start.15 = (s32[2]{0:T(128)S(1)}, s32[2]{0:T(128)}, u32[]{:S(2)}) copy-start(s32[2]{0:T(128)} %len_ref.3) | copy-start | bytes 28
  7.3 47.4 %all-gather.7.cloned.1.call-start = ((), (), s32[]{:S(2)}) async-start(), calls=%async_computation.4 | async-start | bytes 3981312 | tf_op jit(solution)/shard_map/all_gather | solution.py:406
  9.4 86.2 %all-gather.9.cloned.1.call-start = ((), (), s32[]{:S(2)}) async-start(), calls=%async_computation.5 | async-start | bytes 1327104 | tf_op jit(solution)/shard_map/all_gather | solution.py:406
  11.1 120.6 %all-gather.11.cloned.1.call-start = ((), (), s32[]{:S(2)}) async-start(), calls=%async_computation.6 | async-start | bytes 5308416 | tf_op jit(solution)/shard_map/all_gather | solution.py:406
  13.4 170.5 %all-gather.13.cloned.1.call-start = ((), (), s32[]{:S(2)}) async-start(), calls=%async_computation.7 | async-start | bytes 5308416 | tf_op jit(solution)/shard_map/all_gather | solution.py:406
  15.6 419.5 %reduce-scatter.13.cloned.1.call-start = ((), (), s32[]{:S(2)}) async-start(), calls=%async_computation.11 | async-start | bytes 3981312
  33.4 224.2 %copy-start.13 = (f32[768]{0:T(1024)}, f32[768]{0:T(1024)S(1)}, u32[]{:S(2)}) copy-start(f32[768]{0:T(1024)S(1)} %reshape.252) | copy-start | bytes 9220
  33.5 150.4 %copy-start.16 = (f32[768]{0:T(1024)}, f32[768]{0:T(1024)S(1)}, u32[]{:S(2)}) copy-start(f32[768]{0:T(1024)S(1)} %reshape.253) | copy-start | bytes 9220
  54.8 4.4 copy-start.20
  54.8 4.4 copy-start.22
  54.8 4.4 copy-start.33
  95.6 6.5 %copy-start.8 = (bf16[2048,768]{1,0:T(8,128)(2,1)}, bf16[2048,768]{1,0:T(8,128)(2,1)S(1)}, u32[]{:S(2)}) copy-start(bf16[2048,768]{1,0:T(8,128)(2,1)S(1)} %constant_dynamic-update-slice_fusion) | copy-start | bytes 9437188
  102.2 2.6 copy-start
  199.9 1.9 copy-start.6
  201.8 11.9 %slice-start.4 = ((s8[4718592]{0:T(1024)(128)(4,1)}), s8[4194304]{0:T(1024)(128)(4,1)S(1)}, s32[]{:S(2)}) async-start(s8[4718592]{0:T(1024)(128)(4,1)} %bitcast.83), calls=%async_computation.17 | async-start | bytes 8388608
  207.9 5.8 slice-start.5
  207.9 30.1 %slice-start = ((s8[6291456]{0:T(1024)(128)(4,1)}), s8[4194304]{0:T(1024)(128)(4,1)S(1)}, s32[]{:S(2)}) async-start(s8[6291456]{0:T(1024)(128)(4,1)} %bitcast.65), calls=%async_computation.13 | async-start | bytes 8388608
  213.7 24.2 %copy-start.4 = (f32[2048,768]{1,0:T(8,128)}, f32[2048,768]{1,0:T(8,128)S(1)}, u32[]{:S(2)}) copy-start(f32[2048,768]{1,0:T(8,128)S(1)} %get-tuple-element.99) | copy-start | bytes 18874372
  213.7 24.2 %slice-start.1 = ((s8[6291456]{0:T(1024)(128)(4,1)}), s8[2097152]{0:T(1024)(128)(4,1)S(1)}, s32[]{:S(2)}) async-start(s8[6291456]{0:T(1024)(128)(4,1)} %bitcast.65), calls=%async_computation.14 | async-start | bytes 4194304
  257.6 5.3 copy-start.25
  262.8 2.9 copy-start.3
  319.7 3.2 copy-start.2
  319.7 5.5 copy-start.23
  323.1 2.2 copy-start.9
  325.3 4.3 copy-start.7
  325.3 4.3 copy-start.24
  335.4 7.6 %copy-start.14 = (f32[768]{0:T(1024)S(1)}, f32[768]{0:T(1024)}, u32[]{:S(2)}) copy-start(f32[768]{0:T(1024)} %copy-done.13) | copy-start | bytes 9220
  335.4 7.6 %copy-start.17 = (f32[768]{0:T(1024)S(1)}, f32[768]{0:T(1024)}, u32[]{:S(2)}) copy-start(f32[768]{0:T(1024)} %copy-done.16) | copy-start | bytes 9220
  335.4 101.9 %reduce-scatter.7.cloned.1.call-start = ((), (), s32[]{:S(2)}) async-start(), calls=%async_computation.8 | async-start | bytes 1327104 | tf_op jit(solution)/shard_map/reduce_scatter | solution.py:447
  342.9 124.9 %reduce-scatter.9.cloned.1.call-start = ((), (), s32[]{:S(2)}) async-start(), calls=%async_computation.9 | async-start | bytes 5308416 | tf_op jit(solution)/shard_map/reduce_scatter | solution.py:447
  361.2 162.3 %reduce-scatter.11.cloned.1.call-start = ((), (), s32[]{:S(2)}) async-start(), calls=%async_computation.10 | async-start | bytes 5308416 | tf_op jit(solution)/shard_map/reduce_scatter | solution.py:447
  377.7 6.9 %copy-start.10 = (f32[768,32]{1,0:T(8,128)S(1)}, f32[768,32]{1,0:T(8,128)}, u32[]{:S(2)}) copy-start(f32[768,32]{1,0:T(8,128)} %constant.52.clone) | copy-start | bytes 294916
  377.7 55.5 %copy-start.1 = (bf16[2048,768]{1,0:T(8,128)(2,1)S(1)}, bf16[2048,768]{1,0:T(8,128)(2,1)}, u32[]{:S(2)}) copy-start(bf16[2048,768]{1,0:T(8,128)(2,1)} %get-tuple-element.102) | copy-start | bytes 9437188
  377.7 215.2 %all-reduce.4.cloned.1.call-start = ((), (), s32[]{:S(2)}) async-start(), calls=%async_computation.12 | async-start | bytes 3833856 | tf_op jit(solution)/shard_map/psum | solution.py:475
  435.1 95.0 %slice-start.2 = ((s8[6291456]{0:T(1024)(128)(4,1)}), s8[2097152]{0:T(1024)(128)(4,1)S(1)}, s32[]{:S(2)}) async-start(s8[6291456]{0:T(1024)(128)(4,1)} %bitcast.67), calls=%async_computation.15 | async-start | bytes 4194304
  523.5 6.6 %copy-start.21 = (bf16[768,2304]{1,0:T(8,128)(2,1)S(1)}, bf16[768,2304]{1,0:T(8,128)(2,1)}, u32[]{:S(2)}) copy-start(bf16[768,2304]{1,0:T(8,128)(2,1)} %all-gather.7.cloned.1.call-done) | copy-start | bytes 10616836
  524.7 5.4 slice-start.3
  (1 other events, 1.4 us)
Sparse Core Ops, SparseCore 0:
  10.3 44.3 all-gather.6
  57.0 21.6 all-gather.8
  80.9 50.8 all-gather.10
  133.8 49.9 all-gather.12
  335.5 42.4 reduce-scatter.12
  380.7 31.5 reduce-scatter.6
  414.7 53.0 reduce-scatter.8
  470.1 53.3 reduce-scatter.10
  527.5 65.3 all-reduce.3

commit v2 on v1

v2 whole, which is shorter than its diff:
```python
import functools
import math

import jax
import jax.numpy as jnp
import numpy as np
from jax import lax
from jax.experimental import pallas as pl
from jax.experimental.pallas import tpu as pltpu
from jax.sharding import PartitionSpec as P

HEADS = 12
HEAD = 64
BUCKETS = 32
MAX_DIST = 128
LANE = 128
NEAR = 512
ROWS = 16
TABLE_ROW = 12
MASKED = -1e30
LOG2E = 1.4426950408889634
LN2 = 0.6931471805599453
F32 = jnp.float32
BF16 = jnp.bfloat16
MESH = pl.DeviceIdType.MESH
VMEM_BYTES = 60 * 2**20
eps_norm = 1e-05
root_half = 0.7071067811865476
inv_root_tau = 0.3989422804014327


def bucket_of(offset):
    half_count = BUCKETS // 2
    result = (offset < 0).astype(np.int64) * half_count
    distance = np.abs(offset)
    exact_count = half_count // 2
    fraction = np.log(np.maximum(distance, 1) / exact_count) / np.log(MAX_DIST / exact_count)
    beyond = exact_count + (fraction * (half_count - exact_count)).astype(np.int64)
    beyond = np.minimum(beyond, half_count - 1)
    result = result + np.where(distance < exact_count, distance, beyond)
    return result.astype(np.int32)


def nt(a, b):
    return lax.dot_general(a, b, (((1,), (1,)), ((), ())), preferred_element_type=F32)


def nn(a, b):
    return lax.dot_general(a, b, (((1,), (0,)), ((), ())), preferred_element_type=F32)


def signed_places():
    places = np.arange(NEAR)
    return np.where(places < NEAR - LANE, places, places - NEAR)


def near_onehot(sign):
    offset = sign * (signed_places() - LANE)
    return (bucket_of(offset)[None, :] == np.arange(BUCKETS)[:, None]).astype(np.float32)


def skewed(row, width):
    wide = jnp.broadcast_to(row, (LANE, NEAR))
    return pltpu.roll(wide, 0, 1, stride=1, stride_axis=0)[:, :width]


def tile_bias(near, far_pos, far_neg, seq_len, sign):
    blocks = seq_len // LANE
    rows = []
    for rb in range(blocks):
        parts = []
        for cb in range(blocks):
            e = cb - rb
            if abs(e) <= 1:
                parts.append(near[:, (e + 1) * LANE : (e + 2) * LANE])
            else:
                parts.append(jnp.broadcast_to(far_pos if e * sign > 0 else far_neg, (LANE, LANE)))
        rows.append(jnp.concatenate(parts, 1))
    return rows


def head_lanes(shape, t):
    lane = lax.broadcasted_iota(jnp.int32, shape, 1)
    return (lane >= t * HEAD) & (lane < (t + 1) * HEAD)


def flip(v, m):
    a, b = v // 2, v % 2
    if m & 2:
        a = 1 - a
    if m & 1:
        b = 1 - b
    return a * 2 + b


def table_onehot(sign, shards):
    per_shard = BUCKETS // shards
    result = np.zeros((shards * ROWS, NEAR + LANE), np.float32)
    near = near_onehot(sign)
    for bucket in range(BUCKETS):
        row = bucket // per_shard * ROWS + TABLE_ROW + bucket % per_shard
        result[row, :NEAR] = near[bucket]
        result[row, NEAR] = bucket == BUCKETS // 2 - 1
        result[row, NEAR + 1] = bucket == BUCKETS - 1
    return jnp.asarray(result, BF16)


class Links:
    def __init__(self, send, recv):
        self.send, self.recv = send, recv
        self.r = lax.axis_index("rep")
        self.f = lax.axis_index("fsdp")
        self.y, self.x = self.r // 2, self.r % 2
        self.z, self.c = self.f // 2, self.f % 2
        self.xr, self.yr = flip(self.r, 1), flip(self.r, 2)
        self.sib = self.z * 2 + 1 - self.c

    def along(self, s):
        return ((self.z + s) % 4) * 2 + self.c

    def copy(self, at, src, dst, rep, fsdp):
        return pltpu.make_async_remote_copy(
            src_ref=src, dst_ref=dst, send_sem=self.send.at[at], recv_sem=self.recv.at[at],
            device_id={"rep": rep, "fsdp": fsdp}, device_id_type=MESH)

    def barrier(self):
        sem = pltpu.get_barrier_semaphore()
        peers = [(self.r, self.along(s)) for s in (1, 2, 3)]
        peers += [(self.xr, self.f), (self.yr, self.f), (self.r, self.sib)]
        for rep, fsdp in peers:
            pl.semaphore_signal(sem, inc=1, device_id={"rep": rep, "fsdp": fsdp}, device_id_type=MESH)
        pl.semaphore_wait(sem, len(peers))


def quarter_of(ref, rows, cols, owner, q, part=None):
    pr, pc = rows // 2, cols // 2
    r0, c0 = owner * rows + (q // 2) * pr, (q % 2) * pc
    if part is not None:
        if pr % 32 == 0:
            r0, pr = r0 + part * (pr // 2), pr // 2
        else:
            first = (pc // LANE + 1) // 2 * LANE
            c0, pc = (c0, first) if part == 0 else (c0 + first, pc - first)
    return ref.at[pl.ds(pl.multiple_of(r0, 16), pr), pl.ds(pl.multiple_of(c0, LANE), pc)]


class Gather(Links):
    SLOTS = 12

    def __init__(self, shapes, shards, fulls, send, recv):
        super().__init__(send, recv)
        self.shapes, self.shards, self.fulls = shapes, shards, fulls

    def z_send(self, w, s):
        rows, cols = self.shapes[w]
        src = quarter_of(self.shards[w], rows, cols, 0, self.r)
        dst = quarter_of(self.fulls[w], rows, cols, self.f, self.r)
        return self.copy((w, s, 0), src, dst, self.r, self.along(s))

    def hop(self, w, s, slot, q, rep, fsdp, part=None):
        rows, cols = self.shapes[w]
        place = quarter_of(self.fulls[w], rows, cols, self.along(4 - s), q, part)
        return self.copy((w, s, slot), place, place, rep, fsdp)

    def own_place(self, w):
        rows = self.shapes[w][0]
        return self.fulls[w].at[pl.ds(pl.multiple_of(self.f * rows, 16), rows), :]

    def own_sib(self, w):
        return self.copy((w, 0, 0), self.shards[w], self.own_place(w), self.r, self.sib)

    def own_here(self, w):
        return pltpu.make_async_copy(self.shards[w], self.own_place(w), self.send.at[w, 0, 1])

    def h_x(self, w, s):
        return self.hop(w, s, 1, self.r, self.xr, self.f)

    def h_y(self, w, s):
        return self.hop(w, s, 2, self.r, self.yr, self.f)

    def h_dy(self, w, s):
        return self.hop(w, s, 3, self.xr, self.yr, self.f, 0)

    def h_dx(self, w, s):
        return self.hop(w, s, 4, self.yr, self.xr, self.f, 1)

    def h_sib(self, w, s, m):
        return self.hop(w, s, 5 + m, flip(self.r, m), self.r, self.sib)

    def start(self, w):
        for s in (1, 2, 3):
            self.z_send(w, s).start()
        self.own_sib(w).start()
        self.own_here(w).start()

    def relay_z(self, w, s):
        self.z_send(w, s).wait_recv()
        self.h_x(w, s).start()
        self.h_y(w, s).start()
        self.h_sib(w, s, 0).start()

    def relay_xy(self, w, s):
        self.h_x(w, s).wait_recv()
        self.h_dy(w, s).start()
        self.h_sib(w, s, 1).start()
        self.h_y(w, s).wait_recv()
        self.h_dx(w, s).start()
        self.h_sib(w, s, 2).start()

    def relay_diag(self, w, s):
        self.h_dy(w, s).wait_recv()
        self.h_dx(w, s).wait_recv()
        self.h_sib(w, s, 3).start()

    def arrive(self, w):
        for s in (1, 2, 3):
            for m in range(4):
                self.h_sib(w, s, m).wait_recv()
        self.own_sib(w).wait_recv()
        self.own_here(w).wait()

    def drain(self, w):
        for s in (1, 2, 3):
            for d in (self.z_send(w, s), self.h_x(w, s), self.h_y(w, s), self.h_dy(w, s), self.h_dx(w, s)):
                d.wait_send()
            for m in range(4):
                self.h_sib(w, s, m).wait_send()
        self.own_sib(w).wait_send()

    def small_place(self, owner):
        return self.small_full.at[pl.ds(pl.multiple_of(owner * ROWS, ROWS), ROWS), :]

    def small_copies(self):
        w = len(self.shapes)
        far = [self.copy((w, s, 0), self.small_shard, self.small_place(self.f), self.r, self.along(s)) for s in (1, 2, 3)]
        own = self.copy((w, 0, 0), self.small_shard, self.small_place(self.f), self.r, self.sib)
        here = pltpu.make_async_copy(self.small_shard, self.small_place(self.f), self.send.at[w, 0, 1])
        sib = []
        for s in (1, 2, 3):
            place = self.small_place(self.along(4 - s))
            sib.append(self.copy((w, s, 1), place, place, self.r, self.sib))
        return far, own, here, sib


class Reduce(Links):
    SLOTS = 8

    def __init__(self, shapes, grads, outs, bufs, send, recv):
        super().__init__(send, recv)
        self.shapes, self.grads, self.outs, self.bufs = shapes, grads, outs, bufs

    @staticmethod
    def scratch(shapes):
        out = []
        for rows, cols in shapes:
            out += [
                pltpu.VMEM((4, rows, cols), BF16),
                pltpu.VMEM((4, rows, cols), BF16),
                pltpu.VMEM((2, rows, cols // 2), BF16),
                pltpu.VMEM((2, rows // 2, cols), BF16),
                pltpu.VMEM((4, rows // 2, cols // 2), BF16),
                pltpu.VMEM((3, rows // 2, cols // 2), BF16),
                pltpu.VMEM((rows // 2, cols // 2), BF16),
            ]
        return out

    def shard(self, w, s, core):
        rows = self.shapes[w][0]
        at = pl.multiple_of((((self.z + s) % 4) * 2 + core) * rows, 16)
        return self.grads[w].at[pl.ds(at, rows), :]

    def half_rows(self, w, bit):
        h = self.shapes[w][0] // 2
        return pl.ds(pl.multiple_of(bit * h, 16), h)

    def half_cols(self, w, bit):
        h = self.shapes[w][1] // 2
        return pl.ds(pl.multiple_of(bit * h, 128), h)

    def core_copy(self, w, s):
        return self.copy((w, s, 0), self.shard(w, s, 1 - self.c), self.bufs[w][1].at[s], self.r, self.sib)

    def core_load(self, w, s):
        return pltpu.make_async_copy(self.shard(w, s, self.c), self.bufs[w][0].at[s], self.send.at[w, s, 7])

    def start(self, w, s):
        self.core_copy(w, s).start()
        self.core_load(w, s).start()

    def x_first(self, s):
        return s % 2 == 1

    def first_copy(self, w, s):
        own, hx, hy = self.bufs[w][0], self.bufs[w][2], self.bufs[w][3]
        if self.x_first(s):
            return self.copy((w, s, 1), own.at[s, :, self.half_cols(w, 1 - self.x)], hx.at[s // 2], self.xr, self.f)
        return self.copy((w, s, 1), own.at[s, self.half_rows(w, 1 - self.y), :], hy.at[s // 2], self.yr, self.f)

    def add_core(self, w, s):
        self.core_copy(w, s).wait_recv()
        self.core_load(w, s).wait()
        own, got = self.bufs[w][0], self.bufs[w][1]
        own[s] = own[s] + got[s]
        self.first_copy(w, s).start()

    def second_copy(self, w, s):
        own, quarter = self.bufs[w][0], self.bufs[w][4]
        if self.x_first(s):
            src = own.at[s, self.half_rows(w, 1 - self.y), self.half_cols(w, self.x)]
            return self.copy((w, s, 2), src, quarter.at[s], self.yr, self.f)
        src = own.at[s, self.half_rows(w, self.y), self.half_cols(w, 1 - self.x)]
        return self.copy((w, s, 2), src, quarter.at[s], self.xr, self.f)

    def add_first(self, w, s):
        self.first_copy(w, s).wait_recv()
        own, hx, hy = self.bufs[w][0], self.bufs[w][2], self.bufs[w][3]
        if self.x_first(s):
            at = (s, slice(None), self.half_cols(w, self.x))
            own[at] = own[at] + hx[s // 2]
        else:
            at = (s, self.half_rows(w, self.y), slice(None))
            own[at] = own[at] + hy[s // 2]
        self.second_copy(w, s).start()

    def far_copy(self, w, s):
        own, far = self.bufs[w][0], self.bufs[w][5]
        src = own.at[s, self.half_rows(w, self.y), self.half_cols(w, self.x)]
        return self.copy((w, s, 3), src, far.at[s - 1], self.r, self.along(s))

    def add_second(self, w, s):
        self.second_copy(w, s).wait_recv()
        own, quarter = self.bufs[w][0], self.bufs[w][4]
        at = (s, self.half_rows(w, self.y), self.half_cols(w, self.x))
        own[at] = own[at] + quarter[s]
        if s > 0:
            self.far_copy(w, s).start()

    def place(self, w, q, part=None):
        rows, cols = self.shapes[w]
        h = rows // 2
        r0, n = (q // 2) * h, h
        if part is not None:
            n = h // 32 * 16 if part == 0 else h - h // 32 * 16
            r0 = r0 if part == 0 else r0 + h // 32 * 16
        return self.outs[w].at[pl.ds(pl.multiple_of(r0, 16), n), self.half_cols(w, q % 2)]

    def out_local(self, w):
        return pltpu.make_async_copy(self.bufs[w][6], self.place(w, self.r), self.send.at[w, 0, 3])

    def out_x(self, w):
        return self.copy((w, 0, 4), self.bufs[w][6], self.place(w, self.r), self.xr, self.f)

    def out_y(self, w):
        return self.copy((w, 0, 5), self.bufs[w][6], self.place(w, self.r), self.yr, self.f)

    def out_dy(self, w):
        p = self.place(w, flip(self.r, 1), 0)
        return self.copy((w, 1, 4), p, p, self.yr, self.f)

    def out_dx(self, w):
        p = self.place(w, flip(self.r, 2), 1)
        return self.copy((w, 1, 5), p, p, self.xr, self.f)

    def total(self, w):
        own, far, done = self.bufs[w][0], self.bufs[w][5], self.bufs[w][6]
        for s in (1, 2, 3):
            self.far_copy(w, s).wait_recv()
        at = (0, self.half_rows(w, self.y), self.half_cols(w, self.x))
        done[...] = (own[at].astype(F32) + far[0].astype(F32) + far[1].astype(F32) + far[2].astype(F32)).astype(BF16)
        self.out_x(w).start()
        self.out_y(w).start()
        self.out_local(w).start()

    def relay(self, w):
        self.out_x(w).wait_recv()
        self.out_dy(w).start()
        self.out_y(w).wait_recv()
        self.out_dx(w).start()

    def finish(self, w):
        for s in range(4):
            self.core_copy(w, s).wait_send()
            self.first_copy(w, s).wait_send()
            self.second_copy(w, s).wait_send()
            if s:
                self.far_copy(w, s).wait_send()
        self.out_local(w).wait()
        self.out_x(w).wait_send()
        self.out_y(w).wait_send()
        for d in (self.out_dy(w), self.out_dx(w)):
            d.wait_send()
            d.wait_recv()


def plan(red, n, order):
    items = [(w, s) for w in order for s in (1, 2, 3, 0)]
    ticks = []
    m = len(items)
    for k in range(m + 4):
        acts = []
        if k < m:
            acts.append(functools.partial(red.add_core, *items[k]))
        if 0 <= k - 2 < m:
            acts.append(functools.partial(red.add_first, *items[k - 2]))
        if 0 <= k - 4 < m:
            w, s = items[k - 4]
            acts.append(functools.partial(red.add_second, w, s))
            if s == 0:
                j = order.index(w)
                if j > 0:
                    acts.append(functools.partial(red.total, order[j - 1]))
                if j > 1:
                    acts.append(functools.partial(red.relay, order[j - 2]))
        ticks.append(acts)
    tail = [functools.partial(red.total, order[-1])]
    if n > 1:
        tail.append(functools.partial(red.relay, order[-2]))
    tail.append(functools.partial(red.relay, order[-1]))
    ticks.append(tail)
    ticks.append([functools.partial(red.finish, w) for w in order])
    return items, ticks


def spread_rows(small, row, step, count, unit):
    width = count * unit
    lane = lax.broadcasted_iota(jnp.int32, (8, width), 1)
    total = jnp.zeros((8, width), F32)
    for k in range(count):
        one = jnp.broadcast_to(small[row[k] : row[k] + 1, :], (8, LANE))
        wide = jnp.concatenate([one, jnp.zeros((8, width - LANE), F32)], 1)
        wide = jnp.where(lane < unit, wide, 0.0)
        total = total + (pltpu.roll(wide, k * unit, 1) if k else wide)
    return total[0:1]


def fill_mask(mask_ref, ord_ref, limit, s, seq_len, turned):
    blocks = seq_len // LANE
    own = ord_ref[pl.ds(s, 1), :].astype(F32)
    cols = jnp.broadcast_to(own, (LANE, seq_len)).T
    for rb in range(blocks):
        col = cols[rb * LANE : (rb + 1) * LANE, :]
        rank = jnp.concatenate([col] * blocks, 1)
        place = lax.broadcasted_iota(jnp.int32, (LANE, seq_len), 0 if turned else 1)
        if turned:
            place = place + rb * LANE
        order = (rank <= own) if turned else (own <= rank)
        ok = (place < limit) & ((place == 0) | order)
        mask_ref[s, rb * LANE : (rb + 1) * LANE, :] = jnp.where(ok, 0.0, MASKED)


def fill_near(near_ref, small, onehot_ref):
    near_ref[...] = lax.dot_general(small, onehot_ref[...], (((0,), (0,)), ((), ())), preferred_element_type=F32) * LOG2E


def attention_step(hp, s, proj, mask_ref, near_ref, put_out, put_total):
    query_c, keys, value, query_g = proj
    seq_len = keys.shape[0]
    blocks = seq_len // LANE
    values = jnp.concatenate([value, jnp.ones((seq_len, LANE), BF16)], 1)
    lane = lax.broadcasted_iota(jnp.int32, (seq_len, LANE), 1)
    diag_r = lax.broadcasted_iota(jnp.int32, (LANE, LANE), 0)
    diag_c = lax.broadcasted_iota(jnp.int32, (LANE, LANE), 1)
    outs = [[], []]
    totals = [jnp.zeros((seq_len, LANE), F32), jnp.zeros((seq_len, LANE), F32)]
    for t in range(2):
        head = hp * 2 + t
        sel = head_lanes((seq_len, LANE), t)
        head_row = near_ref[pl.ds(head, 1), :]
        near = skewed(head_row[:, :NEAR], 3 * LANE)
        bias = tile_bias(near, head_row[:, NEAR : NEAR + 1], head_row[:, NEAR + 1 : NEAR + 2], seq_len, -1)
        for stream in range(2):
            query = jnp.where(sel, query_g if stream else query_c, jnp.zeros((), BF16))
            raw = nt(query, keys)
            probs = []
            maxes = []
            for rb in range(blocks):
                part = raw[rb * LANE : (rb + 1) * LANE, :] + (bias[rb] + mask_ref[s, rb * LANE : (rb + 1) * LANE, :])
                if stream == 1:
                    hit = diag_r == diag_c
                    if rb == 0:
                        hit = hit & (diag_c != 0)
                    pieces = []
                    if rb > 0:
                        pieces.append(part[:, : rb * LANE])
                    pieces.append(jnp.where(hit, MASKED, part[:, rb * LANE : (rb + 1) * LANE]))
                    if rb < blocks - 1:
                        pieces.append(part[:, (rb + 1) * LANE :])
                    part = jnp.concatenate(pieces, 1)
                top = jnp.max(part, 1, keepdims=True)
                probs.append(jnp.exp2(part - top).astype(BF16))
                maxes.append(jnp.broadcast_to(top, (LANE, LANE)))
            mixed = nn(jnp.concatenate(probs, 0), values)
            total = mixed[:, LANE:]
            outs[stream].append(mixed[:, :LANE] / total)
            log_total = jnp.concatenate(maxes, 0) + jnp.log2(total)
            hi = log_total.astype(BF16).astype(F32)
            totals[stream] = jnp.where(lane == head, -hi, jnp.where(lane == head + HEAD, hi - log_total, totals[stream]))
    first = head_lanes((seq_len, LANE), 0)
    mine = (lane == hp * 2) | (lane == hp * 2 + 1) | (lane == hp * 2 + HEAD) | (lane == hp * 2 + 1 + HEAD)
    for stream in range(2):
        put_out(stream, jnp.where(first, outs[stream][0], outs[stream][1]).astype(BF16))
        put_total(stream, totals[stream].astype(BF16), mine)


def forward_kernel(shapes, linked, len_ref, content_ref, query_ref, ord_ref, onehot_ref, *refs):
    n = len(shapes)
    if linked:
        shards, small_shard, refs = refs[:n], refs[n], refs[n + 1 :]
        full_refs, refs = refs[: n - 1], refs[n - 1 :]
        joined_out, small_out, refs = refs[0], refs[1], refs[2:]
    else:
        joined_in, small_in, refs = refs[0], refs[1], refs[2:]
    mixed_ref, total_ref, proj_out, joined_ref, small_ref, proj_ref, mask_ref, near_ref, own_sem = refs[:9]
    hp = pl.program_id(0)
    s = pl.program_id(1)
    step = hp * pl.num_programs(1) + s
    steps = (HEADS // 2) * total_ref.shape[1]
    seqs = total_ref.shape[1]
    seq_len = total_ref.shape[2]
    row_count, width = content_ref.shape
    if linked:
        send, recv = refs[9:]
        net = Gather(shapes, shards, (joined_ref,) + tuple(full_refs), send, recv)
        net.small_shard, net.small_full = small_shard, small_ref
    proj_copy = pltpu.make_async_copy(proj_ref, proj_out, own_sem.at[0])

    @pl.when(step == 0)
    def _():
        if linked:
            net.barrier()
            far, own, here, sib = net.small_copies()
            for d in far + [own, here]:
                d.start()
            for w in range(n):
                net.start(w)
            for s0 in range(seqs):
                fill_mask(mask_ref, ord_ref, len_ref[s0], s0, seq_len, False)
            for d, e in zip(far, sib):
                d.wait_recv()
                e.start()
            for k in (1, 2, 3):
                net.relay_z(0, k)
            for k in (1, 2, 3):
                net.relay_xy(0, k)
            for k in (1, 2, 3):
                net.relay_z(1, k)
            for k in (1, 2, 3):
                net.relay_diag(0, k)
            for k in (1, 2, 3):
                net.relay_z(2, k)
            for d in far:
                d.wait_send()
            for d in [own] + sib:
                d.wait_send()
                d.wait_recv()
            here.wait()
            net.arrive(0)
            pltpu.make_async_copy(joined_ref, joined_out, own_sem.at[1]).start()
            pltpu.make_async_copy(small_ref, small_out, own_sem.at[2]).start()
        else:
            fetch = (pltpu.make_async_copy(joined_in, joined_ref, own_sem.at[1]), pltpu.make_async_copy(small_in, small_ref, own_sem.at[2]))
            for d in fetch:
                d.start()
            for s0 in range(seqs):
                fill_mask(mask_ref, ord_ref, len_ref[s0], s0, seq_len, False)
            for d in fetch:
                d.wait()
        fill_near(near_ref, small_ref[...], onehot_ref)
        small = small_ref[...].astype(F32)
        shards_all = small.shape[0] // ROWS
        unit = width // shards_all
        half = shards_all // 2
        shift_q = spread_rows(small, [k // 2 * ROWS + k % 2 for k in range(2 * half)], 0, 2 * half, unit)
        shift_v = spread_rows(small, [(half + k // 2) * ROWS + k % 2 for k in range(2 * half)], 0, 2 * half, unit)
        scale = LOG2E / math.sqrt(HEAD)
        chunk = 256

        @pl.loop(0, row_count // chunk)
        def _(i):
            rows = pl.ds(pl.multiple_of(i * chunk, chunk), chunk)
            rows_c = content_ref[rows, :]
            proj_ref[rows, 0:width] = ((nn(rows_c, joined_ref[:, 0:width]) + shift_q) * scale).astype(BF16)
            proj_ref[rows, width : 2 * width] = nn(rows_c, joined_ref[:, width : 2 * width]).astype(BF16)
            proj_ref[rows, 2 * width : 3 * width] = (nn(rows_c, joined_ref[:, 2 * width : 3 * width]) + shift_v).astype(BF16)
            proj_ref[rows, 3 * width : 4 * width] = ((nn(query_ref[rows, :], joined_ref[:, 0:width]) + shift_q) * scale).astype(BF16)

        proj_copy.start()

    if linked:
        agenda = {
            1: [(net.relay_xy, 1, (1, 2, 3))],
            3: [(net.relay_z, 3, (1, 2, 3))],
            4: [(net.relay_xy, 2, (1,))],
            5: [(net.relay_xy, 2, (2,)), (net.relay_diag, 1, (1, 2, 3))],
            6: [(net.relay_xy, 2, (3,))],
            8: [(net.relay_diag, 2, (1, 2)), (net.relay_xy, 3, (1,))],
            9: [(net.relay_diag, 2, (3,)), (net.relay_xy, 3, (2,))],
            10: [(net.relay_xy, 3, (3,))],
        }
        for at, acts in agenda.items():

            @pl.when(step == min(at, steps - 1))
            def _():
                for act, w, ks in acts:
                    for k in ks:
                        act(w, k)

    here_rows = pl.ds(pl.multiple_of(s * seq_len, seq_len), seq_len)
    column = lambda k: pl.ds(pl.multiple_of(k * width + hp * LANE, LANE), LANE)
    proj = [proj_ref[here_rows, column(k)] for k in range(4)]

    def put_out(stream, value):
        mixed_ref[stream] = value

    def put_total(stream, value, mine):
        @pl.when(hp == 0)
        def _():
            total_ref[stream, s] = value

        @pl.when(hp > 0)
        def _():
            total_ref[stream, s] = jnp.where(mine, value, total_ref[stream, s])

    attention_step(hp, s, proj, mask_ref, near_ref, put_out, put_total)

    @pl.when(step == steps - 1)
    def _():
        proj_copy.wait()
        if linked:
            pltpu.make_async_copy(joined_ref, joined_out, own_sem.at[1]).wait()
            pltpu.make_async_copy(small_ref, small_out, own_sem.at[2]).wait()
            for k in (1, 2, 3):
                net.relay_diag(3, k)
            for w in range(n):
                if w:
                    net.arrive(w)
                net.drain(w)


def forward_attention(linked, content_rows, query_rows, lengths, order, weights, small):
    row_count, width = content_rows.shape
    seqs, seq_len = order.shape
    pairs = width // LANE
    shards = 8 if linked else small.shape[0] // ROWS
    onehot = table_onehot(-1, shards)
    shapes = [w.shape for w in weights] if linked else []
    n = len(shapes)
    anywhere = pl.BlockSpec(memory_space=pl.ANY)
    inside = pl.BlockSpec(memory_space=pltpu.VMEM)
    block3 = pl.BlockSpec((2, seq_len, LANE), lambda h, s: (0, s, h))
    joined_shape = (width, 3 * width)
    small_shape = (shards * ROWS, LANE)
    out_specs, out_shape = [], []
    if linked:
        out_specs += [anywhere] * (n + 1)
        out_shape += [jax.ShapeDtypeStruct((8 * a, b), BF16) for a, b in shapes[1:]]
        out_shape += [jax.ShapeDtypeStruct(joined_shape, BF16), jax.ShapeDtypeStruct(small_shape, BF16)]
    out_specs += [block3, pl.BlockSpec((2, seqs, seq_len, LANE), lambda h, s: (0, 0, 0, 0)), anywhere]
    out_shape += [
        jax.ShapeDtypeStruct((2, row_count, width), BF16),
        jax.ShapeDtypeStruct((2, seqs, seq_len, LANE), BF16),
        jax.ShapeDtypeStruct((row_count, 4 * width), BF16),
    ]
    scratch = [
        pltpu.VMEM(joined_shape, BF16),
        pltpu.VMEM(small_shape, BF16),
        pltpu.VMEM((row_count, 4 * width), BF16),
        pltpu.VMEM((seqs, seq_len, seq_len), F32),
        pltpu.VMEM((LANE, NEAR + LANE), F32),
        pltpu.SemaphoreType.DMA((3,)),
    ]
    if linked:
        scratch += [pltpu.SemaphoreType.DMA((n + 1, 4, Gather.SLOTS)), pltpu.SemaphoreType.DMA((n + 1, 4, Gather.SLOTS))]
    flops = 2 * row_count * width * 4 * width + 8 * row_count * seq_len * width
    return pl.pallas_call(
        functools.partial(forward_kernel, shapes, linked),
        grid=(pairs, seqs),
        in_specs=[pl.BlockSpec(memory_space=pltpu.SMEM), inside, inside, inside, inside] + [anywhere] * (n + 1 if linked else 2),
        out_specs=out_specs,
        out_shape=out_shape,
        scratch_shapes=scratch,
        cost_estimate=pl.CostEstimate(flops=flops, bytes_accessed=30 * 2**20, transcendentals=4 * row_count * seq_len * HEADS),
        compiler_params=pltpu.CompilerParams(
            dimension_semantics=("arbitrary", "arbitrary"), vmem_limit_bytes=VMEM_BYTES,
            **(dict(collective_id=0, has_side_effects=True) if linked else {})),
        name="attention_forward",
    )(lengths, content_rows, query_rows, order, onehot, *(list(weights) + [small]))


def backward_kernel(shapes, linked, len_ref, q_ref, k_ref, v_ref, g_ref, dc_ref, dg_ref, oc_ref, og_ref, tot_ref, ord_ref, small_ref, onehot_ref, *refs):
    n = len(shapes)
    grads, refs = refs[:n], refs[n:]
    outs, refs = refs[:n], refs[n:]
    grad_ref, sums_ref, mask_ref, acc_ref, near_ref = refs[:5]
    refs = refs[5:]
    hp = pl.program_id(0)
    s = pl.program_id(1)
    last = pl.num_programs(1) - 1
    step = hp * pl.num_programs(1) + s
    seq_len = q_ref.shape[0]
    blocks = seq_len // LANE
    half = seq_len // 2
    steps = (HEADS // 2) * ord_ref.shape[0]
    if linked:
        bufs = [refs[7 * w : 7 * w + 7] for w in range(n)]
        send, recv = refs[7 * n :]
        net = Reduce(shapes, grads, outs, bufs, send, recv)
        items, ticks = plan(net, n, list(range(n)))

        @pl.when(step == 0)
        def _():
            net.barrier()
            for w, k in items:
                net.start(w, k)

        tail = ticks[-2:]
        ticks = ticks[:-2]
        for at in range(1, steps):
            acts = [a for i, t in enumerate(ticks) if 1 + i * (steps - 1) // len(ticks) == at for a in t]

            @pl.when(step == at)
            def _():
                for act in acts:
                    act()

    @pl.when(hp == 0)
    def _():
        fill_mask(mask_ref, ord_ref, len_ref[s], s, seq_len, True)

    @pl.when(step == 0)
    def _():
        fill_near(near_ref, small_ref[...], onehot_ref)

    lane = lax.broadcasted_iota(jnp.int32, (seq_len, LANE), 1)
    ones = jnp.ones((seq_len, LANE), BF16)
    zero = jnp.zeros((), BF16)
    keys = k_ref[...]
    keys_wide = jnp.concatenate([keys, ones], 1)
    values_wide = jnp.concatenate([v_ref[...], ones], 1)
    keys_turned = keys.astype(F32).T.astype(BF16)
    lane_r = lax.broadcasted_iota(jnp.int32, (LANE, LANE), 0)
    lane_c = lax.broadcasted_iota(jnp.int32, (LANE, LANE), 1)
    pick = (lane_r // HEAD == lane_c).astype(BF16)
    grad_keys = None
    grad_values = None
    grad_query = [[], []]
    streams = []
    for src, grad, out, tot in ((q_ref, dc_ref, oc_ref, tot_ref[0, 0]), (g_ref, dg_ref, og_ref, tot_ref[1, 0])):
        g = grad[...]
        delta = nn((g.astype(F32) * out[...].astype(F32)).astype(BF16), pick)
        streams.append((src[...], g, -delta, tot))
    for t in range(2):
        head = hp * 2 + t
        sel = head_lanes((seq_len, LANE), t)
        head_row = near_ref[pl.ds(head, 1), :]
        near = skewed(head_row[:, :NEAR], 3 * LANE)
        bias = tile_bias(near, head_row[:, NEAR : NEAR + 1], head_row[:, NEAR + 1 : NEAR + 2], seq_len, 1)
        for c0 in range(0, seq_len, half):
            both = None
            for stream in range(2):
                q, g, delta, tot = streams[stream]
                q = jnp.where(sel, q, zero)[c0 : c0 + half]
                g = jnp.where(sel, g, zero)[c0 : c0 + half]
                d = delta[c0 : c0 + half]
                ln = lane[c0 : c0 + half]
                tt = jnp.where((ln == head) | (ln == head + HEAD), tot[c0 : c0 + half], zero)
                dd = jnp.where(ln == t, d, 0.0)
                dhi = dd.astype(BF16)
                dlo = pltpu.roll(dd - dhi.astype(F32), HEAD, 1).astype(BF16)
                raw = nt(keys_wide, jnp.concatenate([q, tt], 1))
                dpr = nt(values_wide, jnp.concatenate([g, dhi + dlo], 1))
                probs, grads = [], []
                for rb in range(blocks):
                    sl = slice(rb * LANE, (rb + 1) * LANE)
                    part = raw[sl] + (bias[rb][:, c0 : c0 + half] + mask_ref[s, sl, c0 : c0 + half])
                    r0 = rb * LANE
                    if stream == 1 and c0 <= r0 < c0 + half:
                        hit = lane_r == lane_c
                        if rb == 0:
                            hit = hit & (lane_r != 0)
                        x0 = r0 - c0
                        diag = jnp.where(hit, MASKED, part[:, x0 : x0 + LANE])
                        pieces = []
                        if x0 > 0:
                            pieces.append(part[:, :x0])
                        pieces.append(diag)
                        if x0 + LANE < half:
                            pieces.append(part[:, x0 + LANE :])
                        part = jnp.concatenate(pieces, 1)
                    p = jnp.exp2(part)
                    probs.append(p.astype(BF16))
                    grads.append(p * dpr[sl])
                low = [x.astype(BF16) for x in grads]
                prob = jnp.concatenate(probs, 0)
                gl = jnp.concatenate(low, 0)
                gv = nn(prob, g)
                gk = nn(gl, q)
                grad_values = gv if grad_values is None else grad_values + gv
                grad_keys = gk if grad_keys is None else grad_keys + gk
                grad_query[stream].append(nn(keys_turned[t * HEAD : (t + 1) * HEAD], gl))
                both = grads if both is None else [a + b for a, b in zip(both, grads)]
            sums = {}
            for rb in range(blocks):
                for cb in range(half // LANE):
                    e = cb + c0 // LANE - rb
                    e = max(-2, min(2, e))
                    x = both[rb][:, cb * LANE : (cb + 1) * LANE]
                    sums[e] = x if e not in sums else sums[e] + x
            for e, x in sums.items():
                lanes = slice((e + 2) * LANE, (e + 3) * LANE)
                fresh = c0 == 0
                if fresh:
                    @pl.when(s == 0)
                    def _():
                        acc_ref[t, :, lanes] = x

                    @pl.when(s > 0)
                    def _():
                        acc_ref[t, :, lanes] = acc_ref[t, :, lanes] + x
                else:
                    acc_ref[t, :, lanes] = acc_ref[t, :, lanes] + x
            if c0 == 0:
                for e in range(-2, 3):
                    if e not in sums:
                        @pl.when(s == 0)
                        def _():
                            acc_ref[t, :, (e + 2) * LANE : (e + 3) * LANE] = jnp.zeros((LANE, LANE), F32)
    count = seq_len // half
    scale = 1.0 / math.sqrt(HEAD)
    for stream, ref in ((0, 0), (1, 3)):
        pieces = grad_query[stream]
        top = jnp.concatenate(pieces[:count], 1)
        bot = jnp.concatenate(pieces[count:], 1)
        grad_ref[ref] = (jnp.concatenate([top, bot], 0) * scale).T.astype(BF16)
    grad_ref[1] = (grad_keys * LN2).astype(BF16)
    grad_ref[2] = grad_values.astype(BF16)

    @pl.when(s == last)
    def _():
        for t in range(2):
            near = jnp.concatenate([acc_ref[t, :, LANE : 4 * LANE], jnp.zeros((LANE, LANE), F32)], 1)
            mirror = (lane_r + lane_c == LANE - 1).astype(F32)
            flipped = lax.dot_general(mirror, near, (((1,), (0,)), ((), ())), precision=lax.Precision.HIGHEST, preferred_element_type=F32)
            turned = pltpu.roll(flipped, 0, 1, stride=1, stride_axis=0)
            row = jnp.sum(turned, 0, keepdims=True)
            below = jnp.sum(acc_ref[t, :, :LANE], 0, keepdims=True)
            above = jnp.sum(acc_ref[t, :, 4 * LANE :], 0, keepdims=True)
            sums_ref[pl.ds(hp * 2 + t, 1), :] = jnp.concatenate([row, below, above], 1)

    if linked:

        @pl.when(step == steps - 1)
        def _():
            for acts in tail:
                for act in acts:
                    act()


def backward_attention(linked, proj, grad_mixed, mixed, totals, lengths, order, small, weight_grads):
    rows, width = grad_mixed.shape
    seqs, seq_len = order.shape
    pairs = width // LANE
    onehot = table_onehot(1, small.shape[0] // ROWS)
    shapes = [(g.shape[0] // 8, g.shape[1]) for g in weight_grads]
    n = len(shapes)
    block = lambda off: pl.BlockSpec((seq_len, LANE), lambda h, s, off=off: (s, off + h))
    low = pl.BlockSpec((seq_len, LANE), lambda h, s: (seqs + s, h))
    anywhere = pl.BlockSpec(memory_space=pl.ANY)
    inside = pl.BlockSpec(memory_space=pltpu.VMEM)
    sums_shape = (2 * pairs, NEAR + 2 * LANE)
    scratch = [
        pltpu.VMEM((seqs, seq_len, seq_len), F32),
        pltpu.VMEM((2, LANE, 5 * LANE), F32),
        pltpu.VMEM((LANE, NEAR + LANE), F32),
    ]
    if linked:
        scratch += Reduce.scratch(shapes)
        scratch += [pltpu.SemaphoreType.DMA((n, 4, Reduce.SLOTS)), pltpu.SemaphoreType.DMA((n, 4, Reduce.SLOTS))]
    outs = pl.pallas_call(
        functools.partial(backward_kernel, shapes, linked),
        grid=(pairs, seqs),
        in_specs=[
            pl.BlockSpec(memory_space=pltpu.SMEM),
            block(0), block(pairs), block(2 * pairs), block(3 * pairs),
            block(0), low, block(0), low,
            pl.BlockSpec((2, 1, seq_len, LANE), lambda h, s: (0, s, 0, 0)),
            inside, inside, inside,
        ] + [anywhere] * n,
        out_specs=[anywhere] * n + [pl.BlockSpec((4, seq_len, LANE), lambda h, s: (0, s, h)), pl.BlockSpec(sums_shape, lambda h, s: (0, 0))],
        out_shape=[jax.ShapeDtypeStruct(a, BF16) for a in shapes] + [jax.ShapeDtypeStruct((4, rows // 2, width), BF16), jax.ShapeDtypeStruct(sums_shape, F32)],
        scratch_shapes=scratch,
        cost_estimate=pl.CostEstimate(flops=20 * rows * seq_len * width, bytes_accessed=30 * 2**20, transcendentals=2 * rows * seq_len * HEADS),
        compiler_params=pltpu.CompilerParams(
            dimension_semantics=("arbitrary", "arbitrary"), vmem_limit_bytes=VMEM_BYTES,
            **(dict(collective_id=1, has_side_effects=True) if linked else {})),
        name="attention_backward",
    )(lengths, proj, proj, proj, proj, grad_mixed, grad_mixed, mixed, mixed, totals, order, small, onehot, *weight_grads)
    sums = outs[n + 1]
    fold = np.zeros((sums_shape[1], BUCKETS), np.float32)
    fold[:NEAR] = np.roll(near_onehot(1).T, LANE - 1, 0)
    fold[NEAR : NEAR + LANE, BUCKETS - 1] = 1
    fold[NEAR + LANE :, BUCKETS // 2 - 1] = 1
    grad_table = jnp.dot(sums, jnp.asarray(fold), precision=lax.Precision.HIGHEST).T
    return outs[:n], outs[n], grad_table


def small_reduce(net, w, part, out, bufs):
    own, core, across_x, across_y, far = bufs
    rows = 4 * ROWS
    mine = part.at[pl.ds(pl.multiple_of(net.c * rows, rows), rows), :]
    other = part.at[pl.ds(pl.multiple_of((1 - net.c) * rows, rows), rows), :]
    load = pltpu.make_async_copy(mine, own.at[0], net.send.at[w, 0, 7])
    to_core = net.copy((w, 0, 0), other, core, net.r, net.sib)
    to_x = net.copy((w, 0, 1), own.at[1], across_x, net.xr, net.f)
    to_y = net.copy((w, 0, 2), own.at[2], across_y, net.yr, net.f)
    z_rows = lambda s: pl.ds(pl.multiple_of((net.z + s) % 4 * ROWS, ROWS), ROWS)
    to_far = [net.copy((w, s, 3), own.at[3, z_rows(s), :], far.at[s - 1], net.r, net.along(s)) for s in (1, 2, 3)]

    def first():
        load.start()
        to_core.start()

    def second():
        load.wait()
        to_core.wait_recv()
        own[1] = own[0] + core[...]
        to_x.start()

    def third():
        to_x.wait_recv()
        own[2] = own[1] + across_x[...]
        to_y.start()

    def fourth():
        to_y.wait_recv()
        own[3] = own[2] + across_y[...]
        for d in to_far:
            d.start()

    def fifth():
        for d in to_far:
            d.wait_recv()
        out[...] = own[3, z_rows(0), :] + far[0] + far[1] + far[2]
        for d in [to_core, to_x, to_y] + to_far:
            d.wait_send()

    return first, second, third, fourth, fifth


def reduce_kernel(shapes, n, *refs):
    grads, small_part, refs = refs[:n], refs[n], refs[n + 1 :]
    outs, small_out, refs = refs[:n], refs[n], refs[n + 1 :]
    bufs = [refs[7 * w : 7 * w + 7] for w in range(n)]
    small_bufs, (send, recv) = refs[7 * n : 7 * n + 5], refs[7 * n + 5 :]
    net = Reduce(shapes, grads, outs, bufs, send, recv)
    first, second, third, fourth, fifth = small_reduce(net, n, small_part, small_out, small_bufs)
    net.barrier()
    items, ticks = plan(net, n, list(range(n)))
    first()
    for w, k in items:
        net.start(w, k)
    extra = {1: second, 4: third, 6: fourth}
    for i, acts in enumerate(ticks):
        for act in acts:
            act()
        if i in extra:
            extra[i]()
    fifth()


def reduce_rest(weight_grads, small_grads):
    n = len(weight_grads)
    shapes = [(g.shape[0] // 8, g.shape[1]) for g in weight_grads]
    anywhere = pl.BlockSpec(memory_space=pl.ANY)
    inside = pl.BlockSpec(memory_space=pltpu.VMEM)
    rows = 4 * ROWS
    scratch = Reduce.scratch(shapes)
    scratch += [pltpu.VMEM((4, rows, LANE), F32)] + [pltpu.VMEM((rows, LANE), F32)] * 3 + [pltpu.VMEM((3, ROWS, LANE), F32)]
    scratch += [pltpu.SemaphoreType.DMA((n + 1, 4, Reduce.SLOTS)), pltpu.SemaphoreType.DMA((n + 1, 4, Reduce.SLOTS))]
    return pl.pallas_call(
        functools.partial(reduce_kernel, shapes, n),
        out_shape=[jax.ShapeDtypeStruct(a, BF16) for a in shapes] + [jax.ShapeDtypeStruct((ROWS, LANE), F32)],
        in_specs=[anywhere] * (n + 1),
        out_specs=[anywhere] * n + [inside],
        scratch_shapes=scratch,
        compiler_params=pltpu.CompilerParams(collective_id=2, has_side_effects=True, vmem_limit_bytes=VMEM_BYTES),
        name="reduce_rest",
    )(*weight_grads, small_grads)


def norm_forward(summed, gain_vec, shift_vec):
    row_mean = jnp.mean(summed, -1, keepdims=True)
    centered = summed - row_mean
    inverse = lax.rsqrt(jnp.mean(centered * centered, -1, keepdims=True) + eps_norm)
    normed = centered * inverse
    return (normed * gain_vec + shift_vec, normed, inverse)


def norm_backward(upstream, normed, inverse, gain_vec):
    scaled = upstream * gain_vec
    centered = (
        scaled
        - jnp.mean(scaled, -1, keepdims=True)
        - normed * jnp.mean(scaled * normed, -1, keepdims=True)
    )
    return (inverse * centered, jnp.sum(upstream * normed, 0), jnp.sum(upstream, 0))


def gelu_value(hidden_in):
    return 0.5 * hidden_in * (1.0 + lax.erf(hidden_in * root_half))


def gelu_slope(hidden_in):
    return (
        0.5 * (1.0 + lax.erf(hidden_in * root_half))
        + hidden_in * jnp.exp(-0.5 * hidden_in * hidden_in) * inv_root_tau
    )


def rows_inner(left_op, right_op):
    return lax.dot_general(
        left_op, right_op, (((0,), (0,)), ((), ())), preferred_element_type=jnp.float32
    )


def times_transpose(left_op, right_op):
    return lax.dot_general(
        left_op, right_op, (((1,), (1,)), ((), ())), preferred_element_type=jnp.float32
    )


def pack_small(groups, shards):
    rows = []
    for g in groups:
        g = g.reshape(shards, -1, g.shape[-1]) if g.ndim > 1 else g
        rows.append(g)
    wide = [jnp.pad(g, ((0, 0), (0, 0), (0, LANE - g.shape[2]))) for g in rows]
    joined = jnp.concatenate(wide, 1)
    joined = jnp.pad(joined, ((0, 0), (0, ROWS - joined.shape[1]), (0, 0)))
    return joined.reshape(shards * ROWS, LANE)


def on_device(axes, content_stream, query_stream, lengths, factor_order, qkv_weight, qv_bias, out_weight, out_bias, norm1_gain, norm1_bias, rel_table, ffn_in_weight, ffn_in_bias, ffn_out_weight, ffn_out_bias, norm2_gain, norm2_bias, content_cot, query_cot):
    linked = axes == (4, 8)
    shards = axes[1]
    seq_count, seq_len, width = content_stream.shape
    row_count = seq_count * seq_len
    unit = width // shards
    small_args = (qv_bias, out_bias, norm1_gain, norm1_bias, ffn_out_bias, norm2_gain, norm2_bias, ffn_in_bias)
    small = pack_small([p.reshape(1, -1, unit) for p in small_args] + [rel_table[None]], 1).astype(BF16)
    weights = [w.astype(BF16) for w in (qkv_weight, out_weight, ffn_in_weight, ffn_out_weight)]
    content_rows = content_stream.reshape(row_count, width)
    query_rows = query_stream.reshape(row_count, width)
    if linked:
        out_proj, in_proj, out_ffn, joined_proj, small, mixed, totals, proj = forward_attention(
            True, content_rows, query_rows, lengths, factor_order, weights, small)
    else:
        gather = lambda a: lax.all_gather(a, "fsdp", axis=0, tiled=True)
        joined_proj, out_proj, in_proj, out_ffn = [gather(w) for w in weights]
        small = gather(small)
        mixed, totals, proj = forward_attention(False, content_rows, query_rows, lengths, factor_order, [joined_proj], small)
    vectors = small.reshape(shards, ROWS, LANE)[:, :, :unit].astype(F32)
    flat = vectors.transpose(1, 0, 2).reshape(ROWS, width)
    out_shift, gain_one, shift_one, ffn_shift, gain_two, shift_two = [flat[k] for k in range(2, 8)]
    in_shift = vectors[:, 8:12].reshape(-1)
    mixed_rows = mixed.reshape(2 * row_count, width)
    input_rows = jnp.concatenate([content_rows, query_rows], 0).astype(F32)
    branch = jnp.dot(mixed_rows, out_proj, preferred_element_type=F32) + out_shift
    first_out, normed_one, inverse_one = norm_forward(input_rows + branch, gain_one, shift_one)
    first_low = first_out.astype(BF16)
    hidden_in = jnp.dot(first_low, in_proj, preferred_element_type=F32) + in_shift
    hidden_low = gelu_value(hidden_in).astype(BF16)
    ffn_rows = jnp.dot(hidden_low, out_ffn, preferred_element_type=F32) + ffn_shift
    final_rows, normed_two, inverse_two = norm_forward(first_low.astype(F32) + ffn_rows, gain_two, shift_two)
    valid_rows = (jnp.arange(seq_len)[None, :] < lengths[:, None]).reshape(row_count, 1).astype(F32)
    valid_both = jnp.concatenate([valid_rows, valid_rows], 0)
    upstream = jnp.concatenate([content_cot.reshape(row_count, width), query_cot.reshape(row_count, width)], 0).astype(F32) * valid_both
    grad_sum_two, grad_gain_two, grad_shift_two = norm_backward(upstream, normed_two, inverse_two, gain_two)
    grad_ffn = grad_sum_two.astype(BF16)
    grad_ffn_shift = jnp.sum(grad_ffn.astype(F32), 0)
    grad_out_ffn = rows_inner(hidden_low, grad_ffn).astype(BF16)
    grad_hidden = (times_transpose(grad_ffn, out_ffn) * gelu_slope(hidden_in)).astype(BF16)
    grad_in_shift = jnp.sum(grad_hidden.astype(F32), 0)
    grad_in_proj = rows_inner(first_low, grad_hidden).astype(BF16)
    grad_first = grad_sum_two + times_transpose(grad_hidden, in_proj)
    grad_sum_one, grad_gain_one, grad_shift_one = norm_backward(grad_first, normed_one, inverse_one, gain_one)
    grad_branch = grad_sum_one.astype(BF16)
    grad_out_shift = jnp.sum(grad_branch.astype(F32), 0)
    grad_out_proj = rows_inner(mixed_rows, grad_branch).astype(BF16)
    grad_mixed = times_transpose(grad_branch, out_proj).astype(BF16)
    ready = [grad_in_proj, grad_out_ffn, grad_out_proj] if linked else []
    early, grads, grad_table = backward_attention(linked, proj, grad_mixed, mixed_rows, totals, lengths, factor_order, small, ready)
    grad_q = rows_inner(content_rows, grads[0]) + rows_inner(query_rows, grads[3])
    grad_joined = jnp.concatenate([grad_q, rows_inner(content_rows, grads[1]), rows_inner(content_rows, grads[2])], 1).astype(BF16)
    low_sums = jnp.sum(grads.astype(F32), 1)
    grad_proj_shift = jnp.concatenate([low_sums[0] + low_sums[3], low_sums[2]])
    small_grads = (grad_proj_shift, grad_out_shift, grad_gain_one, grad_shift_one, grad_ffn_shift, grad_gain_two, grad_shift_two, grad_in_shift)
    packed = pack_small([g.reshape(shards, -1, unit) for g in small_grads] + [grad_table.reshape(shards, -1, HEADS)], shards)
    if linked:
        packed = packed.reshape(4, 2, ROWS, LANE).transpose(1, 0, 2, 3).reshape(8 * ROWS, LANE)
        sum_joined, mine = reduce_rest([grad_joined], packed)
        sum_in, sum_out, sum_proj = early
    else:
        scatter = lambda a: lax.psum(lax.psum_scatter(a, "fsdp", scatter_dimension=0, tiled=True), "rep")
        sum_joined, sum_in, sum_out, sum_proj = [scatter(a) for a in (grad_joined, grad_in_proj, grad_out_ffn, grad_out_proj)]
        mine = scatter(packed)
    sum_joined, sum_in, sum_out, sum_proj = [a.astype(F32) for a in (sum_joined, sum_in, sum_out, sum_proj)]
    content_grad_rows = grad_sum_one[:row_count] + (
        times_transpose(grads[0], joined_proj[:, :width])
        + times_transpose(grads[1], joined_proj[:, width : 2 * width])
        + times_transpose(grads[2], joined_proj[:, 2 * width :])
    )
    query_grad_rows = grad_sum_one[row_count:] + times_transpose(grads[3], joined_proj[:, :width])
    vec = lambda k: mine[k, :unit]
    block_shape = (seq_count, seq_len, width)
    return (
        final_rows[:row_count].reshape(block_shape).astype(BF16),
        final_rows[row_count:].reshape(block_shape).astype(BF16),
        content_grad_rows.reshape(block_shape).astype(BF16),
        query_grad_rows.reshape(block_shape).astype(BF16),
        sum_joined,
        mine[0:2, :unit].reshape(-1),
        sum_proj,
        vec(2),
        vec(3),
        vec(4),
        mine[TABLE_ROW : TABLE_ROW + rel_table.shape[0], :HEADS],
        sum_in,
        mine[8:12, :unit].reshape(-1),
        sum_out,
        vec(5),
        vec(6),
        vec(7),
    )


def solution(mesh):
    in_specs = (
        P(("rep", "fsdp"), None, None),
        P(("rep", "fsdp"), None, None),
        P(("rep", "fsdp")),
        P(("rep", "fsdp"), None),
        P("fsdp", None),
        P("fsdp"),
        P("fsdp", None),
        P("fsdp"),
        P("fsdp"),
        P("fsdp"),
        P("fsdp", None),
        P("fsdp", None),
        P("fsdp"),
        P("fsdp", None),
        P("fsdp"),
        P("fsdp"),
        P("fsdp"),
        P(("rep", "fsdp"), None, None),
        P(("rep", "fsdp"), None, None),
    )
    out_specs = (
        P(("rep", "fsdp"), None, None),
        P(("rep", "fsdp"), None, None),
        P(("rep", "fsdp"), None, None),
        P(("rep", "fsdp"), None, None),
        P("fsdp", None),
        P("fsdp"),
        P("fsdp", None),
        P("fsdp"),
        P("fsdp"),
        P("fsdp"),
        P("fsdp", None),
        P("fsdp", None),
        P("fsdp"),
        P("fsdp", None),
        P("fsdp"),
        P("fsdp"),
        P("fsdp"),
    )
    return jax.shard_map(
        functools.partial(on_device, tuple(mesh.shape[a] for a in mesh.axis_names)),
        mesh=mesh,
        in_specs=in_specs,
        out_specs=out_specs,
        check_vma=False,
    )
```

time: 612 us -> 430 us (0.70)
  waiting for transfers between devices: 218 us -> 0 us
  Pallas kernels: 79.8 us -> 205 us
  blocking collectives: 55.6 us -> 0 us
  local copies, waits for them, and re-layouts: 35.6 us -> 15.7 us
  between operations: 14.7 us -> 1.66 us
  matrix products: 164 us -> 151 us
  other arithmetic: 39.3 us -> 49 us
    pallas_call x2 -> x3, Pallas kernels: 79.8 us -> 205 us  [the longest x1 86.1 us: backward_attention(): pl.pallas_call(functools.partial(backward_kernel, shapes, linked), grid=(...]
    reduce_scatter x3 -> x0, waiting for transfers between devices: 86.2 us -> none  [on_device(): lax.psum_scatter(a.astype(BF16), 'fsdp', scatter_dimension=0, tiled=True)]
    all_gather x4 -> x0, waiting for transfers between devices: 76.7 us -> none  [on_device(): gather = lambda a: lax.all_gather(a, 'fsdp', axis=0, tiled=True)]
    psum x1 -> x0, waiting for transfers between devices: 54.9 us -> none  [on_device(): over = lambda a: lax.psum(a, 'rep').astype(F32)]
    psum x1 -> x0, blocking collectives: 39.5 us -> none  [on_device(): packed_grads = lax.psum(packed_grads, ('rep', 'fsdp'))]
    all_gather x1 -> x0, blocking collectives: 16.1 us -> none  [on_device(): lax.all_gather(pack([p.astype(BF16) for p in small]), 'fsdp', axis=0, til...]
    unnamed x89 -> x65, local copies, waits for them, and re-layouts: 19.1 us -> 5.03 us
    dot_general x5 -> x1, matrix products: 13.2 us -> 1.66 us  [backward_attention(): jnp.dot(sums, jnp.asarray(fold), precision=lax.Precision.HIGHEST)]
  transfers between devices with their start and end apart: 9 -> 0, of which waited for: 6 -> 0; matrix products, arithmetic and copies ran while one was open for 21% -> 0% of each run, Pallas kernels for 5% -> 0%
where the time goes in v2:
time: 430 us; the launch traced here: 422 us
  Pallas kernels  205 us (48%)
  matrix products  151 us (35%)
  other arithmetic  49 us (11%)
  local copies, waits for them, and re-layouts  15.7 us (4%)
    pallas_call x1, Pallas kernels, backward_attention(): pl.pallas_call(functools.partial(backward_kernel, shapes, linked), grid=(...  86.1 us
    pallas_call x1, Pallas kernels, forward_attention(): pl.pallas_call(functools.partial(forward_kernel, shapes, linked), grid=(p...  81.8 us
    dot_general x7, matrix products, times_transpose(): lax.dot_general(left_op, right_op, (((1,), (1,)), ((), ())), preferred_el...  63.1 us
    dot_general x7, matrix products, rows_inner(): lax.dot_general(left_op, right_op, (((0,), (0,)), ((), ())), preferred_el...  44.8 us
    pallas_call x1, Pallas kernels, reduce_rest(): pl.pallas_call(functools.partial(reduce_kernel, shapes, n), out_shape=[ja...  36.9 us
    dot_general x1, matrix products, on_device(): jnp.dot(first_low, in_proj, preferred_element_type=F32) + in_shift  22 us
    dot_general x1, matrix products, on_device(): jnp.dot(hidden_low, out_ffn, preferred_element_type=F32) + ffn_shift  13.7 us

profile of v2, /device:TPU:0, one launch (start us, length us, event | category | flops | bytes accessed | tf_op | source)
XLA Modules:
  0.0 422.2 jit_solution(2380087229547394487)
XLA Ops:
  5.4 0.7 convert_bitcast_fusion
  6.9 1.2 concatenate.28
  8.1 0.7 compare_bitcast_fusion
  8.9 1.6 convert_element_type.139.refs_1_
  10.5 2.0 convert_element_type.138.refs_0_
  12.5 2.2 convert_element_type.140.refs_2_
  14.6 2.1 convert_element_type.141.refs_3_
  16.8 81.8 %attention_forward.1 = (bf16[768,768]{1,0:T(8,128)(2,1)}, bf16[768,3072]{1,0:T(8,128)(2,1)}, bf16[3072,768]{1,0:T(8,128)(2,1)}, bf16[768,2304]{1,0:T(8,128)(2,1)...) custom-call(s32[2]{0:T(128)} %len_ref.3, ...), custom_call_target="tpu_custom_call" | custom-call | flops 8053063680 | bytes 31457280 | tf_op jit(solution)/shard_map/attention_forward/pallas_call | solution.py:675
  98.5 0.8 slice_convert_fusion
  99.9 5.8 %fusion.61 = (f32[2048]{0:T(1024)S(1)}, f32[2048,768]{1,0:T(8,128)S(1)}) fusion(f32[768]{0:T(1024)S(1)} %add.143, bf16[2048,768]{1,0:T(8,128)(2,1)} %bitcast.151, bf16[768,768]{1,0:T(8,128)(2,1)} %get-tuple-element.33, bf16[1024,768]{1,0:T(8,128)(2,1)S(1)} %bitcast.144, bf16[1024,768]{1,0:T(8,128)(2,1)} %bitcast.147), kind=kOutput, calls=%fused_computation.115 | convolution fusion | flops 2426927104 | bytes 13773824 | tf_op jit(solution)/shard_map/dot_general | solution.py:1068
  105.8 0.8 multiply_reduce_fusion.5
  106.7 22.0 %multiply_convert_fusion = (bf16[2048,3072]{1,0:T(8,128)(2,1)}, f32[2048,3072]{1,0:T(8,128)}) fusion(f32[3072]{0:T(1024)S(1)} %add.151, bf16[768,3072]{1,0:T(8,128)(2,1)} %get-tuple-element.35, f32[2048,768]{1,0:T(8,128)S(1)} %get-tuple-element.79, f32[768]{0:T(1024)S(1)} %add.148, f32[768]{0:T(1024)S(1)} %mul.144, f32[2048]{0:T(1024)S(1)} %add_rsqrt_fusion.1, ...), kind=kOutput, calls=%fused_computation.8 | convolution fusion | flops 9709289472 | bytes 48793600 | tf_op jit(solution)/shard_map/dot_general | solution.py:1071
  128.6 13.7 %fusion.62 = (f32[2048]{0:T(1024)S(1)}, f32[2048,768]{1,0:T(8,128)S(1)}) fusion(f32[768]{0:T(1024)S(1)} %add.155, bf16[2048,3072]{1,0:T(8,128)(2,1)} %get-tuple-element.80, bf16[3072,768]{1,0:T(8,128)(2,1)S(1)} %bitcast.159, f32[768]{0:T(1024)S(1)} %add.148, f32[768]{0:T(1024)S(1)} %mul.144, f32[2048]{0:T(1024)S(1)} %add_rsqrt_fusion.1, ...), kind=kOutput, calls=%fused_computation.116 | convolution fusion | flops 9677830144 | bytes 29918208 | tf_op jit(solution)/shard_map/dot_general | solution.py:1073
  142.4 0.8 multiply_reduce_fusion.4
  143.3 1.7 copy-done.5
  144.9 1.6 copy-done.6
  146.5 5.3 %multiply_reduce_fusion = (f32[768]{0:T(1024)S(1)}, f32[2048]{0:T(1024)S(1)}, f32[2048]{0:T(1024)S(1)}, f32[768]{0:T(1024)S(1)}) fusion(f32[2048,768]{1,0:T(8,128)S(1)} %get-tuple-element.83, f32[2048]{0:T(1024)S(1)} %bitcast.131, f32[2048]{0:T(1024)S(1)} %add_rsqrt_fusion, f32[2048]{0:T(1024)S(1)} %broadcast_multiply_fusion.4, ...), kind=kLoop, calls=%fused_computation.11 | loop fusion | flops 22014464 | bytes 9487360 | tf_op jit(solution)/shard_map/reduce_sum | solution.py:1006
  152.1 8.0 %convert_reduce_fusion.2 = (f32[768]{0:T(1024)S(1)}, f32[2048,768]{1,0:T(8,128)S(1)}, bf16[2048,768]{1,0:T(8,128)(2,1)}) fusion(f32[2048]{0:T(1024)S(1)} %get-tuple-element.87, f32[2048,768]{1,0:T(8,128)} %copy-done, f32[2048]{0:T(1024)S(1)} %broadcast_multiply_fusion.4, f32[2048]{0:T(1024)S(1)} %get-tuple-element.88, f32[768]{0:T(1024)S(1)} %mul.153, ...), kind=kLoop, calls=%fused_computation.12 | loop fusion | flops 28310784 | bytes 18924544 | tf_op jit(solution)/shard_map/reduce_sum | solution.py:1080
  160.0 27.2 %convert_reduce_fusion = (f32[3072]{0:T(1024)S(1)}, bf16[2048,3072]{1,0:T(8,128)(2,1)}) fusion(f32[2048,3072]{1,0:T(8,128)} %get-tuple-element.81, f32[3072]{0:T(1024)S(1)} %add.151, bf16[3072,768]{1,0:T(8,128)(2,1)} %get-tuple-element.36, f32[2048,768]{1,0:T(8,128)S(1)} %get-tuple-element.64), kind=kOutput, calls=%fused_computation.7 | convolution fusion | flops 9747035136 | bytes 48783360 | tf_op jit(solution)/shard_map/dot_general | solution.py:1027
  187.3 13.4 %convolution_convert_fusion.refs_1_ = bf16[3072,768]{1,0:T(8,128)(2,1)} fusion(bf16[2048,3072]{1,0:T(8,128)(2,1)S(1)} %bitcast.157, f32[2048,768]{1,0:T(8,128)S(1)} %get-tuple-element.64), kind=kOutput, calls=%fused_computation.32 | convolution fusion | flops 9667608576 | bytes 23592960 | tf_op jit(solution)/shard_map/dot_general | solution.py:1021
  200.9 20.5 %multiply_reduce_fusion.1 = (f32[768]{0:T(1024)S(1)}, f32[2048]{0:T(1024)S(1)}, f32[2048]{0:T(1024)S(1)}, f32[768]{0:T(1024)S(1)}, f32[2048,768]{1,0:T(8,128)}) fusion(f32[2048,768]{1,0:T(8,128)} %copy-done.1, f32[2048]{0:T(1024)S(1)} %add_rsqrt_fusion.1, f32[2048]{0:T(1024)S(1)} %broadcast_multiply_fusion.5, f32[768]{0:T(1024)S(1)} %mul.144, ...), kind=kOutput, calls=%fused_computation.13 | convolution fusion | flops 9679398912 | bytes 36217856 | tf_op jit(solution)/shard_map/dot_general | solution.py:1027
  221.4 16.2 %convolution_convert_fusion.1.refs_0_ = bf16[768,3072]{1,0:T(8,128)(2,1)} fusion(bf16[2048,3072]{1,0:T(8,128)(2,1)} %get-tuple-element.86, f32[2048,768]{1,0:T(8,128)S(1)} %bitcast.113, f32[768]{0:T(1024)S(1)} %add.148, f32[768]{0:T(1024)S(1)} %mul.144, f32[2048]{0:T(1024)S(1)} %add_rsqrt_fusion.1, f32[2048]{0:T(1024)S(1)} %broadcast_multiply_fusion.5), kind=kOutput, calls=%fused_computation.33 | convolution fusion | flops 9673900032 | bytes 23615488 | tf_op jit(solution)/shard_map/dot_general | solution.py:1021
  237.7 7.6 %convert_reduce_fusion.3 = (f32[768]{0:T(1024)S(1)}, f32[2048,768]{1,0:T(8,128)}) fusion(f32[2048]{0:T(1024)S(1)} %broadcast_multiply_fusion, f32[2048,768]{1,0:T(8,128)} %copy-done.1, f32[2048]{0:T(1024)S(1)} %broadcast_multiply_fusion.5, f32[2048]{0:T(1024)S(1)} %broadcast_multiply_fusion.1, f32[2048,768]{1,0:T(8,128)} %get-tuple-element.84, ...), kind=kLoop, calls=%fused_computation.14 | loop fusion | flops 15727872 | bytes 18913280 | tf_op jit(solution)/shard_map/reduce_sum | solution.py:1088
  245.5 6.6 %convolution_convert_fusion.3.refs_2_ = bf16[768,768]{1,0:T(8,128)(2,1)} fusion(bf16[2048,768]{1,0:T(8,128)(2,1)S(1)} %bitcast.154, f32[2048,768]{1,0:T(8,128)} %get-tuple-element.66), kind=kOutput, calls=%fused_computation.59 | convolution fusion | flops 2418081792 | bytes 10616832 | tf_op jit(solution)/shard_map/dot_general | solution.py:1021
  252.1 4.1 convolution_convert_fusion.2.dc_ref.dg_ref
  256.2 86.1 %attention_backward.1 = (bf16[96,3072]{1,0:T(8,128)(2,1)}, bf16[384,768]{1,0:T(8,128)(2,1)}, bf16[96,768]{1,0:T(8,128)(2,1)}, bf16[4,1024,768]{2,1,0:T(8,128)(2,1)}, f32[12,768]{1,0:T(8,128)}) custom-call(s32[2]{0:T(128)} %len_ref.3, bf16[1024,3072]{1,0:T(8,128)(2,1)} %get-tuple-element.37.q_ref.k_ref.v_ref.g_ref, ...), custom_call_target="tpu_custom_call" | custom-call | flops 16106127360 | bytes 31457280 | tf_op jit(solution)/shard_map/attention_backward/pallas_call | solution.py:879
  342.3 1.7 fusion.63
  344.0 3.8 convert_reduce_fusion.1
  348.7 0.7 convert_element_type.167
  349.4 1.1 convert_element_type.168
  350.5 1.1 convert_element_type.169
  351.6 4.1 fusion.36
  355.8 1.5 fusion.33
  357.4 4.0 fusion.9
  361.4 1.5 fusion.11
  362.9 1.5 fusion.39
  364.4 2.2 pad_maximum_fusion.refs_0_
  366.6 36.9 %reduce_rest.1 = (bf16[96,2304]{1,0:T(8,128)(2,1)}, f32[16,128]{1,0:T(8,128)}) custom-call(bf16[768,2304]{1,0:T(8,128)(2,1)} %pad_maximum_fusion.refs_0_, f32[128,128]{1,0:T(8,128)} %bitcast.129), custom_call_target="tpu_custom_call" | custom-call | tf_op jit(solution)/shard_map/reduce_rest/pallas_call | solution.py:980
  403.5 0.7 slice.128
  406.2 1.3 slice.132
  407.5 1.4 slice_bitcast_fusion
  408.9 2.0 convert_element_type.166
  410.9 3.3 fusion.19
  414.2 0.8 copy-done.10
  415.0 1.4 fusion.23
  416.4 0.7 slice-done.5
  417.1 2.7 fusion.10
  419.8 1.9 fusion.60
  (128 shorter events, 10.0 us)
Async XLA Ops:
  16.8 83.1 %copy-start.12 = (bf16[2,512,768]{2,1,0:T(8,128)(2,1)S(1)}, bf16[2,512,768]{2,1,0:T(8,128)(2,1)}, u32[]{:S(2)}) copy-start(bf16[2,512,768]{2,1,0:T(8,128)(2,1)} %param.23) | copy-start | bytes 4718596
  105.8 22.9 %copy-start.1 = (f32[2048,768]{1,0:T(8,128)}, f32[2048,768]{1,0:T(8,128)S(1)}, u32[]{:S(2)}) copy-start(f32[2048,768]{1,0:T(8,128)S(1)} %get-tuple-element.79) | copy-start | bytes 18874372
  105.8 22.9 %slice-start.13 = ((s8[4718592]{0:T(1024)(128)(4,1)}), s8[4194304]{0:T(1024)(128)(4,1)S(1)}, s32[]{:S(2)}) async-start(s8[4718592]{0:T(1024)(128)(4,1)} %bitcast.158), calls=%async_computation.13 | async-start | bytes 8388608
  106.7 22.0 %slice-start.14 = ((s8[4718592]{0:T(1024)(128)(4,1)}), s8[524288]{0:T(1024)(128)(4,1)S(1)}, s32[]{:S(2)}) async-start(s8[4718592]{0:T(1024)(128)(4,1)} %bitcast.158), calls=%async_computation.14 | async-start | bytes 1048576
  142.3 9.5 %copy-start = (f32[2048,768]{1,0:T(8,128)}, f32[2048,768]{1,0:T(8,128)S(1)}, u32[]{:S(2)}) copy-start(f32[2048,768]{1,0:T(8,128)S(1)} %get-tuple-element.83) | copy-start | bytes 18874372
  142.4 2.6 copy-start.5
  142.4 4.1 copy-start.6
  152.0 35.2 %slice-start.10 = ((s8[12582912]{0:T(1024)(128)(4,1)}), s8[4194304]{0:T(1024)(128)(4,1)S(1)}, s32[]{:S(2)}) async-start(s8[12582912]{0:T(1024)(128)(4,1)} %bitcast.156), calls=%async_computation.10 | async-start | bytes 8388608
  160.0 27.2 %copy-start.4 = (f32[2048,768]{1,0:T(8,128)}, f32[2048,768]{1,0:T(8,128)S(1)}, u32[]{:S(2)}) copy-start(f32[2048,768]{1,0:T(8,128)S(1)} %get-tuple-element.64) | copy-start | bytes 18874372
  160.0 27.2 %slice-start.11 = ((s8[12582912]{0:T(1024)(128)(4,1)}), s8[4194304]{0:T(1024)(128)(4,1)S(1)}, s32[]{:S(2)}) async-start(s8[12582912]{0:T(1024)(128)(4,1)} %bitcast.156), calls=%async_computation.11 | async-start | bytes 8388608
  160.0 27.2 %slice-start.12 = ((s8[12582912]{0:T(1024)(128)(4,1)}), s8[4194304]{0:T(1024)(128)(4,1)S(1)}, s32[]{:S(2)}) async-start(s8[12582912]{0:T(1024)(128)(4,1)} %bitcast.156), calls=%async_computation.12 | async-start | bytes 8388608
  187.3 34.1 %slice-start = ((s8[6291456]{0:T(1024)(128)(4,1)}), s8[2097152]{0:T(1024)(128)(4,1)S(1)}, s32[]{:S(2)}) async-start(s8[6291456]{0:T(1024)(128)(4,1)} %bitcast.112), calls=%async_computation | async-start | bytes 4194304
  200.9 20.5 %slice-start.1 = ((s8[6291456]{0:T(1024)(128)(4,1)}), s8[4194304]{0:T(1024)(128)(4,1)S(1)}, s32[]{:S(2)}) async-start(s8[6291456]{0:T(1024)(128)(4,1)} %bitcast.112), calls=%async_computation.1 | async-start | bytes 8388608
  237.7 7.7 %copy-start.15 = (bf16[2,1024,768]{2,1,0:T(8,128)(2,1)S(1)}, bf16[2,1024,768]{2,1,0:T(8,128)(2,1)}, u32[]{:S(2)}) copy-start(bf16[2,1024,768]{2,1,0:T(8,128)(2,1)} %get-tuple-element.32) | copy-start | bytes 9437188
  245.4 6.6 %copy-start.2 = (f32[2048,768]{1,0:T(8,128)S(1)}, f32[2048,768]{1,0:T(8,128)}, u32[]{:S(2)}) copy-start(f32[2048,768]{1,0:T(8,128)} %get-tuple-element.66) | copy-start | bytes 18874372
  245.5 6.6 %copy-start.16 = (bf16[768,768]{1,0:T(8,128)(2,1)S(1)}, bf16[768,768]{1,0:T(8,128)(2,1)}, u32[]{:S(2)}) copy-start(bf16[768,768]{1,0:T(8,128)(2,1)} %get-tuple-element.33) | copy-start | bytes 3538948
  256.2 86.1 %copy-start.9 = (f32[768,32]{1,0:T(8,128)S(1)}, f32[768,32]{1,0:T(8,128)}, u32[]{:S(2)}) copy-start(f32[768,32]{1,0:T(8,128)} %constant.36.clone) | copy-start | bytes 294916
  342.2 6.4 %copy-start.11 = (bf16[96,768]{1,0:T(8,128)(2,1)S(1)}, bf16[96,768]{1,0:T(8,128)(2,1)}, u32[]{:S(2)}) copy-start(bf16[96,768]{1,0:T(8,128)(2,1)} %get-tuple-element.44) | copy-start | bytes 442372
  342.2 7.2 %copy-start.8 = (bf16[96,3072]{1,0:T(8,128)(2,1)S(1)}, bf16[96,3072]{1,0:T(8,128)(2,1)}, u32[]{:S(2)}) copy-start(bf16[96,3072]{1,0:T(8,128)(2,1)} %get-tuple-element.45) | copy-start | bytes 1769476
  342.3 8.3 %copy-start.7 = (bf16[384,768]{1,0:T(8,128)(2,1)S(1)}, bf16[384,768]{1,0:T(8,128)(2,1)}, u32[]{:S(2)}) copy-start(bf16[384,768]{1,0:T(8,128)(2,1)} %get-tuple-element.46) | copy-start | bytes 1769476
  343.9 11.8 %slice-start.6 = ((s8[6291456]{0:T(1024)(128)(4,1)}), s8[2097152]{0:T(1024)(128)(4,1)S(1)}, s32[]{:S(2)}) async-start(s8[6291456]{0:T(1024)(128)(4,1)} %bitcast.118), calls=%async_computation.6 | async-start | bytes 4194304
  350.5 5.2 %slice-start.7 = ((s8[6291456]{0:T(1024)(128)(4,1)}), s8[4194304]{0:T(1024)(128)(4,1)S(1)}, s32[]{:S(2)}) async-start(s8[6291456]{0:T(1024)(128)(4,1)} %bitcast.118), calls=%async_computation.7 | async-start | bytes 8388608
  350.5 5.2 %copy-start.14 = (bf16[2,512,768]{2,1,0:T(8,128)(2,1)S(1)}, bf16[2,512,768]{2,1,0:T(8,128)(2,1)}, u32[]{:S(2)}) copy-start(bf16[2,512,768]{2,1,0:T(8,128)(2,1)} %param.22) | copy-start | bytes 4718596
  351.6 5.6 %slice-start.2 = ((s8[6291456]{0:T(1024)(128)(4,1)}), s8[4194304]{0:T(1024)(128)(4,1)S(1)}, s32[]{:S(2)}) async-start(s8[6291456]{0:T(1024)(128)(4,1)} %bitcast.114), calls=%async_computation.2 | async-start | bytes 8388608
  355.8 1.6 slice-start.3
  357.4 4.0 copy-start.13
  366.6 47.6 %slice-start.8 = ((s8[6291456]{0:T(1024)(128)(4,1)}), s8[2097152]{0:T(1024)(128)(4,1)S(1)}, s32[]{:S(2)}) async-start(s8[6291456]{0:T(1024)(128)(4,1)} %bitcast.120), calls=%async_computation.8 | async-start | bytes 4194304
  410.9 3.3 slice-start.9
  410.9 4.1 copy-start.10
  410.9 5.5 %slice-start.4 = ((s8[6291456]{0:T(1024)(128)(4,1)}), s8[4194304]{0:T(1024)(128)(4,1)S(1)}, s32[]{:S(2)}) async-start(s8[6291456]{0:T(1024)(128)(4,1)} %bitcast.116), calls=%async_computation.4 | async-start | bytes 8388608
  415.0 2.2 slice-start.5
  417.1 2.7 copy-start.3

commit v3 on v2

--- a/solution.py
+++ b/solution.py
@@ -25,7 +25,6 @@
 MESH = pl.DeviceIdType.MESH
 VMEM_BYTES = 60 * 2**20
 eps_norm = 1e-05
-root_half = 0.7071067811865476
 inv_root_tau = 0.3989422804014327
 
 
@@ -988,33 +987,156 @@
     )(*weight_grads, small_grads)
 
 
-def norm_forward(summed, gain_vec, shift_vec):
+ERF_P = 0.3275911 * 0.7071067811865476
+ERF_A = (0.254829592 * 0.5, -0.284496736 * 0.5, 1.421413741 * 0.5, -1.453152027 * 0.5, 1.061405429 * 0.5)
+
+
+def gelu_pair(z):
+    bell = jnp.exp2(z * z * (-0.5 * LOG2E))
+    t = 1.0 / (1.0 + ERF_P * jnp.abs(z))
+    tail = ERF_A[4]
+    for a in ERF_A[3::-1]:
+        tail = tail * t + a
+    tail = tail * t * bell
+    share = jnp.where(z < 0.0, tail, 1.0 - tail)
+    return z * share, share + z * bell * inv_root_tau
+
+
+def norm_rows(summed):
     row_mean = jnp.mean(summed, -1, keepdims=True)
     centered = summed - row_mean
     inverse = lax.rsqrt(jnp.mean(centered * centered, -1, keepdims=True) + eps_norm)
-    normed = centered * inverse
-    return (normed * gain_vec + shift_vec, normed, inverse)
-
-
-def norm_backward(upstream, normed, inverse, gain_vec):
-    scaled = upstream * gain_vec
-    centered = (
-        scaled
-        - jnp.mean(scaled, -1, keepdims=True)
-        - normed * jnp.mean(scaled * normed, -1, keepdims=True)
-    )
-    return (inverse * centered, jnp.sum(upstream * normed, 0), jnp.sum(upstream, 0))
-
-
-def gelu_value(hidden_in):
-    return 0.5 * hidden_in * (1.0 + lax.erf(hidden_in * root_half))
-
-
-def gelu_slope(hidden_in):
-    return (
-        0.5 * (1.0 + lax.erf(hidden_in * root_half))
-        + hidden_in * jnp.exp(-0.5 * hidden_in * hidden_in) * inv_root_tau
-    )
+    return centered * inverse, inverse
+
+
+def norm_rows_back(scaled, normed, inverse):
+    return inverse * (scaled - jnp.mean(scaled, -1, keepdims=True) - normed * jnp.mean(scaled * normed, -1, keepdims=True))
+
+
+def fold8(value):
+    rows, cols = value.shape
+    return jnp.sum(value.reshape(rows // 8, 8, cols), 0)
+
+
+def ffn_kernel(chunk, len_ref, mixed_ref, content_ref, query_ref, ccot_ref, qcot_ref, small_ref, wo_hbm, win_hbm, wout_hbm,
+               cout_ref, qout_ref, hid_ref, dz_ref, first_ref, dffn_ref, dbranch_ref, dmixed_ref, sums_ref, wide_sums_ref,
+               wo_ref, win_ref, wout_ref, vec_ref, shift_ref, slope_ref, acc_ref, wide_acc_ref, sem):
+    i = pl.program_id(0)
+    n = pl.num_programs(0)
+    rows, width = mixed_ref.shape
+    hidden = win_ref.shape[1]
+    loads = [pltpu.make_async_copy(a, b, sem.at[k]) for k, (a, b) in enumerate(((wo_hbm, wo_ref), (win_hbm, win_ref), (wout_hbm, wout_ref)))]
+
+    @pl.when(i == 0)
+    def _():
+        for d in loads:
+            d.start()
+        small = small_ref[...].astype(F32)
+        shards = small.shape[0] // ROWS
+        unit = width // shards
+        for k in range(2, 8):
+            vec_ref[k : k + 1, :] = spread_rows(small, [f * ROWS + k for f in range(shards)], 0, shards, unit)
+        count = hidden // unit
+        shift_ref[0:1, :] = spread_rows(small, [k // 4 * ROWS + 8 + k % 4 for k in range(count)], 0, count, unit)
+        acc_ref[...] = jnp.zeros_like(acc_ref)
+        wide_acc_ref[...] = jnp.zeros_like(wide_acc_ref)
+        for d in loads:
+            d.wait()
+
+    first_stream = i < n // 2
+    vec = lambda k: vec_ref[k : k + 1, :]
+
+    def add_sum(k, value):
+        acc_ref[k] = acc_ref[k] + fold8(value)
+
+    residual = jnp.where(first_stream, content_ref[...], query_ref[...]).astype(F32)
+    branch = nn(mixed_ref[...], wo_ref[...]) + vec(2)
+    normed_one, inverse_one = norm_rows(residual + branch)
+    first_low = (normed_one * vec(3) + vec(4)).astype(BF16)
+    first_ref[...] = first_low
+    for c in range(0, hidden, chunk):
+        cols = slice(c, c + chunk)
+        value, slope = gelu_pair(nn(first_low, win_ref[:, cols]) + shift_ref[0:1, cols])
+        hid_ref[:, cols] = value.astype(BF16)
+        slope_ref[:, cols] = slope.astype(BF16)
+    ffn = nn(hid_ref[...], wout_ref[...]) + vec(5)
+    normed_two, inverse_two = norm_rows(first_low.astype(F32) + ffn)
+    final = (normed_two * vec(6) + vec(7)).astype(BF16)
+
+    @pl.when(first_stream)
+    def _():
+        cout_ref[...] = final
+
+    @pl.when(jnp.logical_not(first_stream))
+    def _():
+        qout_ref[...] = final
+
+    per_stream = n // 2
+    at = jnp.where(first_stream, i, i - per_stream) * rows
+    seq_len = per_stream * rows // len_ref.shape[0]
+    seq = at // seq_len
+    place = at - seq * seq_len + lax.broadcasted_iota(jnp.int32, (rows, 1), 0)
+    upstream = jnp.where(first_stream, ccot_ref[...], qcot_ref[...]).astype(F32)
+    upstream = jnp.where(place < len_ref[seq], upstream, 0.0)
+    add_sum(5, upstream * normed_two)
+    add_sum(6, upstream)
+    grad_two = norm_rows_back(upstream * vec(6), normed_two, inverse_two)
+    grad_ffn = grad_two.astype(BF16)
+    dffn_ref[...] = grad_ffn
+    add_sum(4, grad_ffn.astype(F32))
+    for c in range(0, hidden, chunk):
+        cols = slice(c, c + chunk)
+        grad = nt(grad_ffn, wout_ref[cols, :]) * slope_ref[:, cols].astype(F32)
+        wide_acc_ref[:, cols] = wide_acc_ref[:, cols] + fold8(grad)
+        dz_ref[:, cols] = grad.astype(BF16)
+    grad_first = grad_two + nt(dz_ref[...], win_ref[...])
+    add_sum(2, grad_first * normed_one)
+    add_sum(3, grad_first)
+    grad_branch = norm_rows_back(grad_first * vec(3), normed_one, inverse_one).astype(BF16)
+    dbranch_ref[...] = grad_branch
+    add_sum(1, grad_branch.astype(F32))
+    dmixed_ref[...] = nt(grad_branch, wo_ref[...]).astype(BF16)
+
+    @pl.when(i == n - 1)
+    def _():
+        for k in range(8):
+            sums_ref[k : k + 1, :] = jnp.sum(acc_ref[k], 0, keepdims=True)
+        wide_sums_ref[...] = jnp.sum(wide_acc_ref[...], 0, keepdims=True)
+
+
+def ffn_stage(mixed, content_rows, query_rows, content_cot, query_cot, lengths, small, out_proj, in_proj, out_ffn, rows=256, chunk=768):
+    total, width = mixed.shape
+    hidden = in_proj.shape[1]
+    n = total // rows
+    half = n // 2
+    anywhere = pl.BlockSpec(memory_space=pl.ANY)
+    row_block = lambda cols: pl.BlockSpec((rows, cols), lambda i: (i, 0))
+    low = pl.BlockSpec((rows, width), lambda i: (jnp.minimum(i, half - 1), 0))
+    high = pl.BlockSpec((rows, width), lambda i: (jnp.maximum(i - half, 0), 0))
+    whole = lambda shape: pl.BlockSpec(shape, lambda i: (0,) * len(shape))
+    shape = jax.ShapeDtypeStruct
+    return pl.pallas_call(
+        functools.partial(ffn_kernel, chunk),
+        grid=(n,),
+        in_specs=[pl.BlockSpec(memory_space=pltpu.SMEM), row_block(width), low, high, low, high, whole(small.shape)] + [anywhere] * 3,
+        out_specs=[low, high, row_block(hidden), row_block(hidden)] + [row_block(width)] * 4 + [whole((8, width)), whole((1, hidden))],
+        out_shape=[shape((total // 2, width), BF16)] * 2 + [shape((total, hidden), BF16)] * 2 + [shape((total, width), BF16)] * 4
+        + [shape((8, width), F32), shape((1, hidden), F32)],
+        scratch_shapes=[
+            pltpu.VMEM((width, width), BF16),
+            pltpu.VMEM((width, hidden), BF16),
+            pltpu.VMEM((hidden, width), BF16),
+            pltpu.VMEM((8, width), F32),
+            pltpu.VMEM((8, hidden), F32),
+            pltpu.VMEM((rows, hidden), BF16),
+            pltpu.VMEM((8, 8, width), F32),
+            pltpu.VMEM((8, hidden), F32),
+            pltpu.SemaphoreType.DMA((3,)),
+        ],
+        cost_estimate=pl.CostEstimate(flops=4 * total * width * (2 * hidden + width), bytes_accessed=60 * 2**20, transcendentals=2 * total * hidden),
+        compiler_params=pltpu.CompilerParams(dimension_semantics=("arbitrary",), vmem_limit_bytes=VMEM_BYTES),
+        name="ffn_stage",
+    )(lengths, mixed, content_rows, query_rows, content_cot, query_cot, small, out_proj, in_proj, out_ffn)
 
 
 def rows_inner(left_op, right_op):
@@ -1059,43 +1181,21 @@
         joined_proj, out_proj, in_proj, out_ffn = [gather(w) for w in weights]
         small = gather(small)
         mixed, totals, proj = forward_attention(False, content_rows, query_rows, lengths, factor_order, [joined_proj], small)
-    vectors = small.reshape(shards, ROWS, LANE)[:, :, :unit].astype(F32)
-    flat = vectors.transpose(1, 0, 2).reshape(ROWS, width)
-    out_shift, gain_one, shift_one, ffn_shift, gain_two, shift_two = [flat[k] for k in range(2, 8)]
-    in_shift = vectors[:, 8:12].reshape(-1)
     mixed_rows = mixed.reshape(2 * row_count, width)
-    input_rows = jnp.concatenate([content_rows, query_rows], 0).astype(F32)
-    branch = jnp.dot(mixed_rows, out_proj, preferred_element_type=F32) + out_shift
-    first_out, normed_one, inverse_one = norm_forward(input_rows + branch, gain_one, shift_one)
-    first_low = first_out.astype(BF16)
-    hidden_in = jnp.dot(first_low, in_proj, preferred_element_type=F32) + in_shift
-    hidden_low = gelu_value(hidden_in).astype(BF16)
-    ffn_rows = jnp.dot(hidden_low, out_ffn, preferred_element_type=F32) + ffn_shift
-    final_rows, normed_two, inverse_two = norm_forward(first_low.astype(F32) + ffn_rows, gain_two, shift_two)
-    valid_rows = (jnp.arange(seq_len)[None, :] < lengths[:, None]).reshape(row_count, 1).astype(F32)
-    valid_both = jnp.concatenate([valid_rows, valid_rows], 0)
-    upstream = jnp.concatenate([content_cot.reshape(row_count, width), query_cot.reshape(row_count, width)], 0).astype(F32) * valid_both
-    grad_sum_two, grad_gain_two, grad_shift_two = norm_backward(upstream, normed_two, inverse_two, gain_two)
-    grad_ffn = grad_sum_two.astype(BF16)
-    grad_ffn_shift = jnp.sum(grad_ffn.astype(F32), 0)
+    flat_cot = lambda a: a.reshape(row_count, width)
+    content_out, query_out, hidden_low, grad_hidden, first_low, grad_ffn, grad_branch, grad_mixed, sums, wide_sums = ffn_stage(
+        mixed_rows, content_rows, query_rows, flat_cot(content_cot), flat_cot(query_cot), lengths, small, out_proj, in_proj, out_ffn)
     grad_out_ffn = rows_inner(hidden_low, grad_ffn).astype(BF16)
-    grad_hidden = (times_transpose(grad_ffn, out_ffn) * gelu_slope(hidden_in)).astype(BF16)
-    grad_in_shift = jnp.sum(grad_hidden.astype(F32), 0)
     grad_in_proj = rows_inner(first_low, grad_hidden).astype(BF16)
-    grad_first = grad_sum_two + times_transpose(grad_hidden, in_proj)
-    grad_sum_one, grad_gain_one, grad_shift_one = norm_backward(grad_first, normed_one, inverse_one, gain_one)
-    grad_branch = grad_sum_one.astype(BF16)
-    grad_out_shift = jnp.sum(grad_branch.astype(F32), 0)
     grad_out_proj = rows_inner(mixed_rows, grad_branch).astype(BF16)
-    grad_mixed = times_transpose(grad_branch, out_proj).astype(BF16)
     ready = [grad_in_proj, grad_out_ffn, grad_out_proj] if linked else []
     early, grads, grad_table = backward_attention(linked, proj, grad_mixed, mixed_rows, totals, lengths, factor_order, small, ready)
     grad_q = rows_inner(content_rows, grads[0]) + rows_inner(query_rows, grads[3])
     grad_joined = jnp.concatenate([grad_q, rows_inner(content_rows, grads[1]), rows_inner(content_rows, grads[2])], 1).astype(BF16)
     low_sums = jnp.sum(grads.astype(F32), 1)
     grad_proj_shift = jnp.concatenate([low_sums[0] + low_sums[3], low_sums[2]])
-    small_grads = (grad_proj_shift, grad_out_shift, grad_gain_one, grad_shift_one, grad_ffn_shift, grad_gain_two, grad_shift_two, grad_in_shift)
-    packed = pack_small([g.reshape(shards, -1, unit) for g in small_grads] + [grad_table.reshape(shards, -1, HEADS)], shards)
+    rows_of = lambda g: g.reshape(shards, -1, unit) if g.ndim == 1 or g.shape[0] == 1 else g.reshape(-1, shards, unit).transpose(1, 0, 2)
+    packed = pack_small([rows_of(grad_proj_shift), rows_of(sums[1:7]), rows_of(wide_sums), grad_table.reshape(shards, -1, HEADS)], shards)
     if linked:
         packed = packed.reshape(4, 2, ROWS, LANE).transpose(1, 0, 2, 3).reshape(8 * ROWS, LANE)
         sum_joined, mine = reduce_rest([grad_joined], packed)
@@ -1105,17 +1205,17 @@
         sum_joined, sum_in, sum_out, sum_proj = [scatter(a) for a in (grad_joined, grad_in_proj, grad_out_ffn, grad_out_proj)]
         mine = scatter(packed)
     sum_joined, sum_in, sum_out, sum_proj = [a.astype(F32) for a in (sum_joined, sum_in, sum_out, sum_proj)]
-    content_grad_rows = grad_sum_one[:row_count] + (
+    content_grad_rows = grad_branch[:row_count].astype(F32) + (
         times_transpose(grads[0], joined_proj[:, :width])
         + times_transpose(grads[1], joined_proj[:, width : 2 * width])
         + times_transpose(grads[2], joined_proj[:, 2 * width :])
     )
-    query_grad_rows = grad_sum_one[row_count:] + times_transpose(grads[3], joined_proj[:, :width])
+    query_grad_rows = grad_branch[row_count:].astype(F32) + times_transpose(grads[3], joined_proj[:, :width])
     vec = lambda k: mine[k, :unit]
     block_shape = (seq_count, seq_len, width)
     return (
-        final_rows[:row_count].reshape(block_shape).astype(BF16),
-        final_rows[row_count:].reshape(block_shape).astype(BF16),
+        content_out.reshape(block_shape),
+        query_out.reshape(block_shape),
         content_grad_rows.reshape(block_shape).astype(BF16),
         query_grad_rows.reshape(block_shape).astype(BF16),
         sum_joined,

time: 430 us -> 379 us (0.88)
  matrix products: 151 us -> 50.7 us
  Pallas kernels: 205 us -> 295 us
  other arithmetic: 49 us -> 17.4 us
  local copies, waits for them, and re-layouts: 15.7 us -> 8.93 us
    pallas_call x0 -> x1, Pallas kernels: none -> 89.6 us  [ffn_stage(): pl.pallas_call(functools.partial(ffn_kernel, chunk), grid=(n,), in_specs=...]
    dot_general x7 -> x4, matrix products: 63.1 us -> 10.6 us  [times_transpose(): lax.dot_general(left_op, right_op, (((1,), (1,)), ((), ())), preferred_el...]
    dot_general x3 -> x0, matrix products: 41.5 us -> none  [the longest x1 22 us: on_device(): jnp.dot(first_low, in_proj, preferred_element_type=F32) + in_shift]
    reduce_sum x5 -> x0, other arithmetic: 22.6 us -> none  [the longest x1 7.96 us: on_device(): grad_ffn_shift = jnp.sum(grad_ffn.astype(F32), 0)]
    dot_general x7, matrix products: 44.8 us -> 39.3 us  [rows_inner(): lax.dot_general(left_op, right_op, (((0,), (0,)), ((), ())), preferred_el...]
    unnamed x65 -> x58, local copies, waits for them, and re-layouts: 5.03 us -> 0.66 us
where the time goes in v3:
time: 379 us; the launch traced here: 373 us
  Pallas kernels  295 us (78%)
  matrix products  50.7 us (13%)
  other arithmetic  17.4 us (5%)
  local copies, waits for them, and re-layouts  8.93 us (2%)
    pallas_call x1, Pallas kernels, ffn_stage(): pl.pallas_call(functools.partial(ffn_kernel, chunk), grid=(n,), in_specs=...  89.6 us
    pallas_call x1, Pallas kernels, backward_attention(): pl.pallas_call(functools.partial(backward_kernel, shapes, linked), grid=(...  86.4 us
    pallas_call x1, Pallas kernels, forward_attention(): pl.pallas_call(functools.partial(forward_kernel, shapes, linked), grid=(p...  81.6 us
    dot_general x7, matrix products, rows_inner(): lax.dot_general(left_op, right_op, (((0,), (0,)), ((), ())), preferred_el...  39.3 us
    pallas_call x1, Pallas kernels, reduce_rest(): pl.pallas_call(functools.partial(reduce_kernel, shapes, n), out_shape=[ja...  36.9 us
    dot_general x4, matrix products, times_transpose(): lax.dot_general(left_op, right_op, (((1,), (1,)), ((), ())), preferred_el...  10.6 us

profile of v3, /device:TPU:0, one launch (start us, length us, event | category | flops | bytes accessed | tf_op | source)
XLA Modules:
  0.0 373.0 jit_solution(9837801433261426903)
XLA Ops:
  0.8 2.2 convert_element_type.81.refs_2_
  3.0 2.1 convert_element_type.82.refs_3_
  5.1 0.8 convert_element_type.79.refs_0_
  6.0 0.7 convert_element_type.80.refs_1_
  6.6 0.1 reshape.127
  6.8 0.1 reshape.120
  7.1 1.2 concatenate.17
  8.3 81.6 %attention_forward.1 = (bf16[768,768]{1,0:T(8,128)(2,1)}, bf16[768,3072]{1,0:T(8,128)(2,1)}, bf16[3072,768]{1,0:T(8,128)(2,1)}, bf16[768,2304]{1,0:T(8,128)(2,1)...) custom-call(s32[2]{0:T(128)} %len_ref.5, ...), custom_call_target="tpu_custom_call" | custom-call | flops 8053063680 | bytes 31457280 | tf_op jit(solution)/shard_map/attention_forward/pallas_call | solution.py:674
  89.9 89.6 %ffn_stage.1 = (bf16[1024,768]{1,0:T(8,128)(2,1)}, bf16[1024,768]{1,0:T(8,128)(2,1)}, bf16[2048,3072]{1,0:T(8,128)(2,1)}, bf16[2048,3072]{1,0:T(8,128)(2,1)}, bf...) custom-call(s32[2]{0:T(128)} %len_ref.5, ...), custom_call_target="tpu_custom_call" | custom-call | flops 43486543872 | bytes 62914560 | tf_op jit(solution)/shard_map/ffn_stage/pallas_call | solution.py:1118
  179.6 15.8 %convolution_convert_fusion.refs_1_ = bf16[3072,768]{1,0:T(8,128)(2,1)} fusion(bf16[2048,3072]{1,0:T(8,128)(2,1)} %get-tuple-element.55, bf16[2048,768]{1,0:T(8,128)(2,1)} %get-tuple-element.56), kind=kOutput, calls=%fused_computation.1 | convolution fusion | flops 9666035712 | bytes 20447232 | tf_op jit(solution)/shard_map/dot_general | solution.py:1143
  195.4 11.9 %convolution_convert_fusion.1.refs_0_ = bf16[768,3072]{1,0:T(8,128)(2,1)} fusion(bf16[2048,768]{1,0:T(8,128)(2,1)S(1)} %copy-done.24, bf16[2048,3072]{1,0:T(8,128)(2,1)S(1)} %copy-done.23), kind=kOutput, calls=%fused_computation.2 | convolution fusion | flops 9666035712 | bytes 20447232 | tf_op jit(solution)/shard_map/dot_general | solution.py:1143
  207.3 3.7 convolution_convert_fusion.2.refs_2_
  211.0 86.4 %attention_backward.1 = (bf16[96,3072]{1,0:T(8,128)(2,1)}, bf16[384,768]{1,0:T(8,128)(2,1)}, bf16[96,768]{1,0:T(8,128)(2,1)}, bf16[4,1024,768]{2,1,0:T(8,128)(2,1)}, f32[12,768]{1,0:T(8,128)}) custom-call(s32[2]{0:T(128)} %len_ref.5, bf16[1024,3072]{1,0:T(8,128)(2,1)} %get-tuple-element.50.q_ref.k_ref.v_ref.g_ref, ...), custom_call_target="tpu_custom_call" | custom-call | flops 16106127360 | bytes 31457280 | tf_op jit(solution)/shard_map/attention_backward/pallas_call | solution.py:878
  297.4 0.0 copy-start.6
  297.4 0.0 copy-start.10
  297.4 0.0 copy-start.11
  297.5 3.7 convert_reduce_fusion
  301.2 0.1 add.58
  301.2 0.1 concatenate.19
  301.3 0.0 slice-start
  301.4 0.8 fusion.46
  302.1 0.1 reshape.133
  302.2 0.5 broadcast.49
  302.7 0.7 reduce.7
  303.4 0.1 reshape.134
  303.5 0.6 copy.51
  304.2 3.5 fusion
  307.7 0.1 copy-done.14
  307.8 1.5 fusion.28
  309.3 1.5 fusion.22
  310.8 1.5 fusion.25
  312.2 2.2 pad_maximum_fusion.refs_0_
  314.4 36.9 %reduce_rest.1 = (bf16[96,2304]{1,0:T(8,128)(2,1)}, f32[16,128]{1,0:T(8,128)}) custom-call(bf16[768,2304]{1,0:T(8,128)(2,1)} %pad_maximum_fusion.refs_0_, f32[128,128]{1,0:T(8,128)} %bitcast.99), custom_call_target="tpu_custom_call" | custom-call | tf_op jit(solution)/shard_map/reduce_rest/pallas_call | solution.py:979
  351.4 2.0 convert_element_type.94
  353.3 0.7 slice.89
  354.0 0.7 reshape.138
  354.7 1.4 slice_bitcast_fusion
  356.1 0.7 slice.84
  356.8 0.6 reshape.137
  357.4 1.3 slice.88
  358.7 5.0 %add_convert_fusion = bf16[1024,768]{1,0:T(8,128)(2,1)} fusion(bf16[2048,768]{1,0:T(8,128)(2,1)} %get-tuple-element.49, bf16[4,1024,768]{2,1,0:T(8,128)(2,1)} %get-tuple-element.57, bf16[768,2304]{1,0:T(8,128)(2,1)} %get-tuple-element.58), kind=kOutput, calls=%fused_computation.4 | convolution fusion | flops 1210318848 | bytes 5898240 | tf_op jit(solution)/shard_map/dot_general | solution.py:1149
  363.7 1.4 fusion.8
  365.1 1.4 fusion.12
  366.5 0.4 copy-done.2
  367.0 2.8 add_convert_fusion.1
  369.8 1.1 convert_element_type.96
  370.9 1.1 convert_element_type.97
  372.0 0.7 convert_element_type.95
  (77 shorter events, 0.3 us)
Async XLA Ops:
  0.7 4.5 %copy-start = (f32[96,2304]{1,0:T(8,128)S(1)}, f32[96,2304]{1,0:T(8,128)}, u32[]{:S(2)}) copy-start(f32[96,2304]{1,0:T(8,128)} %param.26) | copy-start | bytes 2654212
  0.7 5.3 %copy-start.7 = (f32[96,768]{1,0:T(8,128)S(1)}, f32[96,768]{1,0:T(8,128)}, u32[]{:S(2)}) copy-start(f32[96,768]{1,0:T(8,128)} %param.28) | copy-start | bytes 884740
  0.7 6.0 %copy-start.12 = (f32[384]{0:T(512)S(1)}, f32[384]{0:T(512)}, u32[]{:S(2)}) copy-start(f32[384]{0:T(512)} %param.34) | copy-start | bytes 4612
  0.7 6.1 %copy-start.13 = (f32[4,12]{1,0:T(4,128)S(1)}, f32[4,12]{1,0:T(4,128)}, u32[]{:S(2)}) copy-start(f32[4,12]{1,0:T(4,128)} %param.32) | copy-start | bytes 580
  0.7 6.1 %copy-start.15 = (f32[192]{0:T(256)S(1)}, f32[192]{0:T(256)}, u32[]{:S(2)}) copy-start(f32[192]{0:T(256)} %param.27) | copy-start | bytes 2308
  0.7 6.2 %copy-start.16 = (f32[96]{0:T(128)S(1)}, f32[96]{0:T(128)}, u32[]{:S(2)}) copy-start(f32[96]{0:T(128)} %param.29) | copy-start | bytes 1156
  0.7 6.2 %copy-start.17 = (f32[96]{0:T(128)S(1)}, f32[96]{0:T(128)}, u32[]{:S(2)}) copy-start(f32[96]{0:T(128)} %param.30) | copy-start | bytes 1156
  0.7 6.2 %copy-start.18 = (f32[96]{0:T(128)S(1)}, f32[96]{0:T(128)}, u32[]{:S(2)}) copy-start(f32[96]{0:T(128)} %param.31) | copy-start | bytes 1156
  0.7 6.2 %copy-start.19 = (f32[96]{0:T(128)S(1)}, f32[96]{0:T(128)}, u32[]{:S(2)}) copy-start(f32[96]{0:T(128)} %param.36) | copy-start | bytes 1156
  0.7 6.3 %copy-start.20 = (f32[96]{0:T(128)S(1)}, f32[96]{0:T(128)}, u32[]{:S(2)}) copy-start(f32[96]{0:T(128)} %param.37) | copy-start | bytes 1156
  0.8 6.3 %copy-start.21 = (f32[96]{0:T(128)S(1)}, f32[96]{0:T(128)}, u32[]{:S(2)}) copy-start(f32[96]{0:T(128)} %param.38) | copy-start | bytes 1156
  179.6 15.8 %copy-start.23 = (bf16[2048,3072]{1,0:T(8,128)(2,1)S(1)}, bf16[2048,3072]{1,0:T(8,128)(2,1)}, u32[]{:S(2)}) copy-start(bf16[2048,3072]{1,0:T(8,128)(2,1)} %get-tuple-element.54) | copy-start | bytes 37748740
  179.6 15.8 %copy-start.24 = (bf16[2048,768]{1,0:T(8,128)(2,1)S(1)}, bf16[2048,768]{1,0:T(8,128)(2,1)}, u32[]{:S(2)}) copy-start(bf16[2048,768]{1,0:T(8,128)(2,1)} %get-tuple-element.53) | copy-start | bytes 9437188
  195.4 11.9 %copy-start.1 = (bf16[2048,768]{1,0:T(8,128)(2,1)S(1)}, bf16[2048,768]{1,0:T(8,128)(2,1)}, u32[]{:S(2)}) copy-start(bf16[2048,768]{1,0:T(8,128)(2,1)} %get-tuple-element.49) | copy-start | bytes 9437188
  195.4 11.9 %copy-start.22 = (bf16[2,1024,768]{2,1,0:T(8,128)(2,1)S(1)}, bf16[2,1024,768]{2,1,0:T(8,128)(2,1)}, u32[]{:S(2)}) copy-start(bf16[2,1024,768]{2,1,0:T(8,128)(2,1)} %get-tuple-element.42) | copy-start | bytes 9437188
  297.4 3.9 %copy-start.6 = (f32[768,32]{1,0:T(8,128)S(1)}, f32[768,32]{1,0:T(8,128)}, u32[]{:S(2)}) copy-start(f32[768,32]{1,0:T(8,128)} %constant.14.clone) | copy-start | bytes 294916
  297.4 3.9 %copy-start.9 = (f32[12,768]{1,0:T(8,128)S(1)}, f32[12,768]{1,0:T(8,128)}, u32[]{:S(2)}) copy-start(f32[12,768]{1,0:T(8,128)} %get-tuple-element.61) | copy-start | bytes 110596
  297.4 4.7 %copy-start.10 = (f32[8,768]{1,0:T(8,128)S(1)}, f32[8,768]{1,0:T(8,128)}, u32[]{:S(2)}) copy-start(f32[8,768]{1,0:T(8,128)} %get-tuple-element.59) | copy-start | bytes 73732
  297.4 5.3 %copy-start.11 = (f32[1,3072]{1,0:T(1,128)S(1)}, f32[1,3072]{1,0:T(1,128)}, u32[]{:S(2)}) copy-start(f32[1,3072]{1,0:T(1,128)} %get-tuple-element.60) | copy-start | bytes 36868
  301.3 6.3 %slice-start = ((s8[6291456]{0:T(1024)(128)(4,1)}), s8[2097152]{0:T(1024)(128)(4,1)S(1)}, s32[]{:S(2)}) async-start(s8[6291456]{0:T(1024)(128)(4,1)} %bitcast.94), calls=%async_computation | async-start | bytes 4194304
  304.2 3.5 slice-start.1
  304.2 3.6 copy-start.14
  314.4 49.3 %slice-start.2 = ((s8[6291456]{0:T(1024)(128)(4,1)}), s8[2097152]{0:T(1024)(128)(4,1)S(1)}, s32[]{:S(2)}) async-start(s8[6291456]{0:T(1024)(128)(4,1)} %bitcast.96), calls=%async_computation.2 | async-start | bytes 4194304
  358.7 5.0 %slice-start.3 = ((s8[6291456]{0:T(1024)(128)(4,1)}), s8[4194304]{0:T(1024)(128)(4,1)S(1)}, s32[]{:S(2)}) async-start(s8[6291456]{0:T(1024)(128)(4,1)} %bitcast.96), calls=%async_computation.3 | async-start | bytes 8388608
  358.7 5.0 %copy-start.5 = (bf16[768,2304]{1,0:T(8,128)(2,1)S(1)}, bf16[768,2304]{1,0:T(8,128)(2,1)}, u32[]{:S(2)}) copy-start(bf16[768,2304]{1,0:T(8,128)(2,1)} %get-tuple-element.58) | copy-start | bytes 10616836
  365.1 1.9 copy-start.2
  367.0 2.8 copy-start.4
  367.0 3.9 %copy-start.3 = (bf16[384,768]{1,0:T(8,128)(2,1)S(1)}, bf16[384,768]{1,0:T(8,128)(2,1)}, u32[]{:S(2)}) copy-start(bf16[384,768]{1,0:T(8,128)(2,1)} %get-tuple-element.66) | copy-start | bytes 1769476
  369.8 2.2 copy-start.8

commit v4 on v3

--- a/solution.py
+++ b/solution.py
@@ -690,8 +690,8 @@
     n = len(shapes)
     grads, refs = refs[:n], refs[n:]
     outs, refs = refs[:n], refs[n:]
-    grad_ref, sums_ref, mask_ref, acc_ref, near_ref = refs[:5]
-    refs = refs[5:]
+    grad_ref, lows_ref, sums_ref, mask_ref, acc_ref, near_ref = refs[:6]
+    refs = refs[6:]
     hp = pl.program_id(0)
     s = pl.program_id(1)
     last = pl.num_programs(1) - 1
@@ -826,13 +826,22 @@
                             acc_ref[t, :, (e + 2) * LANE : (e + 3) * LANE] = jnp.zeros((LANE, LANE), F32)
     count = seq_len // half
     scale = 1.0 / math.sqrt(HEAD)
+
+    @pl.when(s == 0)
+    def _():
+        lows_ref[...] = jnp.zeros_like(lows_ref)
+
+    def put_grad(k, value):
+        grad_ref[k] = value
+        lows_ref[k] = lows_ref[k] + fold8(value.astype(F32))
+
     for stream, ref in ((0, 0), (1, 3)):
         pieces = grad_query[stream]
         top = jnp.concatenate(pieces[:count], 1)
         bot = jnp.concatenate(pieces[count:], 1)
-        grad_ref[ref] = (jnp.concatenate([top, bot], 0) * scale).T.astype(BF16)
-    grad_ref[1] = (grad_keys * LN2).astype(BF16)
-    grad_ref[2] = grad_values.astype(BF16)
+        put_grad(ref, (jnp.concatenate([top, bot], 0) * scale).T.astype(BF16))
+    put_grad(1, (grad_keys * LN2).astype(BF16))
+    put_grad(2, grad_values.astype(BF16))
 
     @pl.when(s == last)
     def _():
@@ -885,8 +894,8 @@
             pl.BlockSpec((2, 1, seq_len, LANE), lambda h, s: (0, s, 0, 0)),
             inside, inside, inside,
         ] + [anywhere] * n,
-        out_specs=[anywhere] * n + [pl.BlockSpec((4, seq_len, LANE), lambda h, s: (0, s, h)), pl.BlockSpec(sums_shape, lambda h, s: (0, 0))],
-        out_shape=[jax.ShapeDtypeStruct(a, BF16) for a in shapes] + [jax.ShapeDtypeStruct((4, rows // 2, width), BF16), jax.ShapeDtypeStruct(sums_shape, F32)],
+        out_specs=[anywhere] * n + [pl.BlockSpec((4, seq_len, LANE), lambda h, s: (0, s, h)), pl.BlockSpec((4, 8, LANE), lambda h, s: (0, 0, h)), pl.BlockSpec(sums_shape, lambda h, s: (0, 0))],
+        out_shape=[jax.ShapeDtypeStruct(a, BF16) for a in shapes] + [jax.ShapeDtypeStruct((4, rows // 2, width), BF16), jax.ShapeDtypeStruct((4, 8, width), F32), jax.ShapeDtypeStruct(sums_shape, F32)],
         scratch_shapes=scratch,
         cost_estimate=pl.CostEstimate(flops=20 * rows * seq_len * width, bytes_accessed=30 * 2**20, transcendentals=2 * rows * seq_len * HEADS),
         compiler_params=pltpu.CompilerParams(
@@ -894,13 +903,13 @@
             **(dict(collective_id=1, has_side_effects=True) if linked else {})),
         name="attention_backward",
     )(lengths, proj, proj, proj, proj, grad_mixed, grad_mixed, mixed, mixed, totals, order, small, onehot, *weight_grads)
-    sums = outs[n + 1]
+    sums = outs[n + 2]
     fold = np.zeros((sums_shape[1], BUCKETS), np.float32)
     fold[:NEAR] = np.roll(near_onehot(1).T, LANE - 1, 0)
     fold[NEAR : NEAR + LANE, BUCKETS - 1] = 1
     fold[NEAR + LANE :, BUCKETS // 2 - 1] = 1
     grad_table = jnp.dot(sums, jnp.asarray(fold), precision=lax.Precision.HIGHEST).T
-    return outs[:n], outs[n], grad_table
+    return outs[:n], outs[n], jnp.sum(outs[n + 1], 1), grad_table
 
 
 def small_reduce(net, w, part, out, bufs):
@@ -946,45 +955,117 @@
     return first, second, third, fourth, fifth
 
 
+def input_grads(rows, grads, joined, branch):
+    width = branch.shape[1]
+    total = grads.shape[1]
+    low = pl.ds(pl.multiple_of(total + rows.start, 256), rows.size)
+    content = branch[rows, :].astype(F32)
+    for k in range(3):
+        content = content + nt(grads[k, rows, :], joined[:, k * width : (k + 1) * width])
+    query = branch[low, :].astype(F32) + nt(grads[3, rows, :], joined[:, :width])
+    return content.astype(BF16), query.astype(BF16)
+
+
 def reduce_kernel(shapes, n, *refs):
-    grads, small_part, refs = refs[:n], refs[n], refs[n + 1 :]
-    outs, small_out, refs = refs[:n], refs[n], refs[n + 1 :]
+    grads, small_part, sources, refs = refs[:n], refs[n], refs[n + 1 : n + 4], refs[n + 4 :]
+    outs, small_out, stream_outs, refs = refs[:n], refs[n], refs[n + 1 : n + 3], refs[n + 3 :]
+    held, results, own_sem, refs = refs[:3], refs[3:5], refs[5], refs[6:]
     bufs = [refs[7 * w : 7 * w + 7] for w in range(n)]
     small_bufs, (send, recv) = refs[7 * n : 7 * n + 5], refs[7 * n + 5 :]
     net = Reduce(shapes, grads, outs, bufs, send, recv)
     first, second, third, fourth, fifth = small_reduce(net, n, small_part, small_out, small_bufs)
+    fetch = [pltpu.make_async_copy(a, b, own_sem.at[k]) for k, (a, b) in enumerate(zip(sources, held))]
+    store = [pltpu.make_async_copy(a, b, own_sem.at[3 + k]) for k, (a, b) in enumerate(zip(results, stream_outs))]
     net.barrier()
     items, ticks = plan(net, n, list(range(n)))
     first()
     for w, k in items:
         net.start(w, k)
+    for d in fetch:
+        d.start()
+    for d in fetch:
+        d.wait()
+    pieces = 4
+    chunk = results[0].shape[0] // pieces
     extra = {1: second, 4: third, 6: fourth}
     for i, acts in enumerate(ticks):
         for act in acts:
             act()
         if i in extra:
             extra[i]()
+        if 3 <= i < 3 + pieces:
+            rows = pl.ds((i - 3) * chunk, chunk)
+            content, query = input_grads(rows, *held)
+            results[0][rows, :] = content
+            results[1][rows, :] = query
+        if i == 2 + pieces:
+            for d in store:
+                d.start()
     fifth()
-
-
-def reduce_rest(weight_grads, small_grads):
+    for d in store:
+        d.wait()
+
+
+def reduce_rest(weight_grads, small_grads, grads, joined, branch):
     n = len(weight_grads)
     shapes = [(g.shape[0] // 8, g.shape[1]) for g in weight_grads]
     anywhere = pl.BlockSpec(memory_space=pl.ANY)
     inside = pl.BlockSpec(memory_space=pltpu.VMEM)
     rows = 4 * ROWS
-    scratch = Reduce.scratch(shapes)
+    stream = grads.shape[1:]
+    scratch = [pltpu.VMEM(a.shape, BF16) for a in (grads, joined, branch)] + [pltpu.VMEM(stream, BF16)] * 2 + [pltpu.SemaphoreType.DMA((5,))]
+    scratch += Reduce.scratch(shapes)
     scratch += [pltpu.VMEM((4, rows, LANE), F32)] + [pltpu.VMEM((rows, LANE), F32)] * 3 + [pltpu.VMEM((3, ROWS, LANE), F32)]
     scratch += [pltpu.SemaphoreType.DMA((n + 1, 4, Reduce.SLOTS)), pltpu.SemaphoreType.DMA((n + 1, 4, Reduce.SLOTS))]
     return pl.pallas_call(
         functools.partial(reduce_kernel, shapes, n),
-        out_shape=[jax.ShapeDtypeStruct(a, BF16) for a in shapes] + [jax.ShapeDtypeStruct((ROWS, LANE), F32)],
-        in_specs=[anywhere] * (n + 1),
-        out_specs=[anywhere] * n + [inside],
+        out_shape=[jax.ShapeDtypeStruct(a, BF16) for a in shapes] + [jax.ShapeDtypeStruct((ROWS, LANE), F32)] + [jax.ShapeDtypeStruct(stream, BF16)] * 2,
+        in_specs=[anywhere] * (n + 4),
+        out_specs=[anywhere] * n + [inside] + [anywhere] * 2,
         scratch_shapes=scratch,
         compiler_params=pltpu.CompilerParams(collective_id=2, has_side_effects=True, vmem_limit_bytes=VMEM_BYTES),
         name="reduce_rest",
-    )(*weight_grads, small_grads)
+    )(*weight_grads, small_grads, grads, joined, branch)
+
+
+def prepare_kernel(unit, places, *refs):
+    count = len(places)
+    vectors, table, weights, refs = refs[:count], refs[count], refs[count + 1 : count + 5], refs[count + 5 :]
+    small_ref, outs, wide_ref, part_ref = refs[0], refs[1:5], refs[5], refs[6]
+    part_ref[...] = jnp.zeros_like(part_ref)
+    lane = lax.broadcasted_iota(jnp.int32, (8, LANE), 1)
+    for (row, chunks), ref in zip(places, vectors):
+        if chunks == 1:
+            part_ref[row : row + 1, :unit] = ref[...][None, :]
+            continue
+        size = chunks * unit
+        wide = wide_ref.shape[1]
+        wide_ref[0:1, :size] = ref[...][None, :]
+        value = jnp.broadcast_to(wide_ref[0:1, :], (8, wide))
+        for k in range(chunks):
+            turned = pltpu.roll(value, wide - k * unit, 1) if k else value
+            part_ref[row + k : row + k + 1, :] = jnp.where(lane < unit, turned[:, :LANE], 0.0)[0:1]
+    part_ref[TABLE_ROW : TABLE_ROW + table.shape[0], : table.shape[1]] = table[...]
+    small_ref[...] = part_ref[...].astype(BF16)
+    for a, b in zip(weights, outs):
+        b[...] = a[...].astype(BF16)
+
+
+def prepare(vectors, table, weights, unit):
+    places, row = [], 0
+    for v in vectors:
+        places.append((row, v.shape[0] // unit))
+        row += v.shape[0] // unit
+    widest = max(v.shape[0] for v in vectors)
+    widest = (widest + LANE - 1) // LANE * LANE
+    outs = pl.pallas_call(
+        functools.partial(prepare_kernel, unit, places),
+        out_shape=[jax.ShapeDtypeStruct((ROWS, LANE), BF16)] + [jax.ShapeDtypeStruct(w.shape, BF16) for w in weights],
+        scratch_shapes=[pltpu.VMEM((8, widest), F32), pltpu.VMEM((ROWS, LANE), F32)],
+        compiler_params=pltpu.CompilerParams(vmem_limit_bytes=VMEM_BYTES),
+        name="prepare",
+    )(*vectors, table, *weights)
+    return outs[0], outs[1:]
 
 
 ERF_P = 0.3275911 * 0.7071067811865476
@@ -1104,7 +1185,7 @@
         wide_sums_ref[...] = jnp.sum(wide_acc_ref[...], 0, keepdims=True)
 
 
-def ffn_stage(mixed, content_rows, query_rows, content_cot, query_cot, lengths, small, out_proj, in_proj, out_ffn, rows=256, chunk=768):
+def ffn_stage(mixed, content_rows, query_rows, content_cot, query_cot, lengths, small, out_proj, in_proj, out_ffn, rows=512, chunk=768):
     total, width = mixed.shape
     hidden = in_proj.shape[1]
     n = total // rows
@@ -1169,8 +1250,12 @@
     row_count = seq_count * seq_len
     unit = width // shards
     small_args = (qv_bias, out_bias, norm1_gain, norm1_bias, ffn_out_bias, norm2_gain, norm2_bias, ffn_in_bias)
-    small = pack_small([p.reshape(1, -1, unit) for p in small_args] + [rel_table[None]], 1).astype(BF16)
-    weights = [w.astype(BF16) for w in (qkv_weight, out_weight, ffn_in_weight, ffn_out_weight)]
+    weights = (qkv_weight, out_weight, ffn_in_weight, ffn_out_weight)
+    if linked:
+        small, weights = prepare(small_args, rel_table, weights, unit)
+    else:
+        small = pack_small([p.reshape(1, -1, unit) for p in small_args] + [rel_table[None]], 1).astype(BF16)
+        weights = [w.astype(BF16) for w in weights]
     content_rows = content_stream.reshape(row_count, width)
     query_rows = query_stream.reshape(row_count, width)
     if linked:
@@ -1189,28 +1274,27 @@
     grad_in_proj = rows_inner(first_low, grad_hidden).astype(BF16)
     grad_out_proj = rows_inner(mixed_rows, grad_branch).astype(BF16)
     ready = [grad_in_proj, grad_out_ffn, grad_out_proj] if linked else []
-    early, grads, grad_table = backward_attention(linked, proj, grad_mixed, mixed_rows, totals, lengths, factor_order, small, ready)
+    early, grads, low_sums, grad_table = backward_attention(linked, proj, grad_mixed, mixed_rows, totals, lengths, factor_order, small, ready)
     grad_q = rows_inner(content_rows, grads[0]) + rows_inner(query_rows, grads[3])
     grad_joined = jnp.concatenate([grad_q, rows_inner(content_rows, grads[1]), rows_inner(content_rows, grads[2])], 1).astype(BF16)
-    low_sums = jnp.sum(grads.astype(F32), 1)
     grad_proj_shift = jnp.concatenate([low_sums[0] + low_sums[3], low_sums[2]])
     rows_of = lambda g: g.reshape(shards, -1, unit) if g.ndim == 1 or g.shape[0] == 1 else g.reshape(-1, shards, unit).transpose(1, 0, 2)
     packed = pack_small([rows_of(grad_proj_shift), rows_of(sums[1:7]), rows_of(wide_sums), grad_table.reshape(shards, -1, HEADS)], shards)
     if linked:
         packed = packed.reshape(4, 2, ROWS, LANE).transpose(1, 0, 2, 3).reshape(8 * ROWS, LANE)
-        sum_joined, mine = reduce_rest([grad_joined], packed)
+        sum_joined, mine, content_grad_rows, query_grad_rows = reduce_rest([grad_joined], packed, grads, joined_proj, grad_branch)
         sum_in, sum_out, sum_proj = early
     else:
         scatter = lambda a: lax.psum(lax.psum_scatter(a, "fsdp", scatter_dimension=0, tiled=True), "rep")
         sum_joined, sum_in, sum_out, sum_proj = [scatter(a) for a in (grad_joined, grad_in_proj, grad_out_ffn, grad_out_proj)]
         mine = scatter(packed)
+        content_grad_rows = grad_branch[:row_count].astype(F32) + (
+            times_transpose(grads[0], joined_proj[:, :width])
+            + times_transpose(grads[1], joined_proj[:, width : 2 * width])
+            + times_transpose(grads[2], joined_proj[:, 2 * width :])
+        )
+        query_grad_rows = grad_branch[row_count:].astype(F32) + times_transpose(grads[3], joined_proj[:, :width])
     sum_joined, sum_in, sum_out, sum_proj = [a.astype(F32) for a in (sum_joined, sum_in, sum_out, sum_proj)]
-    content_grad_rows = grad_branch[:row_count].astype(F32) + (
-        times_transpose(grads[0], joined_proj[:, :width])
-        + times_transpose(grads[1], joined_proj[:, width : 2 * width])
-        + times_transpose(grads[2], joined_proj[:, 2 * width :])
-    )
-    query_grad_rows = grad_branch[row_count:].astype(F32) + times_transpose(grads[3], joined_proj[:, :width])
     vec = lambda k: mine[k, :unit]
     block_shape = (seq_count, seq_len, width)
     return (

time: 379 us -> 375 us (0.989)
  Pallas kernels: 295 us -> 308 us
  matrix products: 50.7 us -> 42 us
  other arithmetic: 17.4 us -> 8.92 us
    dot_general x4 -> x0, matrix products: 10.6 us -> none  [times_transpose(): lax.dot_general(left_op, right_op, (((1,), (1,)), ((), ())), preferred_el...]
    pallas_call x1, Pallas kernels: 89.6 us -> 98.1 us  [ffn_stage(): pl.pallas_call(functools.partial(ffn_kernel, chunk), grid=(n,), in_specs=...]
    convert_element_type x4 -> x0, other arithmetic: 5.86 us -> none  [on_device(): w.astype(BF16)]
where the time goes in v4:
time: 375 us; the launch traced here: 369 us
  Pallas kernels  308 us (82%)
  matrix products  42 us (11%)
  local copies, waits for them, and re-layouts  9.25 us (2%)
  other arithmetic  8.92 us (2%)
    pallas_call x1, Pallas kernels, ffn_stage(): pl.pallas_call(functools.partial(ffn_kernel, chunk), grid=(n,), in_specs=...  98.1 us
    pallas_call x1, Pallas kernels, backward_attention(): pl.pallas_call(functools.partial(backward_kernel, shapes, linked), grid=(...  87.3 us
    pallas_call x1, Pallas kernels, forward_attention(): pl.pallas_call(functools.partial(forward_kernel, shapes, linked), grid=(p...  81.7 us
    dot_general x7, matrix products, rows_inner(): lax.dot_general(left_op, right_op, (((0,), (0,)), ((), ())), preferred_el...  40.3 us
    pallas_call x1, Pallas kernels, reduce_rest(): pl.pallas_call(functools.partial(reduce_kernel, shapes, n), out_shape=[ja...  37.4 us

profile of v4, /device:TPU:0, one launch (start us, length us, event | category | flops | bytes accessed | tf_op | source)
XLA Modules:
  0.0 369.3 jit_solution(1083594322946169686)
XLA Ops:
  0.7 3.4 prepare.1
  4.0 81.7 %attention_forward.1 = (bf16[768,768]{1,0:T(8,128)(2,1)}, bf16[768,3072]{1,0:T(8,128)(2,1)}, bf16[3072,768]{1,0:T(8,128)(2,1)}, bf16[768,2304]{1,0:T(8,128)(2,1)...) custom-call(s32[2]{0:T(128)} %len_ref.5, ...), custom_call_target="tpu_custom_call" | custom-call | flops 8053063680 | bytes 31457280 | tf_op jit(solution)/shard_map/attention_forward/pallas_call | solution.py:674
  85.7 0.0 copy-start.9
  85.7 98.1 %ffn_stage.1 = (bf16[1024,768]{1,0:T(8,128)(2,1)}, bf16[1024,768]{1,0:T(8,128)(2,1)}, bf16[2048,3072]{1,0:T(8,128)(2,1)}, bf16[2048,3072]{1,0:T(8,128)(2,1)}, bf...) custom-call(s32[2]{0:T(128)} %len_ref.5, ...), custom_call_target="tpu_custom_call" | custom-call | flops 43486543872 | bytes 62914560 | tf_op jit(solution)/shard_map/ffn_stage/pallas_call | solution.py:1199
  183.8 0.0 copy-done.9
  183.9 0.0 copy-start.11
  183.9 0.0 slice-start.2
  183.9 5.7 %convolution_convert_fusion.2.refs_2_ = bf16[768,768]{1,0:T(8,128)(2,1)} fusion(bf16[2048,768]{1,0:T(8,128)(2,1)S(1)} %bitcast.92, bf16[2048,768]{1,0:T(8,128)(2,1)} %get-tuple-element.69.refs_4_), kind=kOutput, calls=%fused_computation.18 | convolution fusion | flops 2416508928 | bytes 7471104 | tf_op jit(solution)/shard_map/dot_general | solution.py:1224
  189.6 0.0 copy-done.11
  189.6 14.7 %convolution_convert_fusion.refs_1_ = bf16[3072,768]{1,0:T(8,128)(2,1)} fusion(bf16[2048,3072]{1,0:T(8,128)(2,1)} %get-tuple-element.67, bf16[2048,768]{1,0:T(8,128)(2,1)S(1)} %copy-done.11), kind=kOutput, calls=%fused_computation | convolution fusion | flops 9666035712 | bytes 20447232 | tf_op jit(solution)/shard_map/dot_general | solution.py:1224
  204.3 0.0 slice-done.2
  204.3 0.0 slice-done.3
  204.3 0.0 slice-done.4
  204.3 0.0 copy-done.10
  204.3 11.9 %convolution_convert_fusion.1.refs_0_ = bf16[768,3072]{1,0:T(8,128)(2,1)} fusion(bf16[2048,768]{1,0:T(8,128)(2,1)S(1)} %copy-done.10, bf16[2048,3072]{1,0:T(8,128)(2,1)S(1)} %bitcast.96), kind=kOutput, calls=%fused_computation.1 | convolution fusion | flops 9666035712 | bytes 20447232 | tf_op jit(solution)/shard_map/dot_general | solution.py:1224
  216.3 87.3 %attention_backward.1 = (bf16[96,3072]{1,0:T(8,128)(2,1)}, bf16[384,768]{1,0:T(8,128)(2,1)}, bf16[96,768]{1,0:T(8,128)(2,1)}, bf16[4,1024,768]{2,1,0:T(8,128)(2,...) custom-call(s32[2]{0:T(128)} %len_ref.5, bf16[1024,3072]{1,0:T(8,128)(2,1)} %get-tuple-element.62.q_ref.k_ref.v_ref.g_ref, ...), custom_call_target="tpu_custom_call" | custom-call | flops 16106127360 | bytes 31457280 | tf_op jit(solution)/shard_map/attention_backward/pallas_call | solution.py:887
  303.6 0.9 reduce_sum.9
  304.6 0.1 add.24
  304.6 0.1 concatenate.14
  304.7 0.0 slice-start
  304.8 1.7 fusion.32
  306.5 0.1 reshape.93
  306.6 0.5 broadcast.31
  307.1 0.0 copy-done.7
  307.1 0.7 reduce.7
  307.8 0.1 reshape.94
  307.9 0.6 copy.51
  308.5 3.5 fusion.4
  312.0 0.1 copy-done.8
  312.1 1.5 fusion.26
  313.7 1.5 fusion.20
  315.1 1.5 fusion.23
  316.6 2.2 pad_maximum_fusion.refs_0_
  318.8 37.4 %reduce_rest.1 = (bf16[96,2304]{1,0:T(8,128)(2,1)}, f32[16,128]{1,0:T(8,128)}, bf16[1024,768]{1,0:T(8,128)(2,1)}, bf16[1024,768]{1,0:T(8,128)(2,1)}) custom-call(bf16[768,2304]{1,0:T(8,128)(2,1)} %pad_maximum_fusion.refs_0_, f32[128,128]{1,0:T(8,128)} %bitcast.75, bf16[4,1024,768]{2,1,0:T(8,128)(2,1)} %get-tuple-element.70.refs_2_, ...), custom_call_target="tpu_custom_call" | custom-call | tf_op jit(solution)/shard_map/reduce_rest/pallas_call | solution.py:1020
  356.2 2.1 convert_element_type.33
  358.3 0.7 slice.64
  359.0 0.7 reshape.100
  359.7 1.4 slice_bitcast_fusion
  361.1 0.7 slice.59
  361.8 0.6 reshape.99
  362.4 1.3 slice.63
  363.7 0.0 copy-done.3
  363.7 1.1 convert_element_type.35
  364.8 1.1 convert_element_type.36
  365.9 0.7 convert_element_type.34
  366.6 0.0 copy-done.1
  366.6 1.1 copy.61
  367.8 1.1 copy.62
  (27 shorter events, 0.1 us)
Async XLA Ops:
  85.7 98.2 %copy-start.9 = (bf16[2,1024,768]{2,1,0:T(8,128)(2,1)S(1)}, bf16[2,1024,768]{2,1,0:T(8,128)(2,1)}, u32[]{:S(2)}) copy-start(bf16[2,1024,768]{2,1,0:T(8,128)(2,1)} %get-tuple-element.55) | copy-start | bytes 9437188
  183.9 5.7 %copy-start.11 = (bf16[2048,768]{1,0:T(8,128)(2,1)S(1)}, bf16[2048,768]{1,0:T(8,128)(2,1)}, u32[]{:S(2)}) copy-start(bf16[2048,768]{1,0:T(8,128)(2,1)} %get-tuple-element.68) | copy-start | bytes 9437188
  183.9 20.4 %slice-start.2 = ((s8[12582912]{0:T(1024)(128)(4,1)}), s8[4194304]{0:T(1024)(128)(4,1)S(1)}, s32[]{:S(2)}) async-start(s8[12582912]{0:T(1024)(128)(4,1)} %bitcast.95), calls=%async_computation.2 | async-start | bytes 8388608
  189.6 14.7 %slice-start.3 = ((s8[12582912]{0:T(1024)(128)(4,1)}), s8[4194304]{0:T(1024)(128)(4,1)S(1)}, s32[]{:S(2)}) async-start(s8[12582912]{0:T(1024)(128)(4,1)} %bitcast.95), calls=%async_computation.3 | async-start | bytes 8388608
  189.6 14.7 %slice-start.4 = ((s8[12582912]{0:T(1024)(128)(4,1)}), s8[4194304]{0:T(1024)(128)(4,1)S(1)}, s32[]{:S(2)}) async-start(s8[12582912]{0:T(1024)(128)(4,1)} %bitcast.95), calls=%async_computation.4 | async-start | bytes 8388608
  189.6 14.7 %copy-start.10 = (bf16[2048,768]{1,0:T(8,128)(2,1)S(1)}, bf16[2048,768]{1,0:T(8,128)(2,1)}, u32[]{:S(2)}) copy-start(bf16[2048,768]{1,0:T(8,128)(2,1)} %get-tuple-element.65) | copy-start | bytes 9437188
  216.2 88.5 %copy-start.4 = (f32[768,32]{1,0:T(8,128)S(1)}, f32[768,32]{1,0:T(8,128)}, u32[]{:S(2)}) copy-start(f32[768,32]{1,0:T(8,128)} %constant.12.clone) | copy-start | bytes 294916
  216.3 90.2 %copy-start.6 = (f32[8,768]{1,0:T(8,128)S(1)}, f32[8,768]{1,0:T(8,128)}, u32[]{:S(2)}) copy-start(f32[8,768]{1,0:T(8,128)} %get-tuple-element.72) | copy-start | bytes 73732
  216.3 90.8 %copy-start.7 = (f32[1,3072]{1,0:T(1,128)S(1)}, f32[1,3072]{1,0:T(1,128)}, u32[]{:S(2)}) copy-start(f32[1,3072]{1,0:T(1,128)} %get-tuple-element.73) | copy-start | bytes 36868
  304.7 7.3 %slice-start = ((s8[6291456]{0:T(1024)(128)(4,1)}), s8[2097152]{0:T(1024)(128)(4,1)S(1)}, s32[]{:S(2)}) async-start(s8[6291456]{0:T(1024)(128)(4,1)} %bitcast.71), calls=%async_computation | async-start | bytes 4194304
  308.5 3.5 slice-start.1
  308.5 3.6 copy-start.8
  318.8 44.9 %copy-start.3 = (bf16[96,3072]{1,0:T(8,128)(2,1)S(1)}, bf16[96,3072]{1,0:T(8,128)(2,1)}, u32[]{:S(2)}) copy-start(bf16[96,3072]{1,0:T(8,128)(2,1)} %get-tuple-element.81) | copy-start | bytes 1769476
  356.2 8.6 %copy-start.2 = (bf16[384,768]{1,0:T(8,128)(2,1)S(1)}, bf16[384,768]{1,0:T(8,128)(2,1)}, u32[]{:S(2)}) copy-start(bf16[384,768]{1,0:T(8,128)(2,1)} %get-tuple-element.82) | copy-start | bytes 1769476
  356.2 9.7 %copy-start.5 = (bf16[96,768]{1,0:T(8,128)(2,1)S(1)}, bf16[96,768]{1,0:T(8,128)(2,1)}, u32[]{:S(2)}) copy-start(bf16[96,768]{1,0:T(8,128)(2,1)} %get-tuple-element.80) | copy-start | bytes 442372
  356.2 10.4 %copy-start.1 = (bf16[1024,768]{1,0:T(8,128)(2,1)S(1)}, bf16[1024,768]{1,0:T(8,128)(2,1)}, u32[]{:S(2)}) copy-start(bf16[1024,768]{1,0:T(8,128)(2,1)} %get-tuple-element.76) | copy-start | bytes 4718596
  363.7 4.1 %copy-start = (bf16[1024,768]{1,0:T(8,128)(2,1)S(1)}, bf16[1024,768]{1,0:T(8,128)(2,1)}, u32[]{:S(2)}) copy-start(bf16[1024,768]{1,0:T(8,128)(2,1)} %get-tuple-element.77) | copy-start | bytes 4718596

commit v5 on v4

--- a/solution.py
+++ b/solution.py
@@ -1185,7 +1185,7 @@
         wide_sums_ref[...] = jnp.sum(wide_acc_ref[...], 0, keepdims=True)
 
 
-def ffn_stage(mixed, content_rows, query_rows, content_cot, query_cot, lengths, small, out_proj, in_proj, out_ffn, rows=512, chunk=768):
+def ffn_stage(mixed, content_rows, query_rows, content_cot, query_cot, lengths, small, out_proj, in_proj, out_ffn, rows=256, chunk=768):
     total, width = mixed.shape
     hidden = in_proj.shape[1]
     n = total // rows

time: 375 us -> 367 us (0.979)
  Pallas kernels: 308 us -> 300 us
    pallas_call x1, Pallas kernels: 98.1 us -> 89.6 us  [ffn_stage(): pl.pallas_call(functools.partial(ffn_kernel, chunk), grid=(n,), in_specs=...]
where the time goes in v5:
time: 367 us; the launch traced here: 361 us
  Pallas kernels  300 us (82%)
  matrix products  42.2 us (11%)
  local copies, waits for them, and re-layouts  9.25 us (3%)
  other arithmetic  8.84 us (2%)
    pallas_call x1, Pallas kernels, ffn_stage(): pl.pallas_call(functools.partial(ffn_kernel, chunk), grid=(n,), in_specs=...  89.6 us
    pallas_call x1, Pallas kernels, backward_attention(): pl.pallas_call(functools.partial(backward_kernel, shapes, linked), grid=(...  87.8 us
    pallas_call x1, Pallas kernels, forward_attention(): pl.pallas_call(functools.partial(forward_kernel, shapes, linked), grid=(p...  81.7 us
    dot_general x7, matrix products, rows_inner(): lax.dot_general(left_op, right_op, (((0,), (0,)), ((), ())), preferred_el...  40.5 us
    pallas_call x1, Pallas kernels, reduce_rest(): pl.pallas_call(functools.partial(reduce_kernel, shapes, n), out_shape=[ja...  37.2 us

profile of v5, /device:TPU:0, one launch (start us, length us, event | category | flops | bytes accessed | tf_op | source)
XLA Modules:
  0.0 361.1 jit_solution(15101036627556969321)
XLA Ops:
  0.7 3.4 prepare.1
  4.0 81.7 %attention_forward.1 = (bf16[768,768]{1,0:T(8,128)(2,1)}, bf16[768,3072]{1,0:T(8,128)(2,1)}, bf16[3072,768]{1,0:T(8,128)(2,1)}, bf16[768,2304]{1,0:T(8,128)(2,1)...) custom-call(s32[2]{0:T(128)} %len_ref.5, ...), custom_call_target="tpu_custom_call" | custom-call | flops 8053063680 | bytes 31457280 | tf_op jit(solution)/shard_map/attention_forward/pallas_call | solution.py:674
  85.7 0.0 copy-start.9
  85.7 89.6 %ffn_stage.1 = (bf16[1024,768]{1,0:T(8,128)(2,1)}, bf16[1024,768]{1,0:T(8,128)(2,1)}, bf16[2048,3072]{1,0:T(8,128)(2,1)}, bf16[2048,3072]{1,0:T(8,128)(2,1)}, bf...) custom-call(s32[2]{0:T(128)} %len_ref.5, ...), custom_call_target="tpu_custom_call" | custom-call | flops 43486543872 | bytes 62914560 | tf_op jit(solution)/shard_map/ffn_stage/pallas_call | solution.py:1199
  175.3 0.0 copy-done.9
  175.3 0.0 copy-start.11
  175.4 0.0 slice-start.2
  175.4 5.7 %convolution_convert_fusion.2.refs_2_ = bf16[768,768]{1,0:T(8,128)(2,1)} fusion(bf16[2048,768]{1,0:T(8,128)(2,1)S(1)} %bitcast.92, bf16[2048,768]{1,0:T(8,128)(2,1)} %get-tuple-element.69.refs_4_), kind=kOutput, calls=%fused_computation.18 | convolution fusion | flops 2416508928 | bytes 7471104 | tf_op jit(solution)/shard_map/dot_general | solution.py:1224
  181.1 0.0 copy-done.11
  181.1 14.9 %convolution_convert_fusion.refs_1_ = bf16[3072,768]{1,0:T(8,128)(2,1)} fusion(bf16[2048,3072]{1,0:T(8,128)(2,1)} %get-tuple-element.67, bf16[2048,768]{1,0:T(8,128)(2,1)S(1)} %copy-done.11), kind=kOutput, calls=%fused_computation | convolution fusion | flops 9666035712 | bytes 20447232 | tf_op jit(solution)/shard_map/dot_general | solution.py:1224
  196.0 0.0 slice-done.2
  196.0 0.0 slice-done.3
  196.0 0.0 slice-done.4
  196.0 0.0 copy-done.10
  196.0 11.9 %convolution_convert_fusion.1.refs_0_ = bf16[768,3072]{1,0:T(8,128)(2,1)} fusion(bf16[2048,768]{1,0:T(8,128)(2,1)S(1)} %copy-done.10, bf16[2048,3072]{1,0:T(8,128)(2,1)S(1)} %bitcast.96), kind=kOutput, calls=%fused_computation.1 | convolution fusion | flops 9666035712 | bytes 20447232 | tf_op jit(solution)/shard_map/dot_general | solution.py:1224
  208.0 87.8 %attention_backward.1 = (bf16[96,3072]{1,0:T(8,128)(2,1)}, bf16[384,768]{1,0:T(8,128)(2,1)}, bf16[96,768]{1,0:T(8,128)(2,1)}, bf16[4,1024,768]{2,1,0:T(8,128)(2,...) custom-call(s32[2]{0:T(128)} %len_ref.5, bf16[1024,3072]{1,0:T(8,128)(2,1)} %get-tuple-element.62.q_ref.k_ref.v_ref.g_ref, ...), custom_call_target="tpu_custom_call" | custom-call | flops 16106127360 | bytes 31457280 | tf_op jit(solution)/shard_map/attention_backward/pallas_call | solution.py:887
  295.8 0.9 reduce_sum.9
  296.8 0.1 add.24
  296.8 0.1 concatenate.14
  296.9 0.0 copy-done.4
  297.0 0.0 slice-start
  297.0 1.7 fusion.32
  298.7 0.1 reshape.93
  298.8 0.5 broadcast.31
  299.3 0.7 reduce.7
  300.0 0.1 reshape.94
  300.1 0.6 copy.51
  300.7 3.5 fusion.4
  304.2 0.1 copy-done.8
  304.3 1.5 fusion.26
  305.9 1.5 fusion.20
  307.3 1.5 fusion.23
  308.8 2.1 pad_maximum_fusion.refs_0_
  310.9 37.2 %reduce_rest.1 = (bf16[96,2304]{1,0:T(8,128)(2,1)}, f32[16,128]{1,0:T(8,128)}, bf16[1024,768]{1,0:T(8,128)(2,1)}, bf16[1024,768]{1,0:T(8,128)(2,1)}) custom-call(bf16[768,2304]{1,0:T(8,128)(2,1)} %pad_maximum_fusion.refs_0_, f32[128,128]{1,0:T(8,128)} %bitcast.75, bf16[4,1024,768]{2,1,0:T(8,128)(2,1)} %get-tuple-element.70.refs_2_, ...), custom_call_target="tpu_custom_call" | custom-call | tf_op jit(solution)/shard_map/reduce_rest/pallas_call | solution.py:1020
  348.2 2.1 convert_element_type.33
  350.3 0.7 slice.64
  351.0 0.7 reshape.100
  351.6 1.4 slice_bitcast_fusion
  353.1 0.7 slice.59
  353.7 0.6 reshape.99
  354.4 1.3 slice.63
  355.6 1.1 convert_element_type.35
  356.8 0.0 copy-done.2
  356.8 1.1 convert_element_type.36
  357.8 0.7 convert_element_type.34
  358.6 1.1 copy.61
  359.7 0.0 copy-done
  359.7 1.1 copy.62
  (27 shorter events, 0.1 us)
Async XLA Ops:
  85.7 89.7 %copy-start.9 = (bf16[2,1024,768]{2,1,0:T(8,128)(2,1)S(1)}, bf16[2,1024,768]{2,1,0:T(8,128)(2,1)}, u32[]{:S(2)}) copy-start(bf16[2,1024,768]{2,1,0:T(8,128)(2,1)} %get-tuple-element.55) | copy-start | bytes 9437188
  175.3 5.7 %copy-start.11 = (bf16[2048,768]{1,0:T(8,128)(2,1)S(1)}, bf16[2048,768]{1,0:T(8,128)(2,1)}, u32[]{:S(2)}) copy-start(bf16[2048,768]{1,0:T(8,128)(2,1)} %get-tuple-element.68) | copy-start | bytes 9437188
  175.4 20.6 %slice-start.2 = ((s8[12582912]{0:T(1024)(128)(4,1)}), s8[4194304]{0:T(1024)(128)(4,1)S(1)}, s32[]{:S(2)}) async-start(s8[12582912]{0:T(1024)(128)(4,1)} %bitcast.95), calls=%async_computation.2 | async-start | bytes 8388608
  181.1 14.9 %slice-start.3 = ((s8[12582912]{0:T(1024)(128)(4,1)}), s8[4194304]{0:T(1024)(128)(4,1)S(1)}, s32[]{:S(2)}) async-start(s8[12582912]{0:T(1024)(128)(4,1)} %bitcast.95), calls=%async_computation.3 | async-start | bytes 8388608
  181.1 14.9 %slice-start.4 = ((s8[12582912]{0:T(1024)(128)(4,1)}), s8[4194304]{0:T(1024)(128)(4,1)S(1)}, s32[]{:S(2)}) async-start(s8[12582912]{0:T(1024)(128)(4,1)} %bitcast.95), calls=%async_computation.4 | async-start | bytes 8388608
  181.1 14.9 %copy-start.10 = (bf16[2048,768]{1,0:T(8,128)(2,1)S(1)}, bf16[2048,768]{1,0:T(8,128)(2,1)}, u32[]{:S(2)}) copy-start(bf16[2048,768]{1,0:T(8,128)(2,1)} %get-tuple-element.65) | copy-start | bytes 9437188
  208.0 89.0 %copy-start.4 = (f32[768,32]{1,0:T(8,128)S(1)}, f32[768,32]{1,0:T(8,128)}, u32[]{:S(2)}) copy-start(f32[768,32]{1,0:T(8,128)} %constant.12.clone) | copy-start | bytes 294916
  208.0 90.7 %copy-start.6 = (f32[8,768]{1,0:T(8,128)S(1)}, f32[8,768]{1,0:T(8,128)}, u32[]{:S(2)}) copy-start(f32[8,768]{1,0:T(8,128)} %get-tuple-element.72) | copy-start | bytes 73732
  208.0 91.3 %copy-start.7 = (f32[1,3072]{1,0:T(1,128)S(1)}, f32[1,3072]{1,0:T(1,128)}, u32[]{:S(2)}) copy-start(f32[1,3072]{1,0:T(1,128)} %get-tuple-element.73) | copy-start | bytes 36868
  297.0 7.3 %slice-start = ((s8[6291456]{0:T(1024)(128)(4,1)}), s8[2097152]{0:T(1024)(128)(4,1)S(1)}, s32[]{:S(2)}) async-start(s8[6291456]{0:T(1024)(128)(4,1)} %bitcast.71), calls=%async_computation | async-start | bytes 4194304
  300.7 3.5 slice-start.1
  300.7 3.6 %copy-start.8 = (bf16[2,512,768]{2,1,0:T(8,128)(2,1)S(1)}, bf16[2,512,768]{2,1,0:T(8,128)(2,1)}, u32[]{:S(2)}) copy-start(bf16[2,512,768]{2,1,0:T(8,128)(2,1)} %param.22) | copy-start | bytes 4718596
  310.9 44.7 %copy-start.3 = (bf16[96,3072]{1,0:T(8,128)(2,1)S(1)}, bf16[96,3072]{1,0:T(8,128)(2,1)}, u32[]{:S(2)}) copy-start(bf16[96,3072]{1,0:T(8,128)(2,1)} %get-tuple-element.81) | copy-start | bytes 1769476
  348.1 8.6 %copy-start.2 = (bf16[384,768]{1,0:T(8,128)(2,1)S(1)}, bf16[384,768]{1,0:T(8,128)(2,1)}, u32[]{:S(2)}) copy-start(bf16[384,768]{1,0:T(8,128)(2,1)} %get-tuple-element.82) | copy-start | bytes 1769476
  348.1 9.7 %copy-start.5 = (bf16[96,768]{1,0:T(8,128)(2,1)S(1)}, bf16[96,768]{1,0:T(8,128)(2,1)}, u32[]{:S(2)}) copy-start(bf16[96,768]{1,0:T(8,128)(2,1)} %get-tuple-element.80) | copy-start | bytes 442372
  348.1 10.4 %copy-start.1 = (bf16[1024,768]{1,0:T(8,128)(2,1)S(1)}, bf16[1024,768]{1,0:T(8,128)(2,1)}, u32[]{:S(2)}) copy-start(bf16[1024,768]{1,0:T(8,128)(2,1)} %get-tuple-element.76) | copy-start | bytes 4718596
  355.6 4.1 %copy-start = (bf16[1024,768]{1,0:T(8,128)(2,1)S(1)}, bf16[1024,768]{1,0:T(8,128)(2,1)}, u32[]{:S(2)}) copy-start(bf16[1024,768]{1,0:T(8,128)(2,1)} %get-tuple-element.77) | copy-start | bytes 4718596

commit v6 on v5

--- a/solution.py
+++ b/solution.py
@@ -241,6 +241,15 @@
         return far, own, here, sib
 
 
+def add_tiles(into, term):
+    tile = 48 if into.shape[0] % 32 else 32
+
+    @pl.loop(0, into.shape[0] // tile)
+    def _(k):
+        rows = pl.ds(pl.multiple_of(k * tile, 16), tile)
+        into[rows, :] = into[rows, :] + term[rows, :]
+
+
 class Reduce(Links):
     SLOTS = 8
 
@@ -299,7 +308,7 @@
         self.core_copy(w, s).wait_recv()
         self.core_load(w, s).wait()
         own, got = self.bufs[w][0], self.bufs[w][1]
-        own[s] = own[s] + got[s]
+        add_tiles(own.at[s], got.at[s])
         self.first_copy(w, s).start()
 
     def second_copy(self, w, s):
@@ -315,10 +324,10 @@
         own, hx, hy = self.bufs[w][0], self.bufs[w][2], self.bufs[w][3]
         if self.x_first(s):
             at = (s, slice(None), self.half_cols(w, self.x))
-            own[at] = own[at] + hx[s // 2]
+            add_tiles(own.at[at], hx.at[s // 2])
         else:
             at = (s, self.half_rows(w, self.y), slice(None))
-            own[at] = own[at] + hy[s // 2]
+            add_tiles(own.at[at], hy.at[s // 2])
         self.second_copy(w, s).start()
 
     def far_copy(self, w, s):
@@ -330,7 +339,7 @@
         self.second_copy(w, s).wait_recv()
         own, quarter = self.bufs[w][0], self.bufs[w][4]
         at = (s, self.half_rows(w, self.y), self.half_cols(w, self.x))
-        own[at] = own[at] + quarter[s]
+        add_tiles(own.at[at], quarter.at[s])
         if s > 0:
             self.far_copy(w, s).start()
 
@@ -993,12 +1002,15 @@
             act()
         if i in extra:
             extra[i]()
-        if 3 <= i < 3 + pieces:
-            rows = pl.ds((i - 3) * chunk, chunk)
-            content, query = input_grads(rows, *held)
-            results[0][rows, :] = content
-            results[1][rows, :] = query
-        if i == 2 + pieces:
+        if i == 3:
+
+            @pl.loop(0, pieces)
+            def _(k):
+                rows = pl.ds(pl.multiple_of(k * chunk, chunk), chunk)
+                content, query = input_grads(rows, *held)
+                results[0][rows, :] = content
+                results[1][rows, :] = query
+
             for d in store:
                 d.start()
     fifth()

time: 367 us -> 367 us (level)
  no operation moved by 1% of the time
where the time goes in v6:
time: 367 us; the launch traced here: 362 us
  Pallas kernels  300 us (82%)
  matrix products  42.2 us (11%)
  local copies, waits for them, and re-layouts  9.25 us (3%)
  other arithmetic  8.69 us (2%)
    pallas_call x1, Pallas kernels, ffn_stage(): pl.pallas_call(functools.partial(ffn_kernel, chunk), grid=(n,), in_specs=...  89.6 us
    pallas_call x1, Pallas kernels, backward_attention(): pl.pallas_call(functools.partial(backward_kernel, shapes, linked), grid=(...  87.4 us
    pallas_call x1, Pallas kernels, forward_attention(): pl.pallas_call(functools.partial(forward_kernel, shapes, linked), grid=(p...  81.7 us
    dot_general x7, matrix products, rows_inner(): lax.dot_general(left_op, right_op, (((0,), (0,)), ((), ())), preferred_el...  40.5 us
    pallas_call x1, Pallas kernels, reduce_rest(): pl.pallas_call(functools.partial(reduce_kernel, shapes, n), out_shape=[ja...  38.1 us

profile of v6, /device:TPU:0, one launch (start us, length us, event | category | flops | bytes accessed | tf_op | source)
XLA Modules:
  0.0 361.6 jit_solution(8026370752229405300)
XLA Ops:
  0.7 3.4 prepare.1
  4.0 81.7 %attention_forward.1 = (bf16[768,768]{1,0:T(8,128)(2,1)}, bf16[768,3072]{1,0:T(8,128)(2,1)}, bf16[3072,768]{1,0:T(8,128)(2,1)}, bf16[768,2304]{1,0:T(8,128)(2,1)...) custom-call(s32[2]{0:T(128)} %len_ref.5, ...), custom_call_target="tpu_custom_call" | custom-call | flops 8053063680 | bytes 31457280 | tf_op jit(solution)/shard_map/attention_forward/pallas_call | solution.py:683
  85.7 0.0 copy-start.9
  85.7 89.6 %ffn_stage.1 = (bf16[1024,768]{1,0:T(8,128)(2,1)}, bf16[1024,768]{1,0:T(8,128)(2,1)}, bf16[2048,3072]{1,0:T(8,128)(2,1)}, bf16[2048,3072]{1,0:T(8,128)(2,1)}, bf...) custom-call(s32[2]{0:T(128)} %len_ref.5, ...), custom_call_target="tpu_custom_call" | custom-call | flops 43486543872 | bytes 62914560 | tf_op jit(solution)/shard_map/ffn_stage/pallas_call | solution.py:1211
  175.3 0.0 copy-done.9
  175.4 0.0 copy-start.11
  175.4 0.0 slice-start.2
  175.4 5.7 %convolution_convert_fusion.2.refs_2_ = bf16[768,768]{1,0:T(8,128)(2,1)} fusion(bf16[2048,768]{1,0:T(8,128)(2,1)S(1)} %bitcast.92, bf16[2048,768]{1,0:T(8,128)(2,1)} %get-tuple-element.69.refs_4_), kind=kOutput, calls=%fused_computation.18 | convolution fusion | flops 2416508928 | bytes 7471104 | tf_op jit(solution)/shard_map/dot_general | solution.py:1236
  181.1 0.0 copy-done.11
  181.1 14.9 %convolution_convert_fusion.refs_1_ = bf16[3072,768]{1,0:T(8,128)(2,1)} fusion(bf16[2048,3072]{1,0:T(8,128)(2,1)} %get-tuple-element.67, bf16[2048,768]{1,0:T(8,128)(2,1)S(1)} %copy-done.11), kind=kOutput, calls=%fused_computation | convolution fusion | flops 9666035712 | bytes 20447232 | tf_op jit(solution)/shard_map/dot_general | solution.py:1236
  196.0 0.0 slice-done.2
  196.0 0.0 slice-done.3
  196.0 0.0 slice-done.4
  196.0 0.0 copy-done.10
  196.0 11.9 %convolution_convert_fusion.1.refs_0_ = bf16[768,3072]{1,0:T(8,128)(2,1)} fusion(bf16[2048,768]{1,0:T(8,128)(2,1)S(1)} %copy-done.10, bf16[2048,3072]{1,0:T(8,128)(2,1)S(1)} %bitcast.96), kind=kOutput, calls=%fused_computation.1 | convolution fusion | flops 9666035712 | bytes 20447232 | tf_op jit(solution)/shard_map/dot_general | solution.py:1236
  208.0 87.4 %attention_backward.1 = (bf16[96,3072]{1,0:T(8,128)(2,1)}, bf16[384,768]{1,0:T(8,128)(2,1)}, bf16[96,768]{1,0:T(8,128)(2,1)}, bf16[4,1024,768]{2,1,0:T(8,128)(2,...) custom-call(s32[2]{0:T(128)} %len_ref.5, bf16[1024,3072]{1,0:T(8,128)(2,1)} %get-tuple-element.62.q_ref.k_ref.v_ref.g_ref, ...), custom_call_target="tpu_custom_call" | custom-call | flops 16106127360 | bytes 31457280 | tf_op jit(solution)/shard_map/attention_backward/pallas_call | solution.py:896
  295.4 0.9 reduce_sum.9
  296.4 0.1 add.24
  296.5 0.1 concatenate.14
  296.6 0.0 copy-done.4
  296.6 0.0 slice-start
  296.6 1.7 fusion.32
  298.3 0.0 copy-done.6
  298.3 0.1 reshape.93
  298.4 0.5 broadcast.31
  298.9 0.7 reduce.7
  299.6 0.1 reshape.94
  299.7 0.6 copy.51
  300.3 3.5 fusion.4
  303.9 0.1 copy-done.8
  304.0 1.5 fusion.26
  305.5 1.5 fusion.20
  306.9 1.5 fusion.23
  308.4 2.0 pad_maximum_fusion.refs_0_
  310.3 38.1 %reduce_rest.1 = (bf16[96,2304]{1,0:T(8,128)(2,1)}, f32[16,128]{1,0:T(8,128)}, bf16[1024,768]{1,0:T(8,128)(2,1)}, bf16[1024,768]{1,0:T(8,128)(2,1)}) custom-call(bf16[768,2304]{1,0:T(8,128)(2,1)} %pad_maximum_fusion.refs_0_, f32[128,128]{1,0:T(8,128)} %bitcast.75, bf16[4,1024,768]{2,1,0:T(8,128)(2,1)} %get-tuple-element.70.refs_2_, ...), custom_call_target="tpu_custom_call" | custom-call | tf_op jit(solution)/shard_map/reduce_rest/pallas_call | solution.py:1032
  348.5 2.1 convert_element_type.33
  350.6 0.7 slice.64
  351.3 0.7 reshape.100
  351.9 1.4 slice_bitcast_fusion
  353.4 0.7 slice.59
  354.1 0.6 reshape.99
  354.7 1.3 slice.63
  356.0 1.1 convert_element_type.35
  357.1 1.1 convert_element_type.36
  358.2 0.0 copy-done.5
  358.2 0.7 convert_element_type.34
  358.9 1.1 copy.61
  360.0 1.1 copy.62
  (27 shorter events, 0.1 us)
Async XLA Ops:
  85.7 89.7 %copy-start.9 = (bf16[2,1024,768]{2,1,0:T(8,128)(2,1)S(1)}, bf16[2,1024,768]{2,1,0:T(8,128)(2,1)}, u32[]{:S(2)}) copy-start(bf16[2,1024,768]{2,1,0:T(8,128)(2,1)} %get-tuple-element.55) | copy-start | bytes 9437188
  175.4 5.7 %copy-start.11 = (bf16[2048,768]{1,0:T(8,128)(2,1)S(1)}, bf16[2048,768]{1,0:T(8,128)(2,1)}, u32[]{:S(2)}) copy-start(bf16[2048,768]{1,0:T(8,128)(2,1)} %get-tuple-element.68) | copy-start | bytes 9437188
  175.4 20.6 %slice-start.2 = ((s8[12582912]{0:T(1024)(128)(4,1)}), s8[4194304]{0:T(1024)(128)(4,1)S(1)}, s32[]{:S(2)}) async-start(s8[12582912]{0:T(1024)(128)(4,1)} %bitcast.95), calls=%async_computation.2 | async-start | bytes 8388608
  181.1 14.9 %slice-start.3 = ((s8[12582912]{0:T(1024)(128)(4,1)}), s8[4194304]{0:T(1024)(128)(4,1)S(1)}, s32[]{:S(2)}) async-start(s8[12582912]{0:T(1024)(128)(4,1)} %bitcast.95), calls=%async_computation.3 | async-start | bytes 8388608
  181.1 14.9 %slice-start.4 = ((s8[12582912]{0:T(1024)(128)(4,1)}), s8[4194304]{0:T(1024)(128)(4,1)S(1)}, s32[]{:S(2)}) async-start(s8[12582912]{0:T(1024)(128)(4,1)} %bitcast.95), calls=%async_computation.4 | async-start | bytes 8388608
  181.1 14.9 %copy-start.10 = (bf16[2048,768]{1,0:T(8,128)(2,1)S(1)}, bf16[2048,768]{1,0:T(8,128)(2,1)}, u32[]{:S(2)}) copy-start(bf16[2048,768]{1,0:T(8,128)(2,1)} %get-tuple-element.65) | copy-start | bytes 9437188
  208.0 88.6 %copy-start.4 = (f32[768,32]{1,0:T(8,128)S(1)}, f32[768,32]{1,0:T(8,128)}, u32[]{:S(2)}) copy-start(f32[768,32]{1,0:T(8,128)} %constant.12.clone) | copy-start | bytes 294916
  208.0 90.3 %copy-start.6 = (f32[8,768]{1,0:T(8,128)S(1)}, f32[8,768]{1,0:T(8,128)}, u32[]{:S(2)}) copy-start(f32[8,768]{1,0:T(8,128)} %get-tuple-element.72) | copy-start | bytes 73732
  208.0 90.9 %copy-start.7 = (f32[1,3072]{1,0:T(1,128)S(1)}, f32[1,3072]{1,0:T(1,128)}, u32[]{:S(2)}) copy-start(f32[1,3072]{1,0:T(1,128)} %get-tuple-element.73) | copy-start | bytes 36868
  296.6 7.3 %slice-start = ((s8[6291456]{0:T(1024)(128)(4,1)}), s8[2097152]{0:T(1024)(128)(4,1)S(1)}, s32[]{:S(2)}) async-start(s8[6291456]{0:T(1024)(128)(4,1)} %bitcast.71), calls=%async_computation | async-start | bytes 4194304
  300.3 3.5 slice-start.1
  300.3 3.6 %copy-start.8 = (bf16[2,512,768]{2,1,0:T(8,128)(2,1)S(1)}, bf16[2,512,768]{2,1,0:T(8,128)(2,1)}, u32[]{:S(2)}) copy-start(bf16[2,512,768]{2,1,0:T(8,128)(2,1)} %param.22) | copy-start | bytes 4718596
  310.3 45.6 %copy-start.3 = (bf16[96,3072]{1,0:T(8,128)(2,1)S(1)}, bf16[96,3072]{1,0:T(8,128)(2,1)}, u32[]{:S(2)}) copy-start(bf16[96,3072]{1,0:T(8,128)(2,1)} %get-tuple-element.81) | copy-start | bytes 1769476
  348.4 8.6 %copy-start.2 = (bf16[384,768]{1,0:T(8,128)(2,1)S(1)}, bf16[384,768]{1,0:T(8,128)(2,1)}, u32[]{:S(2)}) copy-start(bf16[384,768]{1,0:T(8,128)(2,1)} %get-tuple-element.82) | copy-start | bytes 1769476
  348.5 9.7 %copy-start.5 = (bf16[96,768]{1,0:T(8,128)(2,1)S(1)}, bf16[96,768]{1,0:T(8,128)(2,1)}, u32[]{:S(2)}) copy-start(bf16[96,768]{1,0:T(8,128)(2,1)} %get-tuple-element.80) | copy-start | bytes 442372
  348.5 10.4 %copy-start.1 = (bf16[1024,768]{1,0:T(8,128)(2,1)S(1)}, bf16[1024,768]{1,0:T(8,128)(2,1)}, u32[]{:S(2)}) copy-start(bf16[1024,768]{1,0:T(8,128)(2,1)} %get-tuple-element.76) | copy-start | bytes 4718596
  356.0 4.1 %copy-start = (bf16[1024,768]{1,0:T(8,128)(2,1)S(1)}, bf16[1024,768]{1,0:T(8,128)(2,1)}, u32[]{:S(2)}) copy-start(bf16[1024,768]{1,0:T(8,128)(2,1)} %get-tuple-element.77) | copy-start | bytes 4718596
